TPU v7x, 128 devices: a whole 4x4x4 slice. The times are simulated.
128 devices in a mesh: rows: 32 (over x, z, core), cols: 4 (over y).
Axes of the slice: x: 4, y: 4, z: 4, core: 2. Of those that a mesh axis runs over, the one named last changes fastest.
Arguments:
- conc: float32 [8, 48, 256, 512], P(None, None, 'rows', 'cols'), may hold values from 0 to 2
- nwp: bfloat16 [2, 137, 65536], P(None, None, 'rows'), may hold values from -0.3 to 0.3
- lev_lo: int32 [48], replicated, may hold values from 0 to 135
- frac: float32 [48], replicated, may hold values from 0 to 1
- pick: int32 [32, 4, 32, 64], P('rows', 'cols'), may hold values from 0 to 2047
- corner_slot: int32 [4, 256, 512], P(None, 'rows', 'cols'), may hold values from 0 to 2047
- corner_wt: float32 [4, 256, 512], P(None, 'rows', 'cols'), may hold values from 0.25 to 1
- settle: float32 [8], replicated, may hold values from 0.015 to 0.15
- source_mask: int32 [256, 512], P('rows', 'cols'), may hold values 0 or 1
- profile: float32 [8, 48], replicated, may hold values from 0.1 to 1
Outputs:
- final_conc: float32 [8, 48, 256, 512], P(None, None, 'rows', 'cols')
- deposit: float32 [8, 256, 512], P(None, 'rows', 'cols')
All inputs are finite; a program needn't handle non-finite values. No bound on the sum of `source_mask` on one device may be relied on, other than what follows from the above.
Results may differ from a plain program's by a relative error of at most 0.0013.
Values may be sent and summed in bfloat16 or wider, within the bound.
No kernel may reach another device: no remote copies, remote signals or barrier semaphores. Data moves between devices by JAX's collectives and lax.ppermute only.
A program may use at most 128 MiB of HBM per device.

v0:
```python
import functools

import jax
import jax.numpy as jnp
from jax import lax
from jax.experimental import pallas as pl
from jax.experimental.pallas import tpu as pltpu
from jax.sharding import PartitionSpec as P

STEPS = 3
KAPPA = 0.05
HALO = STEPS
LANES = 128
STRIP = 10
STRIP_ROWS = 12
F32 = jnp.float32
BF16 = jnp.bfloat16
VMEM_LIMIT = 48 * 1024 * 1024


def lane_ids(shape):
    return lax.broadcasted_iota(jnp.int32, shape, len(shape) - 1)


def roll_lanes(x, shift):
    return pltpu.roll(x, shift % LANES, x.ndim - 1)


def call(kernel, out_shape, args, scratch=(), flops=0, smem=()):
    moved = sum(a.size * a.dtype.itemsize for a in args) + sum(
        s.size * s.dtype.itemsize for s in jax.tree.leaves(out_shape)
    )
    return pl.pallas_call(
        kernel,
        out_shape=out_shape,
        in_specs=[
            pl.BlockSpec(memory_space=pltpu.SMEM if i in smem else pltpu.VMEM)
            for i in range(len(args))
        ],
        out_specs=jax.tree.map(lambda _: pl.BlockSpec(memory_space=pltpu.VMEM), out_shape),
        scratch_shapes=list(scratch),
        compiler_params=pltpu.CompilerParams(vmem_limit_bytes=VMEM_LIMIT),
        cost_estimate=pl.CostEstimate(flops=flops, bytes_accessed=moved, transcendentals=0),
    )(*args)


def select_kernel(lev_ref, frac_ref, pick_ref, nwp_ref, out_ref):
    fields, levels_in, count = nwp_ref.shape
    kept = lev_ref.shape[1]
    ids = lax.broadcasted_iota(jnp.int32, (levels_in, kept), 0)
    low, share = lev_ref[...], frac_ref[...]
    weight = jnp.where(ids == low, 1.0 - share, 0.0) + jnp.where(ids == low + 1, share, 0.0)
    parts = []
    for _ in range(3):
        part = weight.astype(BF16)
        weight = weight - part.astype(F32)
        parts.append(part)
    rows = []
    for field in range(fields):
        mixed = None
        for part in parts:
            term = lax.dot_general(
                part, nwp_ref[field], (((0,), (0,)), ((), ())), preferred_element_type=F32
            )
            mixed = term if mixed is None else mixed + term
        rows.append(mixed.astype(BF16))
    levels = jnp.concatenate(rows, axis=0)
    half = LANES // 2
    width = 2 * LANES
    columns = lax.broadcasted_iota(jnp.int32, (count, width), 0)
    first = lane_ids((kept, LANES)) < half
    for block in range(pick_ref.shape[1] // width):
        wanted = pick_ref[:, block * width : (block + 1) * width]
        hit = jnp.where(columns == wanted, 1.0, 0.0).astype(BF16)
        got = jnp.dot(levels, hit, preferred_element_type=F32)
        for h in range(2):
            east = got[:kept, h * LANES : (h + 1) * LANES]
            north = got[kept:, h * LANES : (h + 1) * LANES]
            out_ref[4 * block + 2 * h] = jnp.where(first, east, roll_lanes(north, half)).astype(BF16)
            out_ref[4 * block + 2 * h + 1] = jnp.where(
                first, roll_lanes(east, half), north
            ).astype(BF16)


def horizontal_kernel(recv_ref, slot_ref, wt_ref, winds_ref, a_ref, b_ref, lev_ref):
    kept = recv_ref.shape[1]
    half = LANES // 2
    first = lane_ids((kept, LANES)) < half
    for pair in range(recv_ref.shape[0] // 2):
        one = recv_ref[2 * pair].astype(F32)
        two = recv_ref[2 * pair + 1].astype(F32)
        at = slice(pair * LANES, (pair + 1) * LANES)
        lev_ref[:kept, at] = jnp.where(first, one, roll_lanes(two, half)).astype(BF16)
        lev_ref[kept:, at] = jnp.where(first, roll_lanes(one, half), two).astype(BF16)
    slots = [slot_ref[q] for q in range(4)]
    raw = [wt_ref[q] for q in range(4)]
    total = raw[0] + raw[1] + raw[2] + raw[3]
    norm = [w / total for w in raw]
    merged = []
    for q in range(4):
        share = None
        for other in range(4):
            term = jnp.where(slots[q] == slots[other], norm[other], 0.0)
            share = term if share is None else share + term
        merged.append(share)
    count = lev_ref.shape[1]
    chunk = 512
    rows = slot_ref.shape[1]
    for y in range(rows):
        acc = None
        for base in range(0, count, chunk):
            ids = lax.broadcasted_iota(jnp.int32, (chunk, LANES), 0) + base
            table = jnp.zeros((chunk, LANES), F32)
            for q in range(4):
                table = jnp.where(
                    ids == slots[q][y : y + 1], merged[q][y : y + 1], table
                )
            high = table.astype(BF16)
            low = (table - high.astype(F32)).astype(BF16)
            lev = lev_ref[:, base : base + chunk]
            term = jnp.dot(lev, high, preferred_element_type=F32) + jnp.dot(
                lev, low, preferred_element_type=F32
            )
            acc = term if acc is None else acc + term
        winds_ref[y] = acc
    odd = lax.axis_index("rows") % 2 == 1
    for j in range(HALO):
        upper = winds_ref[j]
        lower = winds_ref[rows - HALO + j]
        a_ref[j] = jnp.where(odd, upper, lower).astype(BF16)
        b_ref[j] = jnp.where(odd, lower, upper).astype(BF16)


def swap(array, axis, first):
    peers = lax.axis_size(axis)
    start = 0 if first else 1
    pairs = []
    for i in range(start, peers - 1, 2):
        pairs += [(i, i + 1), (i + 1, i)]
    return lax.ppermute(array, axis, pairs)


def strip_parts(load, shape):
    lanes = lane_ids(shape)
    own = jnp.zeros(shape, F32)
    left = jnp.zeros(shape, F32)
    right = jnp.zeros(shape, F32)
    for i in range(STRIP_ROWS):
        row = load(i - 2)
        base = STRIP * i
        at = lanes - base
        own = jnp.where((at >= 3) & (at < 5), roll_lanes(row, base + 3), own)
        own = jnp.where((at >= 5) & (at < 7), roll_lanes(row, base + 5 - 126), own)
        left = jnp.where((at >= 7) & (at < 10), roll_lanes(row, base + 7), left)
        right = jnp.where((at >= 0) & (at < 3), roll_lanes(row, base - 125), right)
    return own, left, right


def wind_strip_kernel(winds_ref, ra_ref, rb_ref, own_ref, a_ref, b_ref):
    row_odd = lax.axis_index("rows") % 2 == 1
    col_odd = lax.axis_index("cols") % 2 == 1
    rows = winds_ref.shape[0]

    def load(y):
        if 0 <= y < rows:
            return winds_ref[y].astype(BF16).astype(F32)
        j = y + HALO if y < 0 else y - rows
        got_a, got_b = ra_ref[j].astype(F32), rb_ref[j].astype(F32)
        above = jnp.where(row_odd, got_a, got_b)
        below = jnp.where(row_odd, got_b, got_a)
        return above if y < 0 else below

    own, left, right = strip_parts(load, winds_ref.shape[1:])
    own_ref[...] = own.astype(BF16)
    a_ref[...] = jnp.where(col_odd, left, right).astype(BF16)
    b_ref[...] = jnp.where(col_odd, right, left).astype(BF16)


def conc_edge_kernel(conc_ref, mask_ref, a_ref, b_ref):
    odd = lax.axis_index("rows") % 2 == 1
    bins = conc_ref.shape[0] // (mask_ref.shape[0] * (a_ref.shape[1] - 1))
    levels = a_ref.shape[1] - 1
    rows = mask_ref.shape[0]

    def level(k, carry):
        for j in range(HALO):
            upper = conc_ref[pl.ds(k * rows + j, bins, stride=levels * rows), :]
            lower = conc_ref[pl.ds(k * rows + rows - HALO + j, bins, stride=levels * rows), :]
            a_ref[j, k] = jnp.where(odd, upper, lower)
            b_ref[j, k] = jnp.where(odd, lower, upper)
        return carry

    lax.fori_loop(0, levels, level, 0, unroll=4)
    mask = mask_ref[...].astype(F32)
    for j in range(HALO):
        upper = jnp.broadcast_to(mask[j : j + 1], (bins, LANES))
        lower = jnp.broadcast_to(mask[rows - HALO + j : rows - HALO + j + 1], (bins, LANES))
        a_ref[j, levels] = jnp.where(odd, upper, lower)
        b_ref[j, levels] = jnp.where(odd, lower, upper)


def conc_strip_kernel(conc_ref, mask_ref, ra_ref, rb_ref, own_ref, a_ref, b_ref):
    row_odd = lax.axis_index("rows") % 2 == 1
    col_odd = lax.axis_index("cols") % 2 == 1
    levels = ra_ref.shape[1] - 1
    bins = ra_ref.shape[2]
    rows = mask_ref.shape[0]

    def halo(y, k):
        j = y + HALO if y < 0 else y - rows
        got_a, got_b = ra_ref[j, k], rb_ref[j, k]
        return jnp.where(row_odd == (y < 0), got_a, got_b)

    def store(k, load):
        own, left, right = strip_parts(load, (bins, LANES))
        own_ref[k] = own
        a_ref[k] = jnp.where(col_odd, left, right)
        b_ref[k] = jnp.where(col_odd, right, left)

    def level(k, carry):
        def load(y):
            if 0 <= y < rows:
                return conc_ref[pl.ds(k * rows + y, bins, stride=levels * rows), :]
            return halo(y, k)

        store(k, load)
        return carry

    lax.fori_loop(0, levels, level, 0)
    mask = mask_ref[...].astype(F32)

    def load_mask(y):
        if 0 <= y < rows:
            return jnp.broadcast_to(mask[y : y + 1], (bins, LANES))
        return halo(y, levels)

    store(levels, load_mask)


def coefficients(east_w, east, east_e, north_s, north, north_n, valid):
    face_w = 0.5 * (east_w + east)
    face_e = 0.5 * (east + east_e)
    face_s = 0.5 * (north_s + north)
    face_n = 0.5 * (north + north_n)
    out_e = jnp.maximum(face_e, 0.0)
    out_n = jnp.maximum(face_n, 0.0)
    out_w = jnp.minimum(face_w, 0.0)
    out_s = jnp.minimum(face_s, 0.0)
    centre = (1.0 - 4.0 * KAPPA) - (out_e - out_w) - (out_n - out_s)
    west = KAPPA + jnp.maximum(face_w, 0.0)
    east_c = KAPPA - jnp.minimum(face_e, 0.0)
    south = KAPPA + jnp.maximum(face_s, 0.0)
    north_c = KAPPA - jnp.minimum(face_n, 0.0)
    result = (centre, west, east_c, south, north_c)
    return result if valid is None else tuple(jnp.where(valid, c, 0.0) for c in result)


def transport_kernel(
    conc_ref, mask_ref, settle_ref, profile_ref,
    ra_ref, rb_ref, own_ref, ca_ref, cb_ref,
    winds_ref, wra_ref, wrb_ref, wown_ref, wca_ref, wcb_ref,
    out_ref, deposit_ref,
    coef_ref, strip_coef_ref, prof_ref, mask_all_ref, mask_strip_ref, fall_ref, state_ref,
):
    row, col = lax.axis_index("rows"), lax.axis_index("cols")
    last_row, last_col = lax.axis_size("rows") - 1, lax.axis_size("cols") - 1
    row_odd = row % 2 == 1
    levels = ra_ref.shape[1] - 1
    bins = ra_ref.shape[2]
    rows = mask_ref.shape[0]
    tile = (bins, LANES)
    stride = levels * rows

    def halo_of(y, get_a, get_b):
        return jnp.where(row_odd == (y < 0), get_a, get_b)

    def halo_at(y):
        return y + HALO if y < 0 else y - rows

    def wind_row(y):
        if 0 <= y < rows:
            return winds_ref[y]
        j = halo_at(y)
        return halo_of(y, wra_ref[j].astype(F32), wrb_ref[j].astype(F32))

    strip = wown_ref[...].astype(F32) + wca_ref[...].astype(F32) + wcb_ref[...].astype(F32)
    strip_u, strip_v = strip[:levels], strip[levels:]
    lanes = lane_ids((levels, LANES))
    at = lanes % STRIP
    inside = (
        ((at >= 3) | (col > 0))
        & ((at < 7) | (col < last_col))
        & ((lanes >= 2 * STRIP) | (row > 0))
        & ((lanes < (2 + rows) * STRIP) | (row < last_row))
    )
    found = coefficients(
        roll_lanes(strip_u, 1), strip_u, roll_lanes(strip_u, -1),
        roll_lanes(strip_v, STRIP), strip_v, roll_lanes(strip_v, -STRIP),
        inside,
    )
    for i in range(5):
        strip_coef_ref[i] = found[i]
    for y in range(-2, rows + 2):
        u = wind_row(y)[:levels]
        base = STRIP * (y + 2)
        u_w = jnp.where(lanes == 0, roll_lanes(strip_u, -(base + 2)), roll_lanes(u, 1))
        u_e = jnp.where(
            lanes == LANES - 1, roll_lanes(strip_u, LANES - 1 - (base + 7)), roll_lanes(u, -1)
        )
        valid = None
        if y < 0:
            valid = row > 0
        elif y >= rows:
            valid = row < last_row
        found = coefficients(
            u_w, u, u_e,
            wind_row(y - 1)[levels:], wind_row(y)[levels:], wind_row(y + 1)[levels:],
            valid,
        )
        for i in range(5):
            coef_ref[5 * (y + 2) + i] = found[i]

    mask = mask_ref[...].astype(F32)
    for y in range(-2, rows + 2):
        if 0 <= y < rows:
            mask_all_ref[y + 2] = jnp.broadcast_to(mask[y : y + 1], tile)
        else:
            j = halo_at(y)
            mask_all_ref[y + 2] = halo_of(y, ra_ref[j, levels], rb_ref[j, levels])
    mask_strip_ref[...] = own_ref[levels] + ca_ref[levels] + cb_ref[levels]
    sublanes = lax.broadcasted_iota(jnp.int32, tile, 0)
    settle = jnp.zeros(tile, F32)
    for b in range(bins):
        settle = jnp.where(sublanes == b, settle_ref[b], settle)
    for k in range(levels):
        prof_ref[k] = jnp.broadcast_to(profile_ref[:, k : k + 1], tile)
    fall_ref[...] = jnp.zeros(fall_ref.shape, F32)

    tile_lanes = lane_ids(tile)
    at_west = tile_lanes == 0
    at_east = tile_lanes == LANES - 1

    def level(k, carry):
        prof = prof_ref[k]

        def spread(ref, i):
            return ref[i, pl.ds(k, bins, stride=0), :]

        state = {}
        for y in range(-HALO, rows + HALO):
            if 0 <= y < rows:
                state[y] = conc_ref[pl.ds(k * rows + y, bins, stride=stride), :]
            else:
                j = halo_at(y)
                state[y] = halo_of(y, ra_ref[j, k], rb_ref[j, k])
        edge = own_ref[k] + ca_ref[k] + cb_ref[k]
        slot = 0
        for step in range(STEPS):
            reach = STEPS - 1 - step
            fresh = {}
            for y in range(-reach, rows + reach):
                a = state[y]
                base = STRIP * (y + 2)
                a_w = jnp.where(at_west, roll_lanes(edge, -(base + 2)), roll_lanes(a, 1))
                a_e = jnp.where(
                    at_east, roll_lanes(edge, LANES - 1 - (base + 7)), roll_lanes(a, -1)
                )
                c = [spread(coef_ref, 5 * (y + 2) + i) for i in range(5)]
                fall = settle * a
                source = fall_ref[slot] + prof * mask_all_ref[y + 2]
                fall_ref[slot] = fall
                fresh[y] = (
                    (c[0] * a - fall)
                    + (c[1] * a_w + c[2] * a_e)
                    + (c[3] * state[y - 1] + c[4] * state[y + 1])
                    + source
                )
                slot += 1
            if reach:
                c = [spread(strip_coef_ref, i) for i in range(5)]
                fall = settle * edge
                source = fall_ref[slot] + prof * mask_strip_ref[...]
                fall_ref[slot] = fall
                edge = (
                    (c[0] * edge - fall)
                    + (c[1] * roll_lanes(edge, 1) + c[2] * roll_lanes(edge, -1))
                    + (c[3] * roll_lanes(edge, STRIP) + c[4] * roll_lanes(edge, -STRIP))
                    + source
                )
                slot += 1
            state = fresh
        for y in range(rows):
            out_ref[pl.ds(k * rows + y, bins, stride=stride), :] = state[y]
        return carry

    lax.fori_loop(0, levels, level, 0)
    first, second, third = 2, rows + 2 * 2 + 1 + 1, (rows + 2 * 2 + 1) + (rows + 2 + 1)
    for y in range(rows):
        deposit_ref[pl.ds(y, bins, stride=rows), :] = (
            fall_ref[first + y] + fall_ref[second + y] + fall_ref[third + y]
        )


def per_device(conc, nwp, lev_lo, frac, pick, corner_slot, corner_wt, settle, source_mask, profile):
    bins, levels, rows, cols = conc.shape
    peers = pick.shape[2]
    shape = jax.ShapeDtypeStruct
    flat = conc.reshape(bins * levels * rows, cols)

    sent = call(
        select_kernel,
        shape((peers, levels, LANES), BF16),
        (lev_lo.reshape(1, -1), frac.reshape(1, -1), pick.reshape(1, -1), nwp),
        flops=2 * 2 * levels * 2048 * 2048,
    )
    received = lax.all_to_all(sent, "rows", split_axis=0, concat_axis=0, tiled=True)

    edge_rows = shape((HALO, levels + 1, bins, cols), F32)
    strips = shape((levels + 1, bins, LANES), F32)
    ca, cb = call(conc_edge_kernel, (edge_rows, edge_rows), (flat, source_mask))
    ra, rb = swap(ca, "rows", True), swap(cb, "rows", False)
    own, sa, sb = call(conc_strip_kernel, (strips, strips, strips), (flat, source_mask, ra, rb))
    xa, xb = swap(sa, "cols", True), swap(sb, "cols", False)

    wind_rows = shape((HALO, 2 * levels, cols), BF16)
    winds, wa, wb = call(
        horizontal_kernel,
        (shape((rows, 2 * levels, cols), F32), wind_rows, wind_rows),
        (received, corner_slot, corner_wt),
        scratch=(pltpu.VMEM((2 * levels, peers * LANES // 2), BF16),),
        flops=2 * 2 * 2 * levels * 2048 * 1024,
    )
    wra, wrb = swap(wa, "rows", True), swap(wb, "rows", False)
    wind_strip = shape((2 * levels, LANES), BF16)
    wown, wsa, wsb = call(
        wind_strip_kernel, (wind_strip, wind_strip, wind_strip), (winds, wra, wrb)
    )
    wxa, wxb = swap(wsa, "cols", True), swap(wsb, "cols", False)

    tile = (bins, LANES)
    updates = sum(rows + 2 * (STEPS - 1 - s) for s in range(STEPS)) + STEPS - 1
    final, deposit = call(
        transport_kernel,
        (shape(flat.shape, F32), shape((bins * rows, cols), F32)),
        (flat, source_mask, settle, profile, ra, rb, own, xa, xb,
         winds, wra, wrb, wown, wxa, wxb),
        scratch=(
            pltpu.VMEM((5 * (rows + 4), levels, LANES), F32),
            pltpu.VMEM((5, levels, LANES), F32),
            pltpu.VMEM((levels,) + tile, F32),
            pltpu.VMEM((rows + 4,) + tile, F32),
            pltpu.VMEM(tile, F32),
            pltpu.VMEM((updates,) + tile, F32),
            pltpu.VMEM(tile, F32),
        ),
        smem=(2,),
        flops=16 * updates * levels * bins * LANES,
    )
    return final.reshape(conc.shape), deposit.reshape(bins, rows, cols)


def solution(mesh):
    placed = (
        P(None, None, "rows", "cols"),
        P(None, None, "rows"),
        P(),
        P(),
        P("rows", "cols", None, None),
        P(None, "rows", "cols"),
        P(None, "rows", "cols"),
        P(),
        P("rows", "cols"),
        P(),
    )
    return jax.shard_map(
        per_device,
        mesh=mesh,
        in_specs=placed,
        out_specs=(P(None, None, "rows", "cols"), P(None, "rows", "cols")),
        check_vma=False,
    )
```

profile of v0, /device:TPU:10, one launch (start us, length us, event | category | flops | bytes accessed | tf_op | source)
XLA Modules:
  0.0 70.1 jit_solution(7346005336366622377)
XLA Ops:
  0.6 0.0 copy-start
  0.6 1.4 %copy-done = f32[8,48,8,128]{3,2,1,0:T(8,128)S(1)} copy-done((f32[8,48,8,128]{3,2,1,0:T(8,128)S(1)}, f32[8,48,8,128]{3,2,1,0:T(8,128)}, u32[]{:S(2)}) %copy-start) | copy-done | bytes 1572888
  2.0 0.0 copy-start.3
  2.0 0.7 copy-done.3
  2.7 0.0 copy-start.11
  2.7 0.0 copy-start.9
  2.7 0.0 copy-start.10
  2.7 1.7 %shard_map.113 = (f32[3,49,8,128]{3,2,1,0:T(8,128)}, f32[3,49,8,128]{3,2,1,0:T(8,128)}) custom-call(f32[3072,128]{1,0:T(8,128)S(1)} %bitcast.7, s32[8,128]{1,0:T(8,128)S(1)} %copy-done.3), custom_call_target="tpu_custom_call" | custom-call | bytes 2781184 | tf_op jit(solution)/shard_map/pallas_call | solution.py:33
  4.5 0.0 collective-permute-start
  4.5 6.0 %collective-permute-start.1 = (f32[3,49,8,128]{3,2,1,0:T(8,128)}, f32[3,49,8,128]{3,2,1,0:T(8,128)S(1)}, u32[]{:S(2)}, u32[]{:S(2)}) collective-permute-start(f32[3,49,8,128]{3,2,1,0:T(8,128)} %get-tuple-element.16), channel_id=1, source_target_pairs={{4,8},{8,4},{12,16},{16,12},{20,24},{24,20},{28,32},{32,28},{36,40... | collective-permute-start | bytes 1806344 | tf_op jit(solution)/shard_map/ppermute | solution.py:140
  10.5 0.0 copy-done.11
  10.5 0.1 reshape.25.pick_ref
  10.6 1.7 %copy.12.nwp_ref = bf16[2,137,2048]{2,1,0:T(8,128)(2,1)S(1)} copy(bf16[2,137,2048]{2,0,1:T(2,128)(2,1)} %param.11) | data formatting | bytes 2244608 | tf_op args[1]
  12.3 0.0 copy-done.9
  12.3 0.0 copy-done.10
  12.3 0.0 copy-start.1
  12.3 0.0 copy-start.4
  12.3 2.4 %shard_map.115 = bf16[32,48,128]{2,1,0:T(8,128)(2,1)S(1)} custom-call(s32[1,48]{1,0:T(1,128)S(1)} %bitcast.10, f32[1,48]{1,0:T(1,128)S(1)} %bitcast.11, s32[1,2048]{1,0:T(1,128)S(1)} %reshape.25.pick_ref, bf16[2,137,2048]{2,1,0:T(8,128)(2,1)S(1)} %copy.12.nwp_ref), custom_call_target="tpu_custom_call" | custom-call | flops 805306368 | bytes 1524096 | tf_op jit(solution)/shard_map/pallas_call | solution.py:33
  14.7 0.0 copy-start.2
  14.7 0.7 %copy-done.2 = bf16[32,48,128]{2,1,0:T(8,128)(2,1)} copy-done((bf16[32,48,128]{2,1,0:T(8,128)(2,1)}, bf16[32,48,128]{2,1,0:T(8,128)(2,1)S(1)}, u32[]{:S(2)}) %copy-start.2) | copy-done | bytes 393240
  15.4 5.5 %all-to-all-start = ((bf16[32,48,128]{2,1,0:T(8,128)(2,1)}), bf16[32,48,128]{2,1,0:T(8,128)(2,1)S(1)}, u32[]{:S(2)}, u32[]{:S(2)}) async-start(bf16[32,48,128]{2,1,0:T(8,128)(2,1)} %copy-done.2), calls=%async_computation | async-start | bytes 786432 | tf_op jit(solution)/shard_map/all_to_all | solution.py:416
  21.0 0.0 copy-start.7
  21.0 0.0 copy-start.8
  21.0 0.0 collective-permute-done.ra_ref
  21.0 0.0 collective-permute-done.1.rb_ref
  21.0 0.0 copy-done.1
  21.0 0.0 copy-done.4
  21.0 6.4 %shard_map.114 = (f32[49,8,128]{2,1,0:T(8,128)S(1)}, f32[49,8,128]{2,1,0:T(8,128)}, f32[49,8,128]{2,1,0:T(8,128)}) custom-call(f32[3072,128]{1,0:T(8,128)S(1)} %bitcast.8, s32[8,128]{1,0:T(8,128)S(1)} %copy-done.4, f32[3,49,8,128]{3,2,1,0:T(8,128)S(1)} %collective-permute-done.ra_ref, f32[3,49,8,128]{3,2,1,0:T(8,128)S(1)} %collective-permute-done.1.rb_ref), custom_call_target="tpu_custom_call" | custom-call | bytes 3383296 | tf_op jit(solution)/shard_map/pallas_call | solution.py:33
  27.4 0.4 collective-permute-start.2
  27.9 0.0 copy-start.5
  27.9 0.0 copy-start.6
  27.9 4.4 %collective-permute-start.3 = (f32[49,8,128]{2,1,0:T(8,128)}, f32[49,8,128]{2,1,0:T(8,128)}, u32[]{:S(2)}, u32[]{:S(2)}) collective-permute-start(f32[49,8,128]{2,1,0:T(8,128)} %get-tuple-element.19), channel_id=1, source_target_pairs={{1,2},{2,1},{5,6},{6,5},{9,10},{10,9},{13,14},{14,13},{17,18},{18,... | collective-permute-start | bytes 602120 | tf_op jit(solution)/shard_map/ppermute | solution.py:140
  32.3 0.0 all-to-all-done.recv_ref
  32.3 0.0 copy-done.7
  32.3 0.0 copy-done.8
  32.3 5.0 %shard_map.116 = (f32[8,96,128]{2,1,0:T(8,128)S(1)}, bf16[3,96,128]{2,1,0:T(8,128)(2,1)S(1)}, bf16[3,96,128]{2,1,0:T(8,128)(2,1)S(1)}) custom-call(bf16[32,48,128]{2,1,0:T(8,128)(2,1)S(1)} %all-to-all-done.recv_ref, s32[4,8,128]{2,1,0:T(8,128)S(1)} %copy-done.7, f32[4,8,128]{2,1,0:T(8,128)S(1)} %copy-done.8), custom_call_target="tpu_custom_call" | custom-call | flops 805306368 | bytes 966656 | tf_op jit(solution)/shard_map/pallas_call | solution.py:33
  37.3 0.1 collective-permute-start.4
  37.4 4.7 %collective-permute-start.5 = (bf16[3,96,128]{2,1,0:T(8,128)(2,1)S(1)}, bf16[3,96,128]{2,1,0:T(8,128)(2,1)S(1)}, u32[]{:S(2)}, u32[]{:S(2)}) collective-permute-start(bf16[3,96,128]{2,1,0:T(8,128)(2,1)S(1)} %get-tuple-element.22), channel_id=1, source_target_pairs={{4,8},{8,4},{12,16},{16,12},{20,24},{24,20},{28,32},{32,28},{36,40... | collective-permute-start | bytes 221192 | tf_op jit(solution)/shard_map/ppermute | solution.py:140
  42.1 0.0 collective-permute-done.4.ra_ref.wra_ref
  42.1 3.1 %collective-permute-done.5.rb_ref.wrb_ref = bf16[3,96,128]{2,1,0:T(8,128)(2,1)S(1)} collective-permute-done((bf16[3,96,128]{2,1,0:T(8,128)(2,1)S(1)}, bf16[3,96,128]{2,1,0:T(8,128)(2,1)S(1)}, u32[]{:S(2)}, u32[]{:S(2)}) %collective-permute-start.5) | collective-permute-done | bytes 73760 | tf_op jit(solution)/shard_map/ppermute | solution.py:140
  45.2 0.2 shard_map.117
  45.5 0.1 collective-permute-start.6
  45.5 2.6 %collective-permute-start.7 = (bf16[96,128]{1,0:T(8,128)(2,1)S(1)}, bf16[96,128]{1,0:T(8,128)(2,1)S(1)}, u32[]{:S(2)}, u32[]{:S(2)}) collective-permute-start(bf16[96,128]{1,0:T(8,128)(2,1)S(1)} %get-tuple-element.25), channel_id=1, source_target_pairs={{1,2},{2,1},{5,6},{6,5},{9,10},{10,9},{13,14},{14,13},{17,18},{18,... | collective-permute-start | bytes 73736 | tf_op jit(solution)/shard_map/ppermute | solution.py:140
  48.2 1.2 %collective-permute-done.6.wca_ref = bf16[96,128]{1,0:T(8,128)(2,1)S(1)} collective-permute-done((bf16[96,128]{1,0:T(8,128)(2,1)S(1)}, bf16[96,128]{1,0:T(8,128)(2,1)S(1)}, u32[]{:S(2)}, u32[]{:S(2)}) %collective-permute-start.6) | collective-permute-done | bytes 24608 | tf_op jit(solution)/shard_map/ppermute | solution.py:140
  49.4 1.9 %collective-permute-done.7.wcb_ref = bf16[96,128]{1,0:T(8,128)(2,1)S(1)} collective-permute-done((bf16[96,128]{1,0:T(8,128)(2,1)S(1)}, bf16[96,128]{1,0:T(8,128)(2,1)S(1)}, u32[]{:S(2)}, u32[]{:S(2)}) %collective-permute-start.7) | collective-permute-done | bytes 24608 | tf_op jit(solution)/shard_map/ppermute | solution.py:140
  51.3 0.0 collective-permute-done.2.ca_ref
  51.3 0.0 collective-permute-done.3.cb_ref
  51.3 0.0 copy-done.5
  51.3 0.0 copy-done.6
  51.3 18.8 %shard_map.118 = (f32[3072,128]{1,0:T(8,128)}, f32[64,128]{1,0:T(8,128)}) custom-call(f32[3072,128]{1,0:T(8,128)S(1)} %bitcast.9, s32[8,128]{1,0:T(8,128)S(1)} %copy-done.4, f32[8]{0:T(128)S(1)} %copy-done.6, f32[8,48]{1,0:T(8,128)S(1)} %copy-done.5, f32[3,49,8,128]{3,2,1,0:T(8,128)S(1)} %collective-permute-done.ra_ref, ...), custom_call_target="tpu_custom_call" | custom-call | flops 25165824 | bytes 5604896 | tf_op jit(solution)/shard_map/pallas_call | solution.py:33
Async XLA Ops:
  0.6 1.4 %copy-start = (f32[8,48,8,128]{3,2,1,0:T(8,128)S(1)}, f32[8,48,8,128]{3,2,1,0:T(8,128)}, u32[]{:S(2)}) copy-start(f32[8,48,8,128]{3,2,1,0:T(8,128)} %param.10) | copy-start | bytes 4718596
  2.0 0.7 copy-start.3
  2.7 7.8 %copy-start.11 = (s32[1,1,32,64]{3,2,1,0:T(8,128)S(1)}, s32[1,1,32,64]{3,2,1,0:T(8,128)}, u32[]{:S(2)}) copy-start(s32[1,1,32,64]{3,2,1,0:T(8,128)} %param.14) | copy-start | bytes 24580
  2.7 9.5 %copy-start.9 = (s32[48]{0:T(128)S(1)}, s32[48]{0:T(128)}, u32[]{:S(2)}) copy-start(s32[48]{0:T(128)} %param.12) | copy-start | bytes 580
  2.7 9.5 %copy-start.10 = (f32[48]{0:T(128)S(1)}, f32[48]{0:T(128)}, u32[]{:S(2)}) copy-start(f32[48]{0:T(128)} %param.13) | copy-start | bytes 580
  4.5 16.5 %collective-permute-start = (f32[3,49,8,128]{3,2,1,0:T(8,128)}, f32[3,49,8,128]{3,2,1,0:T(8,128)S(1)}, u32[]{:S(2)}, u32[]{:S(2)}) collective-permute-start(f32[3,49,8,128]{3,2,1,0:T(8,128)} %get-tuple-element.15), channel_id=1, source_target_pairs={{0,4},{4,0},{8,12},{12,8},{16,20},{20,16},{24,28},{28,24},{32,36},... | collective-permute-start | bytes 1806344 | tf_op jit(solution)/shard_map/ppermute | solution.py:140
  4.5 16.5 %collective-permute-start.1 = (f32[3,49,8,128]{3,2,1,0:T(8,128)}, f32[3,49,8,128]{3,2,1,0:T(8,128)S(1)}, u32[]{:S(2)}, u32[]{:S(2)}) collective-permute-start(f32[3,49,8,128]{3,2,1,0:T(8,128)} %get-tuple-element.16), channel_id=1, source_target_pairs={{4,8},{8,4},{12,16},{16,12},{20,24},{24,20},{28,32},{32,28},{36,40... | collective-permute-start | bytes 1806344 | tf_op jit(solution)/shard_map/ppermute | solution.py:140
  12.3 8.7 %copy-start.1 = (f32[8,48,8,128]{3,2,1,0:T(8,128)S(1)}, f32[8,48,8,128]{3,2,1,0:T(8,128)}, u32[]{:S(2)}) copy-start(f32[8,48,8,128]{3,2,1,0:T(8,128)} %param.10) | copy-start | bytes 4718596
  12.3 8.7 %copy-start.4 = (s32[8,128]{1,0:T(8,128)S(1)}, s32[8,128]{1,0:T(8,128)}, u32[]{:S(2)}) copy-start(s32[8,128]{1,0:T(8,128)} %mask_ref.5) | copy-start | bytes 12292
  14.7 0.7 %copy-start.2 = (bf16[32,48,128]{2,1,0:T(8,128)(2,1)}, bf16[32,48,128]{2,1,0:T(8,128)(2,1)S(1)}, u32[]{:S(2)}) copy-start(bf16[32,48,128]{2,1,0:T(8,128)(2,1)S(1)} %shard_map.115) | copy-start | bytes 1179652
  15.4 16.9 %all-to-all-start = ((bf16[32,48,128]{2,1,0:T(8,128)(2,1)}), bf16[32,48,128]{2,1,0:T(8,128)(2,1)S(1)}, u32[]{:S(2)}, u32[]{:S(2)}) async-start(bf16[32,48,128]{2,1,0:T(8,128)(2,1)} %copy-done.2), calls=%async_computation | async-start | bytes 786432 | tf_op jit(solution)/shard_map/all_to_all | solution.py:416
  21.0 11.4 %copy-start.7 = (s32[4,8,128]{2,1,0:T(8,128)S(1)}, s32[4,8,128]{2,1,0:T(8,128)}, u32[]{:S(2)}) copy-start(s32[4,8,128]{2,1,0:T(8,128)} %slot_ref.1) | copy-start | bytes 49156
  21.0 11.4 %copy-start.8 = (f32[4,8,128]{2,1,0:T(8,128)S(1)}, f32[4,8,128]{2,1,0:T(8,128)}, u32[]{:S(2)}) copy-start(f32[4,8,128]{2,1,0:T(8,128)} %wt_ref.1) | copy-start | bytes 49156
  27.4 23.9 %collective-permute-start.2 = (f32[49,8,128]{2,1,0:T(8,128)}, f32[49,8,128]{2,1,0:T(8,128)}, u32[]{:S(2)}, u32[]{:S(2)}) collective-permute-start(f32[49,8,128]{2,1,0:T(8,128)} %get-tuple-element.18), channel_id=1, source_target_pairs={{0,1},{1,0},{2,3},{3,2},{4,5},{5,4},{6,7},{7,6},{8,9},{9,8},{10,11... | collective-permute-start | bytes 602120 | tf_op jit(solution)/shard_map/ppermute | solution.py:140
  27.9 23.4 %copy-start.5 = (f32[8,48]{1,0:T(8,128)S(1)}, f32[8,48]{1,0:T(8,128)}, u32[]{:S(2)}) copy-start(f32[8,48]{1,0:T(8,128)} %profile_ref.1) | copy-start | bytes 4612
  27.9 23.4 %copy-start.6 = (f32[8]{0:T(128)S(1)}, f32[8]{0:T(128)}, u32[]{:S(2)}) copy-start(f32[8]{0:T(128)} %settle_ref.1) | copy-start | bytes 100
  27.9 23.4 %collective-permute-start.3 = (f32[49,8,128]{2,1,0:T(8,128)}, f32[49,8,128]{2,1,0:T(8,128)}, u32[]{:S(2)}, u32[]{:S(2)}) collective-permute-start(f32[49,8,128]{2,1,0:T(8,128)} %get-tuple-element.19), channel_id=1, source_target_pairs={{1,2},{2,1},{5,6},{6,5},{9,10},{10,9},{13,14},{14,13},{17,18},{18,... | collective-permute-start | bytes 602120 | tf_op jit(solution)/shard_map/ppermute | solution.py:140
  37.3 4.8 %collective-permute-start.4 = (bf16[3,96,128]{2,1,0:T(8,128)(2,1)S(1)}, bf16[3,96,128]{2,1,0:T(8,128)(2,1)S(1)}, u32[]{:S(2)}, u32[]{:S(2)}) collective-permute-start(bf16[3,96,128]{2,1,0:T(8,128)(2,1)S(1)} %get-tuple-element.21), channel_id=1, source_target_pairs={{0,4},{4,0},{8,12},{12,8},{16,20},{20,16},{24,28},{28,24},{32,36},... | collective-permute-start | bytes 221192 | tf_op jit(solution)/shard_map/ppermute | solution.py:140
  37.4 7.8 %collective-permute-start.5 = (bf16[3,96,128]{2,1,0:T(8,128)(2,1)S(1)}, bf16[3,96,128]{2,1,0:T(8,128)(2,1)S(1)}, u32[]{:S(2)}, u32[]{:S(2)}) collective-permute-start(bf16[3,96,128]{2,1,0:T(8,128)(2,1)S(1)} %get-tuple-element.22), channel_id=1, source_target_pairs={{4,8},{8,4},{12,16},{16,12},{20,24},{24,20},{28,32},{32,28},{36,40... | collective-permute-start | bytes 221192 | tf_op jit(solution)/shard_map/ppermute | solution.py:140
  45.5 3.9 %collective-permute-start.6 = (bf16[96,128]{1,0:T(8,128)(2,1)S(1)}, bf16[96,128]{1,0:T(8,128)(2,1)S(1)}, u32[]{:S(2)}, u32[]{:S(2)}) collective-permute-start(bf16[96,128]{1,0:T(8,128)(2,1)S(1)} %get-tuple-element.24), channel_id=1, source_target_pairs={{0,1},{1,0},{2,3},{3,2},{4,5},{5,4},{6,7},{7,6},{8,9},{9,8},{10,11... | collective-permute-start | bytes 73736 | tf_op jit(solution)/shard_map/ppermute | solution.py:140
  45.5 5.7 %collective-permute-start.7 = (bf16[96,128]{1,0:T(8,128)(2,1)S(1)}, bf16[96,128]{1,0:T(8,128)(2,1)S(1)}, u32[]{:S(2)}, u32[]{:S(2)}) collective-permute-start(bf16[96,128]{1,0:T(8,128)(2,1)S(1)} %get-tuple-element.25), channel_id=1, source_target_pairs={{1,2},{2,1},{5,6},{6,5},{9,10},{10,9},{13,14},{14,13},{17,18},{18,... | collective-permute-start | bytes 73736 | tf_op jit(solution)/shard_map/ppermute | solution.py:140
where the time goes:
time: 70.5 us; the launch traced here: 70.1 us
  Pallas kernels  34.5 us (49%)
  starting transfers between devices  23.9 us (34%)
  waiting for transfers between devices  6.21 us (9%)
  local copies, waits for them, and re-layouts  4.61 us (7%)
  between operations  0.87 us (1%)
    pallas_call x6, Pallas kernels, call(): pl.pallas_call(kernel, out_shape=out_shape, in_specs=[pl.BlockSpec(memory...  34.5 us
    ppermute x8, starting transfers between devices, swap(): return lax.ppermute(array, axis, pairs)  18.4 us
    ppermute x8, waiting for transfers between devices, swap(): return lax.ppermute(array, axis, pairs)  6.21 us
    all_to_all x1, starting transfers between devices, per_device(): lax.all_to_all(sent, 'rows', split_axis=0, concat_axis=0, tiled=True)  5.53 us
    unnamed x25, local copies, waits for them, and re-layouts  4.53 us
  transfers between devices with their start and end apart: 9, of which 3 were waited for; matrix products, arithmetic and copies ran while one was open for 2% of the time, Pallas kernels for 20%

commit v1 on v0

--- a/solution.py
+++ b/solution.py
@@ -140,40 +140,39 @@
     return lax.ppermute(array, axis, pairs)
 
 
-def strip_parts(load, shape):
-    lanes = lane_ids(shape)
-    own = jnp.zeros(shape, F32)
-    left = jnp.zeros(shape, F32)
-    right = jnp.zeros(shape, F32)
+def strip_select():
+    lane = lane_ids((LANES, LANES))
+    column = lax.broadcasted_iota(jnp.int32, (LANES, LANES), 0)
+    chosen = []
     for i in range(STRIP_ROWS):
-        row = load(i - 2)
-        base = STRIP * i
-        at = lanes - base
-        own = jnp.where((at >= 3) & (at < 5), roll_lanes(row, base + 3), own)
-        own = jnp.where((at >= 5) & (at < 7), roll_lanes(row, base + 5 - 126), own)
-        left = jnp.where((at >= 7) & (at < 10), roll_lanes(row, base + 7), left)
-        right = jnp.where((at >= 0) & (at < 3), roll_lanes(row, base - 125), right)
-    return own, left, right
-
-
-def wind_strip_kernel(winds_ref, ra_ref, rb_ref, own_ref, a_ref, b_ref):
+        at = lane - STRIP * i
+        source = jnp.where(at < 3, at + 125, jnp.where(at < 5, at - 3, jnp.where(at < 7, at + 121, at - 7)))
+        hit = (source == column) & (at >= 0) & (at < STRIP)
+        chosen.append(jnp.where(hit, 1.0, 0.0).astype(BF16))
+    return chosen
+
+
+def whole_strip(mine, got_a, got_b, at, odd):
+    from_left = jnp.where(odd, got_a, got_b)
+    from_right = jnp.where(odd, got_b, got_a)
+    return jnp.where(at < 3, from_left, jnp.where(at < 7, mine, from_right))
+
+
+def wind_strip_kernel(winds_ref, ra_ref, rb_ref, strip_ref):
     row_odd = lax.axis_index("rows") % 2 == 1
-    col_odd = lax.axis_index("cols") % 2 == 1
     rows = winds_ref.shape[0]
-
-    def load(y):
+    chosen = strip_select()
+    total = None
+    for i in range(STRIP_ROWS):
+        y = i - 2
         if 0 <= y < rows:
-            return winds_ref[y].astype(BF16).astype(F32)
-        j = y + HALO if y < 0 else y - rows
-        got_a, got_b = ra_ref[j].astype(F32), rb_ref[j].astype(F32)
-        above = jnp.where(row_odd, got_a, got_b)
-        below = jnp.where(row_odd, got_b, got_a)
-        return above if y < 0 else below
-
-    own, left, right = strip_parts(load, winds_ref.shape[1:])
-    own_ref[...] = own.astype(BF16)
-    a_ref[...] = jnp.where(col_odd, left, right).astype(BF16)
-    b_ref[...] = jnp.where(col_odd, right, left).astype(BF16)
+            line = winds_ref[y].astype(BF16)
+        else:
+            j = y + HALO if y < 0 else y - rows
+            line = jnp.where(row_odd == (y < 0), ra_ref[j], rb_ref[j])
+        term = jnp.dot(line, chosen[i], preferred_element_type=F32)
+        total = term if total is None else total + term
+    strip_ref[...] = total.astype(BF16)
 
 
 def conc_edge_kernel(conc_ref, mask_ref, a_ref, b_ref):
@@ -199,42 +198,36 @@
         b_ref[j, levels] = jnp.where(odd, lower, upper)
 
 
-def conc_strip_kernel(conc_ref, mask_ref, ra_ref, rb_ref, own_ref, a_ref, b_ref):
+def conc_strip_kernel(conc_ref, mask_ref, ra_ref, rb_ref, strip_ref, high_ref, low_ref):
     row_odd = lax.axis_index("rows") % 2 == 1
-    col_odd = lax.axis_index("cols") % 2 == 1
     levels = ra_ref.shape[1] - 1
     bins = ra_ref.shape[2]
     rows = mask_ref.shape[0]
-
-    def halo(y, k):
-        j = y + HALO if y < 0 else y - rows
-        got_a, got_b = ra_ref[j, k], rb_ref[j, k]
-        return jnp.where(row_odd == (y < 0), got_a, got_b)
-
-    def store(k, load):
-        own, left, right = strip_parts(load, (bins, LANES))
-        own_ref[k] = own
-        a_ref[k] = jnp.where(col_odd, left, right)
-        b_ref[k] = jnp.where(col_odd, right, left)
-
-    def level(k, carry):
-        def load(y):
-            if 0 <= y < rows:
-                return conc_ref[pl.ds(k * rows + y, bins, stride=levels * rows), :]
-            return halo(y, k)
-
-        store(k, load)
-        return carry
-
-    lax.fori_loop(0, levels, level, 0)
     mask = mask_ref[...].astype(F32)
-
-    def load_mask(y):
-        if 0 <= y < rows:
-            return jnp.broadcast_to(mask[y : y + 1], (bins, LANES))
-        return halo(y, levels)
-
-    store(levels, load_mask)
+    chosen = strip_select()
+    total = None
+    for i in range(STRIP_ROWS):
+        y = i - 2
+        for k in range(0, levels + 1, 2):
+            pair = []
+            for level in (k, min(k + 1, levels)):
+                if not 0 <= y < rows:
+                    j = y + HALO if y < 0 else y - rows
+                    pair.append(jnp.where(row_odd == (y < 0), ra_ref[j, level], rb_ref[j, level]))
+                elif level < levels:
+                    pair.append(conc_ref[pl.ds(level * rows + y, bins, stride=levels * rows), :])
+                else:
+                    pair.append(jnp.broadcast_to(mask[y : y + 1], (bins, LANES)))
+            both = jnp.concatenate(pair, axis=0)
+            high = both.astype(BF16)
+            at = slice(k * bins, (k + 2) * bins)
+            high_ref[i % 2, at] = high
+            low_ref[i % 2, at] = (both - high.astype(F32)).astype(BF16)
+        term = jnp.dot(high_ref[i % 2], chosen[i], preferred_element_type=F32) + jnp.dot(
+            low_ref[i % 2], chosen[i], preferred_element_type=F32
+        )
+        total = term if total is None else total + term
+    strip_ref[...] = total[: (levels + 1) * bins]
 
 
 def coefficients(east_w, east, east_e, north_s, north, north_n, valid):
@@ -260,11 +253,11 @@
     ra_ref, rb_ref, own_ref, ca_ref, cb_ref,
     winds_ref, wra_ref, wrb_ref, wown_ref, wca_ref, wcb_ref,
     out_ref, deposit_ref,
-    coef_ref, strip_coef_ref, prof_ref, mask_all_ref, mask_strip_ref, fall_ref, state_ref,
+    coef_ref, strip_coef_ref, edge_ref, bound_ref, source_ref, fall_ref,
 ):
     row, col = lax.axis_index("rows"), lax.axis_index("cols")
     last_row, last_col = lax.axis_size("rows") - 1, lax.axis_size("cols") - 1
-    row_odd = row % 2 == 1
+    row_odd, col_odd = row % 2 == 1, col % 2 == 1
     levels = ra_ref.shape[1] - 1
     bins = ra_ref.shape[2]
     rows = mask_ref.shape[0]
@@ -283,10 +276,13 @@
         j = halo_at(y)
         return halo_of(y, wra_ref[j].astype(F32), wrb_ref[j].astype(F32))
 
-    strip = wown_ref[...].astype(F32) + wca_ref[...].astype(F32) + wcb_ref[...].astype(F32)
-    strip_u, strip_v = strip[:levels], strip[levels:]
     lanes = lane_ids((levels, LANES))
     at = lanes % STRIP
+    wide = lane_ids((2 * levels, LANES)) % STRIP
+    strip = whole_strip(
+        wown_ref[...].astype(F32), wca_ref[...].astype(F32), wcb_ref[...].astype(F32), wide, col_odd
+    )
+    strip_u, strip_v = strip[:levels], strip[levels:]
     inside = (
         ((at >= 3) | (col > 0))
         & ((at < 7) | (col < last_col))
@@ -312,92 +308,142 @@
             valid = row > 0
         elif y >= rows:
             valid = row < last_row
-        found = coefficients(
+        centre, west, east, south, north = coefficients(
             u_w, u, u_e,
             wind_row(y - 1)[levels:], wind_row(y)[levels:], wind_row(y + 1)[levels:],
             valid,
         )
-        for i in range(5):
-            coef_ref[5 * (y + 2) + i] = found[i]
-
-    mask = mask_ref[...].astype(F32)
-    for y in range(-2, rows + 2):
-        if 0 <= y < rows:
-            mask_all_ref[y + 2] = jnp.broadcast_to(mask[y : y + 1], tile)
-        else:
-            j = halo_at(y)
-            mask_all_ref[y + 2] = halo_of(y, ra_ref[j, levels], rb_ref[j, levels])
-    mask_strip_ref[...] = own_ref[levels] + ca_ref[levels] + cb_ref[levels]
+        west = jnp.where(lanes == 0, 0.0, west)
+        east = jnp.where(lanes == LANES - 1, 0.0, east)
+        for i, c in enumerate((centre, west, east, south, north)):
+            coef_ref[5 * (y + 2) + i] = c
+
     sublanes = lax.broadcasted_iota(jnp.int32, tile, 0)
     settle = jnp.zeros(tile, F32)
     for b in range(bins):
         settle = jnp.where(sublanes == b, settle_ref[b], settle)
+
+    tile_lanes = lane_ids(tile)
+    tile_at = tile_lanes % STRIP
+    spare = STRIP * STRIP_ROWS
+
+    def edge_of(k):
+        at_k = pl.ds(k * bins, bins)
+        return whole_strip(own_ref[at_k, :], ca_ref[at_k, :], cb_ref[at_k, :], tile_at, col_odd)
+
+    mask_strip = edge_of(levels)
+    zero = jnp.zeros(tile, F32)
+    fall_before = [zero] * (STEPS - 1)
     for k in range(levels):
-        prof_ref[k] = jnp.broadcast_to(profile_ref[:, k : k + 1], tile)
-    fall_ref[...] = jnp.zeros(fall_ref.shape, F32)
-
-    tile_lanes = lane_ids(tile)
-    at_west = tile_lanes == 0
-    at_east = tile_lanes == LANES - 1
-
-    def level(k, carry):
-        prof = prof_ref[k]
-
-        def spread(ref, i):
-            return ref[i, pl.ds(k, bins, stride=0), :]
-
-        state = {}
-        for y in range(-HALO, rows + HALO):
-            if 0 <= y < rows:
-                state[y] = conc_ref[pl.ds(k * rows + y, bins, stride=stride), :]
-            else:
-                j = halo_at(y)
-                state[y] = halo_of(y, ra_ref[j, k], rb_ref[j, k])
-        edge = own_ref[k] + ca_ref[k] + cb_ref[k]
-        slot = 0
+        edge = edge_of(k)
+        prof = jnp.broadcast_to(profile_ref[:, k : k + 1], tile)
+        parts = []
+        rest = prof
+        for _ in range(3):
+            part = rest.astype(BF16).astype(F32)
+            rest = rest - part
+            parts.append(part)
+        emitted = prof * mask_strip
+        c = [jnp.broadcast_to(strip_coef_ref[i, k : k + 1, :], tile) for i in range(5)]
         for step in range(STEPS):
-            reach = STEPS - 1 - step
-            fresh = {}
-            for y in range(-reach, rows + reach):
-                a = state[y]
-                base = STRIP * (y + 2)
-                a_w = jnp.where(at_west, roll_lanes(edge, -(base + 2)), roll_lanes(a, 1))
-                a_e = jnp.where(
-                    at_east, roll_lanes(edge, LANES - 1 - (base + 7)), roll_lanes(a, -1)
-                )
-                c = [spread(coef_ref, 5 * (y + 2) + i) for i in range(5)]
-                fall = settle * a
-                source = fall_ref[slot] + prof * mask_all_ref[y + 2]
-                fall_ref[slot] = fall
-                fresh[y] = (
-                    (c[0] * a - fall)
-                    + (c[1] * a_w + c[2] * a_e)
-                    + (c[3] * state[y - 1] + c[4] * state[y + 1])
-                    + source
-                )
-                slot += 1
-            if reach:
-                c = [spread(strip_coef_ref, i) for i in range(5)]
+            from_w = c[1] * roll_lanes(edge, 1)
+            from_e = c[2] * roll_lanes(edge, -1)
+            flow = jnp.where(tile_at == 3, from_w, jnp.where(tile_at == 6, from_e, 0.0))
+            for i, part in enumerate(parts):
+                flow = jnp.where(tile_lanes == spare + i, part, flow)
+            flow = jnp.where(tile_lanes >= spare + 3, 0.0, flow)
+            bound_ref[step, k * bins : (k + 1) * bins] = flow
+            if step < STEPS - 1:
                 fall = settle * edge
-                source = fall_ref[slot] + prof * mask_strip_ref[...]
-                fall_ref[slot] = fall
                 edge = (
                     (c[0] * edge - fall)
-                    + (c[1] * roll_lanes(edge, 1) + c[2] * roll_lanes(edge, -1))
+                    + (from_w + from_e)
                     + (c[3] * roll_lanes(edge, STRIP) + c[4] * roll_lanes(edge, -STRIP))
-                    + source
+                    + (fall_before[step] + emitted)
                 )
-                slot += 1
-            state = fresh
-        for y in range(rows):
-            out_ref[pl.ds(k * rows + y, bins, stride=stride), :] = state[y]
+                fall_before[step] = fall
+
+    lane_of = lax.broadcasted_iota(jnp.int32, (LANES, LANES), 0)
+    x_of = lane_ids((LANES, LANES))
+    mask = mask_ref[...].astype(F32)
+    spread = []
+    for y in range(-2, rows + 2):
+        base = STRIP * (y + 2)
+        hit = ((x_of == 0) & (lane_of == base + 3)) | ((x_of == LANES - 1) & (lane_of == base + 6))
+        if 0 <= y < rows:
+            line = mask[y : y + 1]
+        else:
+            j = halo_at(y)
+            line = halo_of(y, ra_ref[j, levels], rb_ref[j, levels])[:1]
+        emits = (lane_of >= spare) & (lane_of < spare + 3)
+        table = jnp.where(hit, 1.0, jnp.where(emits, line, 0.0)).astype(BF16)
+        spread.append(jnp.concatenate([table, table], axis=0))
+    slot = 0
+    slots = {}
+    for step in range(STEPS):
+        flow = bound_ref[step]
+        high = flow.astype(BF16)
+        low = (flow - high.astype(F32)).astype(BF16)
+        both = jnp.concatenate([high, low], axis=1)
+        reach = STEPS - 1 - step
+        for y in range(-reach, rows + reach):
+            slots[step, y] = slot
+            source_ref[slot] = jnp.dot(both, spread[y + 2], preferred_element_type=F32)
+            slot += 1
+
+    fall_ref[...] = jnp.zeros(fall_ref.shape, F32)
+    unroll = 4
+
+    def some_levels(trip, carry):
+        ks = [trip * unroll + u for u in range(unroll)]
+
+        def start_of(y, k):
+            if 0 <= y < rows:
+                return conc_ref[pl.ds(k * rows + y, bins, stride=stride), :]
+            j = halo_at(y)
+            return halo_of(y, ra_ref[j, k], rb_ref[j, k])
+
+        coefs = [{} for _ in ks]
+        states = [[{} for _ in range(STEPS + 1)] for _ in ks]
+        for u, k in enumerate(ks):
+            for y in (-3, -2):
+                states[u][0][y] = start_of(y, k)
+        for front in range(-2, rows + 4):
+            for step in range(STEPS):
+                y = front - step
+                reach = STEPS - 1 - step
+                if not -reach <= y < rows + reach:
+                    continue
+                index = slots[step, y]
+                fall = fall_ref[index]
+                for u, k in enumerate(ks):
+                    state = states[u][step]
+                    if step == 0:
+                        state[y + 1] = start_of(y + 1, k)
+                        coefs[u][y] = [
+                            coef_ref[5 * (y + 2) + i, pl.ds(k, bins, stride=0), :] for i in range(5)
+                        ]
+                    c = coefs[u][y]
+                    a = state[y]
+                    source = source_ref[index, pl.ds(k * bins, bins), :] + fall
+                    fall = settle * a
+                    fresh = (
+                        (c[0] * a - fall)
+                        + (c[1] * roll_lanes(a, 1) + c[2] * roll_lanes(a, -1))
+                        + (c[3] * state[y - 1] + c[4] * state[y + 1])
+                        + source
+                    )
+                    if step < STEPS - 1:
+                        states[u][step + 1][y] = fresh
+                    else:
+                        out_ref[pl.ds(k * rows + y, bins, stride=stride), :] = fresh
+                fall_ref[index] = fall
         return carry
 
-    lax.fori_loop(0, levels, level, 0)
-    first, second, third = 2, rows + 2 * 2 + 1 + 1, (rows + 2 * 2 + 1) + (rows + 2 + 1)
+    lax.fori_loop(0, levels // unroll, some_levels, 0)
     for y in range(rows):
         deposit_ref[pl.ds(y, bins, stride=rows), :] = (
-            fall_ref[first + y] + fall_ref[second + y] + fall_ref[third + y]
+            fall_ref[slots[0, y]] + fall_ref[slots[1, y]] + fall_ref[slots[2, y]]
         )
 
 
@@ -413,14 +459,20 @@
         (lev_lo.reshape(1, -1), frac.reshape(1, -1), pick.reshape(1, -1), nwp),
         flops=2 * 2 * levels * 2048 * 2048,
     )
+
+    flat, sent = lax.optimization_barrier((flat, sent))
     received = lax.all_to_all(sent, "rows", split_axis=0, concat_axis=0, tiled=True)
 
     edge_rows = shape((HALO, levels + 1, bins, cols), F32)
-    strips = shape((levels + 1, bins, LANES), F32)
+    strips = shape(((levels + 1) * bins, LANES), F32)
     ca, cb = call(conc_edge_kernel, (edge_rows, edge_rows), (flat, source_mask))
     ra, rb = swap(ca, "rows", True), swap(cb, "rows", False)
-    own, sa, sb = call(conc_strip_kernel, (strips, strips, strips), (flat, source_mask, ra, rb))
-    xa, xb = swap(sa, "cols", True), swap(sb, "cols", False)
+    padded = (levels + 2) * bins
+    own = call(
+        conc_strip_kernel, strips, (flat, source_mask, ra, rb),
+        scratch=(pltpu.VMEM((2, padded, LANES), BF16), pltpu.VMEM((2, padded, LANES), BF16)),
+    )
+    xa, xb = swap(own, "cols", True), swap(own, "cols", False)
 
     wind_rows = shape((HALO, 2 * levels, cols), BF16)
     winds, wa, wb = call(
@@ -431,14 +483,11 @@
         flops=2 * 2 * 2 * levels * 2048 * 1024,
     )
     wra, wrb = swap(wa, "rows", True), swap(wb, "rows", False)
-    wind_strip = shape((2 * levels, LANES), BF16)
-    wown, wsa, wsb = call(
-        wind_strip_kernel, (wind_strip, wind_strip, wind_strip), (winds, wra, wrb)
-    )
-    wxa, wxb = swap(wsa, "cols", True), swap(wsb, "cols", False)
+    wown = call(wind_strip_kernel, shape((2 * levels, LANES), BF16), (winds, wra, wrb))
+    wxa, wxb = swap(wown, "cols", True), swap(wown, "cols", False)
 
     tile = (bins, LANES)
-    updates = sum(rows + 2 * (STEPS - 1 - s) for s in range(STEPS)) + STEPS - 1
+    updates = sum(rows + 2 * (STEPS - 1 - s) for s in range(STEPS))
     final, deposit = call(
         transport_kernel,
         (shape(flat.shape, F32), shape((bins * rows, cols), F32)),
@@ -447,11 +496,10 @@
         scratch=(
             pltpu.VMEM((5 * (rows + 4), levels, LANES), F32),
             pltpu.VMEM((5, levels, LANES), F32),
-            pltpu.VMEM((levels,) + tile, F32),
-            pltpu.VMEM((rows + 4,) + tile, F32),
             pltpu.VMEM(tile, F32),
+            pltpu.VMEM((STEPS, levels * bins, LANES), F32),
+            pltpu.VMEM((updates, levels * bins, LANES), F32),
             pltpu.VMEM((updates,) + tile, F32),
-            pltpu.VMEM(tile, F32),
         ),
         smem=(2,),
         flops=16 * updates * levels * bins * LANES,

time: 70.5 us -> 61.2 us (0.87)
  the two profiles are of different devices: /device:TPU:10 before, /device:TPU:14 now
where the time goes in v1:
time: 61.2 us; the launch traced here: 60.8 us
  starting transfers between devices  24.8 us (41%)
  Pallas kernels  22.4 us (37%)
  waiting for transfers between devices  10.3 us (17%)
  local copies, waits for them, and re-layouts  2.51 us (4%)
  between operations  0.86 us (1%)
    pallas_call x6, Pallas kernels, call(): pl.pallas_call(kernel, out_shape=out_shape, in_specs=[pl.BlockSpec(memory...  22.4 us
    ppermute x8, starting transfers between devices, swap(): return lax.ppermute(array, axis, pairs)  19.5 us
    ppermute x8, waiting for transfers between devices, swap(): return lax.ppermute(array, axis, pairs)  10.3 us
    all_to_all x1, starting transfers between devices, per_device(): lax.all_to_all(sent, 'rows', split_axis=0, concat_axis=0, tiled=True)  5.23 us
    unnamed x17, local copies, waits for them, and re-layouts  1.71 us
  transfers between devices with their start and end apart: 9, of which 4 were waited for; matrix products, arithmetic and copies ran while one was open for 0% of the time, Pallas kernels for 12%

profile of v1, /device:TPU:14, one launch (start us, length us, event | category | flops | bytes accessed | tf_op | source)
XLA Modules:
  0.0 60.8 jit_solution(15634590507385676823)
XLA Ops:
  0.6 0.0 copy-start.7
  0.6 0.0 copy-start.6
  0.7 0.8 %reshape.25.pick_ref = s32[1,2048]{1,0:T(1,128)S(1)} reshape(s32[1,1,32,64]{3,2,1,0:T(8,128)} %param.14) | data formatting | bytes 16384 | tf_op jit(solution)/shard_map/reshape | solution.py:459
  1.5 1.7 %copy.12.nwp_ref = bf16[2,137,2048]{2,1,0:T(8,128)(2,1)S(1)} copy(bf16[2,137,2048]{2,0,1:T(2,128)(2,1)} %param.11) | data formatting | bytes 2244608 | tf_op args[1]
  3.1 0.0 copy-start
  3.1 0.0 copy-start.1
  3.1 0.0 copy-done.7
  3.2 0.0 copy-done.6
  3.2 3.1 %shard_map.113 = bf16[32,48,128]{2,1,0:T(8,128)(2,1)} custom-call(s32[1,48]{1,0:T(1,128)S(1)} %bitcast.10, f32[1,48]{1,0:T(1,128)S(1)} %bitcast.11, s32[1,2048]{1,0:T(1,128)S(1)} %reshape.25.pick_ref, bf16[2,137,2048]{2,1,0:T(8,128)(2,1)S(1)} %copy.12.nwp_ref), custom_call_target="tpu_custom_call" | custom-call | flops 805306368 | bytes 1524096 | tf_op jit(solution)/shard_map/pallas_call | solution.py:33
  6.3 0.0 copy-done
  6.3 0.0 copy-done.1
  6.3 1.8 %shard_map.114 = (f32[3,49,8,128]{3,2,1,0:T(8,128)}, f32[3,49,8,128]{3,2,1,0:T(8,128)}) custom-call(f32[3072,128]{1,0:T(8,128)S(1)} %bitcast.7, s32[8,128]{1,0:T(8,128)S(1)} %copy-done.1), custom_call_target="tpu_custom_call" | custom-call | bytes 2781184 | tf_op jit(solution)/shard_map/pallas_call | solution.py:33
  8.0 0.0 collective-permute-start
  8.0 6.3 %collective-permute-start.1 = (f32[3,49,8,128]{3,2,1,0:T(8,128)}, f32[3,49,8,128]{3,2,1,0:T(8,128)S(1)}, u32[]{:S(2)}, u32[]{:S(2)}) collective-permute-start(f32[3,49,8,128]{3,2,1,0:T(8,128)} %get-tuple-element.13), channel_id=1, source_target_pairs={{4,8},{8,4},{12,16},{16,12},{20,24},{24,20},{28,32},{32,28},{36,40... | collective-permute-start | bytes 1806344 | tf_op jit(solution)/shard_map/ppermute | solution.py:140
  14.3 5.2 %all-to-all-start = ((bf16[32,48,128]{2,1,0:T(8,128)(2,1)}), bf16[32,48,128]{2,1,0:T(8,128)(2,1)S(1)}, u32[]{:S(2)}, u32[]{:S(2)}) async-start(bf16[32,48,128]{2,1,0:T(8,128)(2,1)} %shard_map.113), calls=%async_computation | async-start | bytes 786432 | tf_op jit(solution)/shard_map/all_to_all | solution.py:464
  19.6 0.0 copy-start.4
  19.6 0.0 copy-start.5
  19.6 0.0 collective-permute-done.ra_ref
  19.6 4.4 %collective-permute-done.1.rb_ref = f32[3,49,8,128]{3,2,1,0:T(8,128)S(1)} collective-permute-done((f32[3,49,8,128]{3,2,1,0:T(8,128)}, f32[3,49,8,128]{3,2,1,0:T(8,128)S(1)}, u32[]{:S(2)}, u32[]{:S(2)}) %collective-permute-start.1) | collective-permute-done | bytes 602144 | tf_op jit(solution)/shard_map/ppermute | solution.py:140
  24.1 2.3 %shard_map.115.own_ref = f32[392,128]{1,0:T(8,128)S(1)} custom-call(f32[3072,128]{1,0:T(8,128)S(1)} %bitcast.8, s32[8,128]{1,0:T(8,128)S(1)} %copy-done.1, f32[3,49,8,128]{3,2,1,0:T(8,128)S(1)} %collective-permute-done.ra_ref, f32[3,49,8,128]{3,2,1,0:T(8,128)S(1)} %collective-permute-done.1.rb_ref), custom_call_target="tpu_custom_call" | custom-call | bytes 2981888 | tf_op jit(solution)/shard_map/pallas_call | solution.py:33
  26.4 0.0 copy-start.2
  26.4 0.0 copy-start.3
  26.4 3.5 %collective-permute-start.3 = (f32[392,128]{1,0:T(8,128)S(1)}, f32[392,128]{1,0:T(8,128)}, u32[]{:S(2)}, u32[]{:S(2)}) collective-permute-start(f32[392,128]{1,0:T(8,128)S(1)} %shard_map.115.own_ref), channel_id=1, source_target_pairs={{1,2},{2,1},{5,6},{6,5},{9,10},{10,9},{13,14},{14,13},{17,18},{18,... | collective-permute-start | bytes 602120 | tf_op jit(solution)/shard_map/ppermute | solution.py:140
  29.9 0.1 collective-permute-start.2
  30.0 0.0 all-to-all-done.recv_ref
  30.0 0.0 copy-done.4
  30.0 0.0 copy-done.5
  30.0 5.0 %shard_map.116 = (f32[8,96,128]{2,1,0:T(8,128)S(1)}, bf16[3,96,128]{2,1,0:T(8,128)(2,1)S(1)}, bf16[3,96,128]{2,1,0:T(8,128)(2,1)S(1)}) custom-call(bf16[32,48,128]{2,1,0:T(8,128)(2,1)S(1)} %all-to-all-done.recv_ref, s32[4,8,128]{2,1,0:T(8,128)S(1)} %copy-done.4, f32[4,8,128]{2,1,0:T(8,128)S(1)} %copy-done.5), custom_call_target="tpu_custom_call" | custom-call | flops 805306368 | bytes 966656 | tf_op jit(solution)/shard_map/pallas_call | solution.py:33
  35.0 0.1 collective-permute-start.4
  35.1 6.8 %collective-permute-start.5 = (bf16[3,96,128]{2,1,0:T(8,128)(2,1)S(1)}, bf16[3,96,128]{2,1,0:T(8,128)(2,1)S(1)}, u32[]{:S(2)}, u32[]{:S(2)}) collective-permute-start(bf16[3,96,128]{2,1,0:T(8,128)(2,1)S(1)} %get-tuple-element.17), channel_id=1, source_target_pairs={{4,8},{8,4},{12,16},{16,12},{20,24},{24,20},{28,32},{32,28},{36,40... | collective-permute-start | bytes 221192 | tf_op jit(solution)/shard_map/ppermute | solution.py:140
  41.9 0.0 collective-permute-done.4.ra_ref.wra_ref
  41.9 2.0 %collective-permute-done.5.rb_ref.wrb_ref = bf16[3,96,128]{2,1,0:T(8,128)(2,1)S(1)} collective-permute-done((bf16[3,96,128]{2,1,0:T(8,128)(2,1)S(1)}, bf16[3,96,128]{2,1,0:T(8,128)(2,1)S(1)}, u32[]{:S(2)}, u32[]{:S(2)}) %collective-permute-start.5) | collective-permute-done | bytes 73760 | tf_op jit(solution)/shard_map/ppermute | solution.py:140
  43.9 0.3 shard_map.117.wown_ref
  44.2 2.5 %collective-permute-start.7 = (bf16[96,128]{1,0:T(8,128)(2,1)S(1)}, bf16[96,128]{1,0:T(8,128)(2,1)S(1)}, u32[]{:S(2)}, u32[]{:S(2)}) collective-permute-start(bf16[96,128]{1,0:T(8,128)(2,1)S(1)} %shard_map.117.wown_ref), channel_id=1, source_target_pairs={{1,2},{2,1},{5,6},{6,5},{9,10},{10,9},{13,14},{14,13},{17,18},{18,... | collective-permute-start | bytes 73736 | tf_op jit(solution)/shard_map/ppermute | solution.py:140
  46.7 0.3 collective-permute-start.6
  47.0 2.9 %collective-permute-done.7.wcb_ref = bf16[96,128]{1,0:T(8,128)(2,1)S(1)} collective-permute-done((bf16[96,128]{1,0:T(8,128)(2,1)S(1)}, bf16[96,128]{1,0:T(8,128)(2,1)S(1)}, u32[]{:S(2)}, u32[]{:S(2)}) %collective-permute-start.7) | collective-permute-done | bytes 24608 | tf_op jit(solution)/shard_map/ppermute | solution.py:140
  49.9 0.9 %collective-permute-done.6.wca_ref = bf16[96,128]{1,0:T(8,128)(2,1)S(1)} collective-permute-done((bf16[96,128]{1,0:T(8,128)(2,1)S(1)}, bf16[96,128]{1,0:T(8,128)(2,1)S(1)}, u32[]{:S(2)}, u32[]{:S(2)}) %collective-permute-start.6) | collective-permute-done | bytes 24608 | tf_op jit(solution)/shard_map/ppermute | solution.py:140
  50.8 0.0 collective-permute-done.3.cb_ref
  50.8 0.0 collective-permute-done.2.ca_ref
  50.8 0.0 copy-done.2
  50.8 0.0 copy-done.3
  50.8 10.0 %shard_map.118 = (f32[3072,128]{1,0:T(8,128)}, f32[64,128]{1,0:T(8,128)}) custom-call(f32[3072,128]{1,0:T(8,128)S(1)} %bitcast.9, s32[8,128]{1,0:T(8,128)S(1)} %copy-done.1, f32[8]{0:T(128)S(1)} %copy-done.3, f32[8,48]{1,0:T(8,128)S(1)} %copy-done.2, f32[3,49,8,128]{3,2,1,0:T(8,128)S(1)} %collective-permute-done.ra_ref, ...), custom_call_target="tpu_custom_call" | custom-call | flops 23592960 | bytes 5604896 | tf_op jit(solution)/shard_map/pallas_call | solution.py:33
Async XLA Ops:
  0.6 2.5 %copy-start.7 = (f32[48]{0:T(128)S(1)}, f32[48]{0:T(128)}, u32[]{:S(2)}) copy-start(f32[48]{0:T(128)} %param.13) | copy-start | bytes 580
  0.6 2.5 %copy-start.6 = (s32[48]{0:T(128)S(1)}, s32[48]{0:T(128)}, u32[]{:S(2)}) copy-start(s32[48]{0:T(128)} %param.12) | copy-start | bytes 580
  3.1 3.1 %copy-start = (f32[8,48,8,128]{3,2,1,0:T(8,128)S(1)}, f32[8,48,8,128]{3,2,1,0:T(8,128)}, u32[]{:S(2)}) copy-start(f32[8,48,8,128]{3,2,1,0:T(8,128)} %param.10) | copy-start | bytes 4718596
  3.1 3.1 %copy-start.1 = (s32[8,128]{1,0:T(8,128)S(1)}, s32[8,128]{1,0:T(8,128)}, u32[]{:S(2)}) copy-start(s32[8,128]{1,0:T(8,128)} %mask_ref.5) | copy-start | bytes 12292
  8.0 11.6 %collective-permute-start = (f32[3,49,8,128]{3,2,1,0:T(8,128)}, f32[3,49,8,128]{3,2,1,0:T(8,128)S(1)}, u32[]{:S(2)}, u32[]{:S(2)}) collective-permute-start(f32[3,49,8,128]{3,2,1,0:T(8,128)} %get-tuple-element.12), channel_id=1, source_target_pairs={{0,4},{4,0},{8,12},{12,8},{16,20},{20,16},{24,28},{28,24},{32,36},... | collective-permute-start | bytes 1806344 | tf_op jit(solution)/shard_map/ppermute | solution.py:140
  8.0 16.0 %collective-permute-start.1 = (f32[3,49,8,128]{3,2,1,0:T(8,128)}, f32[3,49,8,128]{3,2,1,0:T(8,128)S(1)}, u32[]{:S(2)}, u32[]{:S(2)}) collective-permute-start(f32[3,49,8,128]{3,2,1,0:T(8,128)} %get-tuple-element.13), channel_id=1, source_target_pairs={{4,8},{8,4},{12,16},{16,12},{20,24},{24,20},{28,32},{32,28},{36,40... | collective-permute-start | bytes 1806344 | tf_op jit(solution)/shard_map/ppermute | solution.py:140
  14.3 15.6 %all-to-all-start = ((bf16[32,48,128]{2,1,0:T(8,128)(2,1)}), bf16[32,48,128]{2,1,0:T(8,128)(2,1)S(1)}, u32[]{:S(2)}, u32[]{:S(2)}) async-start(bf16[32,48,128]{2,1,0:T(8,128)(2,1)} %shard_map.113), calls=%async_computation | async-start | bytes 786432 | tf_op jit(solution)/shard_map/all_to_all | solution.py:464
  19.6 10.4 %copy-start.4 = (s32[4,8,128]{2,1,0:T(8,128)S(1)}, s32[4,8,128]{2,1,0:T(8,128)}, u32[]{:S(2)}) copy-start(s32[4,8,128]{2,1,0:T(8,128)} %slot_ref.1) | copy-start | bytes 49156
  19.6 10.4 %copy-start.5 = (f32[4,8,128]{2,1,0:T(8,128)S(1)}, f32[4,8,128]{2,1,0:T(8,128)}, u32[]{:S(2)}) copy-start(f32[4,8,128]{2,1,0:T(8,128)} %wt_ref.1) | copy-start | bytes 49156
  26.4 24.4 %copy-start.2 = (f32[8,48]{1,0:T(8,128)S(1)}, f32[8,48]{1,0:T(8,128)}, u32[]{:S(2)}) copy-start(f32[8,48]{1,0:T(8,128)} %profile_ref.1) | copy-start | bytes 4612
  26.4 24.4 %copy-start.3 = (f32[8]{0:T(128)S(1)}, f32[8]{0:T(128)}, u32[]{:S(2)}) copy-start(f32[8]{0:T(128)} %settle_ref.1) | copy-start | bytes 100
  26.4 24.4 %collective-permute-start.3 = (f32[392,128]{1,0:T(8,128)S(1)}, f32[392,128]{1,0:T(8,128)}, u32[]{:S(2)}, u32[]{:S(2)}) collective-permute-start(f32[392,128]{1,0:T(8,128)S(1)} %shard_map.115.own_ref), channel_id=1, source_target_pairs={{1,2},{2,1},{5,6},{6,5},{9,10},{10,9},{13,14},{14,13},{17,18},{18,... | collective-permute-start | bytes 602120 | tf_op jit(solution)/shard_map/ppermute | solution.py:140
  29.9 20.9 %collective-permute-start.2 = (f32[392,128]{1,0:T(8,128)S(1)}, f32[392,128]{1,0:T(8,128)}, u32[]{:S(2)}, u32[]{:S(2)}) collective-permute-start(f32[392,128]{1,0:T(8,128)S(1)} %shard_map.115.own_ref), channel_id=1, source_target_pairs={{0,1},{1,0},{2,3},{3,2},{4,5},{5,4},{6,7},{7,6},{8,9},{9,8},{10,11... | collective-permute-start | bytes 602120 | tf_op jit(solution)/shard_map/ppermute | solution.py:140
  35.0 6.9 %collective-permute-start.4 = (bf16[3,96,128]{2,1,0:T(8,128)(2,1)S(1)}, bf16[3,96,128]{2,1,0:T(8,128)(2,1)S(1)}, u32[]{:S(2)}, u32[]{:S(2)}) collective-permute-start(bf16[3,96,128]{2,1,0:T(8,128)(2,1)S(1)} %get-tuple-element.16), channel_id=1, source_target_pairs={{0,4},{4,0},{8,12},{12,8},{16,20},{20,16},{24,28},{28,24},{32,36},... | collective-permute-start | bytes 221192 | tf_op jit(solution)/shard_map/ppermute | solution.py:140
  35.1 8.8 %collective-permute-start.5 = (bf16[3,96,128]{2,1,0:T(8,128)(2,1)S(1)}, bf16[3,96,128]{2,1,0:T(8,128)(2,1)S(1)}, u32[]{:S(2)}, u32[]{:S(2)}) collective-permute-start(bf16[3,96,128]{2,1,0:T(8,128)(2,1)S(1)} %get-tuple-element.17), channel_id=1, source_target_pairs={{4,8},{8,4},{12,16},{16,12},{20,24},{24,20},{28,32},{32,28},{36,40... | collective-permute-start | bytes 221192 | tf_op jit(solution)/shard_map/ppermute | solution.py:140
  44.2 5.7 %collective-permute-start.7 = (bf16[96,128]{1,0:T(8,128)(2,1)S(1)}, bf16[96,128]{1,0:T(8,128)(2,1)S(1)}, u32[]{:S(2)}, u32[]{:S(2)}) collective-permute-start(bf16[96,128]{1,0:T(8,128)(2,1)S(1)} %shard_map.117.wown_ref), channel_id=1, source_target_pairs={{1,2},{2,1},{5,6},{6,5},{9,10},{10,9},{13,14},{14,13},{17,18},{18,... | collective-permute-start | bytes 73736 | tf_op jit(solution)/shard_map/ppermute | solution.py:140
  46.7 4.1 %collective-permute-start.6 = (bf16[96,128]{1,0:T(8,128)(2,1)S(1)}, bf16[96,128]{1,0:T(8,128)(2,1)S(1)}, u32[]{:S(2)}, u32[]{:S(2)}) collective-permute-start(bf16[96,128]{1,0:T(8,128)(2,1)S(1)} %shard_map.117.wown_ref), channel_id=1, source_target_pairs={{0,1},{1,0},{2,3},{3,2},{4,5},{5,4},{6,7},{7,6},{8,9},{9,8},{10,11... | collective-permute-start | bytes 73736 | tf_op jit(solution)/shard_map/ppermute | solution.py:140

commit v2 on v1

--- a/solution.py
+++ b/solution.py
@@ -15,7 +15,9 @@
 STRIP_ROWS = 12
 F32 = jnp.float32
 BF16 = jnp.bfloat16
-VMEM_LIMIT = 48 * 1024 * 1024
+SPLIT = 64
+MIB = 1024 * 1024
+HIDES = 50_000_000_000
 
 
 def lane_ids(shape):
@@ -26,10 +28,11 @@
     return pltpu.roll(x, shift % LANES, x.ndim - 1)
 
 
-def call(kernel, out_shape, args, scratch=(), flops=0, smem=()):
-    moved = sum(a.size * a.dtype.itemsize for a in args) + sum(
-        s.size * s.dtype.itemsize for s in jax.tree.leaves(out_shape)
-    )
+def call(kernel, out_shape, args, scratch=(), flops=0, smem=(), limit=16, moved=None, out_space=pltpu.VMEM):
+    if moved is None:
+        moved = sum(a.size * a.dtype.itemsize for a in args) + sum(
+            s.size * s.dtype.itemsize for s in jax.tree.leaves(out_shape)
+        )
     return pl.pallas_call(
         kernel,
         out_shape=out_shape,
@@ -37,14 +40,14 @@
             pl.BlockSpec(memory_space=pltpu.SMEM if i in smem else pltpu.VMEM)
             for i in range(len(args))
         ],
-        out_specs=jax.tree.map(lambda _: pl.BlockSpec(memory_space=pltpu.VMEM), out_shape),
+        out_specs=jax.tree.map(lambda _: pl.BlockSpec(memory_space=out_space), out_shape),
         scratch_shapes=list(scratch),
-        compiler_params=pltpu.CompilerParams(vmem_limit_bytes=VMEM_LIMIT),
+        compiler_params=pltpu.CompilerParams(vmem_limit_bytes=limit * MIB),
         cost_estimate=pl.CostEstimate(flops=flops, bytes_accessed=moved, transcendentals=0),
     )(*args)
 
 
-def select_kernel(lev_ref, frac_ref, pick_ref, nwp_ref, out_ref):
+def select_kernel(lev_ref, frac_ref, pick_ref, nwp_ref, sent_ref, out_ref, sem):
     fields, levels_in, count = nwp_ref.shape
     kept = lev_ref.shape[1]
     ids = lax.broadcasted_iota(jnp.int32, (levels_in, kept), 0)
@@ -67,11 +70,16 @@
     levels = jnp.concatenate(rows, axis=0)
     half = LANES // 2
     width = 2 * LANES
-    columns = lax.broadcasted_iota(jnp.int32, (count, width), 0)
+    inner = lax.broadcasted_iota(jnp.int32, (SPLIT, width), 0)
+    none = jnp.zeros((SPLIT, width), BF16)
     first = lane_ids((kept, LANES)) < half
-    for block in range(pick_ref.shape[1] // width):
-        wanted = pick_ref[:, block * width : (block + 1) * width]
-        hit = jnp.where(columns == wanted, 1.0, 0.0).astype(BF16)
+    copies = []
+    for block in range(pick_ref.shape[0] // 4):
+        wanted = jnp.concatenate([pick_ref[4 * block + i : 4 * block + i + 1] for i in range(4)], axis=1)
+        group = wanted // SPLIT
+        unit = jnp.where(inner == wanted - group * SPLIT, 1.0, 0.0).astype(BF16)
+        group = jnp.broadcast_to(group.astype(F32), (SPLIT, width)).astype(BF16)
+        hit = jnp.concatenate([jnp.where(group == g, unit, none) for g in range(count // SPLIT)], axis=0)
         got = jnp.dot(levels, hit, preferred_element_type=F32)
         for h in range(2):
             east = got[:kept, h * LANES : (h + 1) * LANES]
@@ -80,6 +88,50 @@
             out_ref[4 * block + 2 * h + 1] = jnp.where(
                 first, roll_lanes(east, half), north
             ).astype(BF16)
+        at = pl.ds(4 * block, 4)
+        copies.append(pltpu.make_async_copy(out_ref.at[at], sent_ref.at[at], sem.at[block]))
+        copies[-1].start()
+    for copy in copies:
+        copy.wait()
+
+
+def corner_tables(slot_ref, wt_ref, count):
+    slots = [slot_ref[q] for q in range(4)]
+    raw = [wt_ref[q] for q in range(4)]
+    total = raw[0] + raw[1] + raw[2] + raw[3]
+    norm = [w / total for w in raw]
+    groups, units, highs, lows = [], [], [], []
+    for q in range(4):
+        share = None
+        for other in range(4):
+            term = jnp.where(slots[q] == slots[other], norm[other], 0.0)
+            share = term if share is None else share + term
+        for other in range(q):
+            share = jnp.where(slots[q] == slots[other], 0.0, share)
+        high = share.astype(BF16).astype(F32)
+        group = slots[q] // SPLIT
+        groups.append(group.astype(F32))
+        units.append(slots[q] - group * SPLIT)
+        highs.append(high)
+        lows.append(share - high)
+    inner = lax.broadcasted_iota(jnp.int32, (SPLIT, LANES), 0)
+    none = jnp.zeros((SPLIT, LANES), BF16)
+
+    def tables(y):
+        line = slice(y, y + 1)
+        hits = [inner == units[q][line] for q in range(4)]
+        group = [jnp.broadcast_to(groups[q][line], (SPLIT, LANES)).astype(BF16) for q in range(4)]
+        result = []
+        for parts in (highs, lows):
+            own = [jnp.where(hits[q], parts[q][line], 0.0).astype(BF16) for q in range(4)]
+            blocks = []
+            for g in range(count // SPLIT):
+                two = [jnp.where(group[q] == g, own[q], none) for q in range(4)]
+                blocks.append((two[0] + two[1]) + (two[2] + two[3]))
+            result.append(jnp.concatenate(blocks, axis=0))
+        return result
+
+    return tables
 
 
 def horizontal_kernel(recv_ref, slot_ref, wt_ref, winds_ref, a_ref, b_ref, lev_ref):
@@ -92,37 +144,17 @@
         at = slice(pair * LANES, (pair + 1) * LANES)
         lev_ref[:kept, at] = jnp.where(first, one, roll_lanes(two, half)).astype(BF16)
         lev_ref[kept:, at] = jnp.where(first, roll_lanes(one, half), two).astype(BF16)
-    slots = [slot_ref[q] for q in range(4)]
-    raw = [wt_ref[q] for q in range(4)]
-    total = raw[0] + raw[1] + raw[2] + raw[3]
-    norm = [w / total for w in raw]
-    merged = []
-    for q in range(4):
-        share = None
-        for other in range(4):
-            term = jnp.where(slots[q] == slots[other], norm[other], 0.0)
-            share = term if share is None else share + term
-        merged.append(share)
-    count = lev_ref.shape[1]
-    chunk = 512
-    rows = slot_ref.shape[1]
-    for y in range(rows):
-        acc = None
-        for base in range(0, count, chunk):
-            ids = lax.broadcasted_iota(jnp.int32, (chunk, LANES), 0) + base
-            table = jnp.zeros((chunk, LANES), F32)
-            for q in range(4):
-                table = jnp.where(
-                    ids == slots[q][y : y + 1], merged[q][y : y + 1], table
-                )
-            high = table.astype(BF16)
-            low = (table - high.astype(F32)).astype(BF16)
-            lev = lev_ref[:, base : base + chunk]
-            term = jnp.dot(lev, high, preferred_element_type=F32) + jnp.dot(
-                lev, low, preferred_element_type=F32
-            )
-            acc = term if acc is None else acc + term
-        winds_ref[y] = acc
+    rows = winds_ref.shape[0]
+    lev = lev_ref[...]
+    tables = corner_tables(slot_ref, wt_ref, lev_ref.shape[1])
+    for y in range(0, rows, 2):
+        one, two = tables(y), tables(y + 1)
+        got = sum(
+            jnp.dot(lev, jnp.concatenate(pair, axis=1), preferred_element_type=F32)
+            for pair in zip(one, two)
+        )
+        winds_ref[y] = got[:, :LANES]
+        winds_ref[y + 1] = got[:, LANES:]
     odd = lax.axis_index("rows") % 2 == 1
     for j in range(HALO):
         upper = winds_ref[j]
@@ -386,13 +418,16 @@
         low = (flow - high.astype(F32)).astype(BF16)
         both = jnp.concatenate([high, low], axis=1)
         reach = STEPS - 1 - step
-        for y in range(-reach, rows + reach):
-            slots[step, y] = slot
-            source_ref[slot] = jnp.dot(both, spread[y + 2], preferred_element_type=F32)
-            slot += 1
+        for y in range(-reach, rows + reach, 2):
+            pair = jnp.concatenate([spread[y + 2], spread[y + 3]], axis=1)
+            got = jnp.dot(both, pair, preferred_element_type=F32)
+            for side in range(2):
+                slots[step, y + side] = slot
+                source_ref[slot] = got[:, side * LANES : (side + 1) * LANES]
+                slot += 1
 
     fall_ref[...] = jnp.zeros(fall_ref.shape, F32)
-    unroll = 4
+    unroll = 8
 
     def some_levels(trip, carry):
         ks = [trip * unroll + u for u in range(unroll)]
@@ -423,12 +458,13 @@
                         coefs[u][y] = [
                             coef_ref[5 * (y + 2) + i, pl.ds(k, bins, stride=0), :] for i in range(5)
                         ]
+                        coefs[u][y][0] = coefs[u][y][0] - settle
                     c = coefs[u][y]
                     a = state[y]
                     source = source_ref[index, pl.ds(k * bins, bins), :] + fall
                     fall = settle * a
                     fresh = (
-                        (c[0] * a - fall)
+                        c[0] * a
                         + (c[1] * roll_lanes(a, 1) + c[2] * roll_lanes(a, -1))
                         + (c[3] * state[y - 1] + c[4] * state[y + 1])
                         + source
@@ -456,7 +492,12 @@
     sent = call(
         select_kernel,
         shape((peers, levels, LANES), BF16),
-        (lev_lo.reshape(1, -1), frac.reshape(1, -1), pick.reshape(1, -1), nwp),
+        (lev_lo.reshape(1, -1), frac.reshape(1, -1), pick.reshape(peers, -1), nwp),
+        scratch=(
+            pltpu.VMEM((peers, levels, LANES), BF16),
+            pltpu.SemaphoreType.DMA((peers // 4,)),
+        ),
+        out_space=pltpu.HBM,
         flops=2 * 2 * levels * 2048 * 2048,
     )
 
@@ -464,15 +505,8 @@
     received = lax.all_to_all(sent, "rows", split_axis=0, concat_axis=0, tiled=True)
 
     edge_rows = shape((HALO, levels + 1, bins, cols), F32)
-    strips = shape(((levels + 1) * bins, LANES), F32)
-    ca, cb = call(conc_edge_kernel, (edge_rows, edge_rows), (flat, source_mask))
+    ca, cb = call(conc_edge_kernel, (edge_rows, edge_rows), (flat, source_mask), moved=0)
     ra, rb = swap(ca, "rows", True), swap(cb, "rows", False)
-    padded = (levels + 2) * bins
-    own = call(
-        conc_strip_kernel, strips, (flat, source_mask, ra, rb),
-        scratch=(pltpu.VMEM((2, padded, LANES), BF16), pltpu.VMEM((2, padded, LANES), BF16)),
-    )
-    xa, xb = swap(own, "cols", True), swap(own, "cols", False)
 
     wind_rows = shape((HALO, 2 * levels, cols), BF16)
     winds, wa, wb = call(
@@ -480,10 +514,23 @@
         (shape((rows, 2 * levels, cols), F32), wind_rows, wind_rows),
         (received, corner_slot, corner_wt),
         scratch=(pltpu.VMEM((2 * levels, peers * LANES // 2), BF16),),
-        flops=2 * 2 * 2 * levels * 2048 * 1024,
+        flops=HIDES,
+        limit=20,
     )
     wra, wrb = swap(wa, "rows", True), swap(wb, "rows", False)
-    wown = call(wind_strip_kernel, shape((2 * levels, LANES), BF16), (winds, wra, wrb))
+
+    ra, rb, wa = lax.optimization_barrier((ra, rb, wa))
+    strips = shape(((levels + 1) * bins, LANES), F32)
+    padded = (levels + 2) * bins
+    own = call(
+        conc_strip_kernel, strips, (flat, source_mask, ra, rb),
+        scratch=(pltpu.VMEM((2, padded, LANES), BF16), pltpu.VMEM((2, padded, LANES), BF16)),
+        moved=0,
+    )
+    xa, xb = swap(own, "cols", True), swap(own, "cols", False)
+    wown = call(
+        wind_strip_kernel, shape((2 * levels, LANES), BF16), (winds, wra, wrb), flops=HIDES
+    )
     wxa, wxb = swap(wown, "cols", True), swap(wown, "cols", False)
 
     tile = (bins, LANES)
@@ -503,6 +550,7 @@
         ),
         smem=(2,),
         flops=16 * updates * levels * bins * LANES,
+        limit=32,
     )
     return final.reshape(conc.shape), deposit.reshape(bins, rows, cols)
 

time: 61.2 us -> 52.9 us (0.86)
  the two profiles are of different devices: /device:TPU:14 before, /device:TPU:10 now
where the time goes in v2:
time: 52.9 us; the launch traced here: 52.6 us
  starting transfers between devices  24 us (45%)
  Pallas kernels  19.1 us (36%)
  waiting for transfers between devices  6.83 us (13%)
  local copies, waits for them, and re-layouts  1.73 us (3%)
  between operations  0.88 us (2%)
    pallas_call x6, Pallas kernels, call(): pl.pallas_call(kernel, out_shape=out_shape, in_specs=[pl.BlockSpec(memory...  19.1 us
    ppermute x8, starting transfers between devices, swap(): return lax.ppermute(array, axis, pairs)  15.5 us
    all_to_all x1, starting transfers between devices, per_device(): lax.all_to_all(sent, 'rows', split_axis=0, concat_axis=0, tiled=True)  8.47 us
    ppermute x8, waiting for transfers between devices, swap(): return lax.ppermute(array, axis, pairs)  4.57 us
    all_to_all x1, waiting for transfers between devices, per_device(): lax.all_to_all(sent, 'rows', split_axis=0, concat_axis=0, tiled=True)  2.25 us
    unnamed x19, local copies, waits for them, and re-layouts  1.73 us
  transfers between devices with their start and end apart: 9, of which 3 were waited for; matrix products, arithmetic and copies ran while one was open for 0% of the time, Pallas kernels for 16%

profile of v2, /device:TPU:10, one launch (start us, length us, event | category | flops | bytes accessed | tf_op | source)
XLA Modules:
  0.0 52.6 jit_solution(3512965860080185675)
XLA Ops:
  0.6 0.0 copy-start.4
  0.6 0.0 copy-start.8
  0.7 0.0 copy-start.7
  0.7 1.7 %copy.12.nwp_ref = bf16[2,137,2048]{2,1,0:T(8,128)(2,1)S(1)} copy(bf16[2,137,2048]{2,0,1:T(2,128)(2,1)} %param.11) | data formatting | bytes 2244608 | tf_op args[1]
  2.3 0.0 copy-done.4
  2.4 0.0 copy-done.8
  2.4 0.0 copy-done.7
  2.4 0.0 copy-start
  2.4 0.0 copy-start.1
  2.4 2.8 %shard_map.113 = bf16[32,48,128]{2,1,0:T(8,128)(2,1)} custom-call(s32[1,48]{1,0:T(1,128)S(1)} %bitcast.10, f32[1,48]{1,0:T(1,128)S(1)} %bitcast.11, s32[32,64]{1,0:T(8,128)S(1)} %bitcast.9, bf16[2,137,2048]{2,1,0:T(8,128)(2,1)S(1)} %copy.12.nwp_ref), custom_call_target="tpu_custom_call" | custom-call | flops 805306368 | bytes 1524096 | tf_op jit(solution)/shard_map/pallas_call | solution.py:36
  5.2 0.0 copy-start.5
  5.2 0.0 copy-start.6
  5.3 8.5 %all-to-all-start = ((bf16[32,48,128]{2,1,0:T(8,128)(2,1)}), bf16[32,48,128]{2,1,0:T(8,128)(2,1)S(1)}, u32[]{:S(2)}, u32[]{:S(2)}) async-start(bf16[32,48,128]{2,1,0:T(8,128)(2,1)} %shard_map.113), calls=%async_computation | async-start | bytes 786432 | tf_op jit(solution)/shard_map/all_to_all | solution.py:505
  13.7 0.0 copy-done
  13.7 0.0 copy-done.1
  13.8 1.8 %shard_map.114 = (f32[3,49,8,128]{3,2,1,0:T(8,128)}, f32[3,49,8,128]{3,2,1,0:T(8,128)}) custom-call(f32[3072,128]{1,0:T(8,128)S(1)} %bitcast.6, s32[8,128]{1,0:T(8,128)S(1)} %copy-done.1), custom_call_target="tpu_custom_call" | custom-call | tf_op jit(solution)/shard_map/pallas_call | solution.py:36
  15.5 0.1 collective-permute-start
  15.7 4.5 %collective-permute-start.1 = (f32[3,49,8,128]{3,2,1,0:T(8,128)}, f32[3,49,8,128]{3,2,1,0:T(8,128)S(1)}, u32[]{:S(2)}, u32[]{:S(2)}) collective-permute-start(f32[3,49,8,128]{3,2,1,0:T(8,128)} %get-tuple-element.15), channel_id=1, source_target_pairs={{4,8},{8,4},{12,16},{16,12},{20,24},{24,20},{28,32},{32,28},{36,40... | collective-permute-start | bytes 1806344 | tf_op jit(solution)/shard_map/ppermute | solution.py:172
  20.2 2.3 %all-to-all-done.recv_ref = bf16[32,48,128]{2,1,0:T(8,128)(2,1)S(1)} async-done(((bf16[32,48,128]{2,1,0:T(8,128)(2,1)}), bf16[32,48,128]{2,1,0:T(8,128)(2,1)S(1)}, u32[]{:S(2)}, u32[]{:S(2)}) %all-to-all-start) | async-done | bytes 393248 | tf_op jit(solution)/shard_map/all_to_all | solution.py:505
  22.5 0.0 copy-done.5
  22.5 0.0 copy-done.6
  22.5 4.0 %shard_map.115 = (f32[8,96,128]{2,1,0:T(8,128)S(1)}, bf16[3,96,128]{2,1,0:T(8,128)(2,1)S(1)}, bf16[3,96,128]{2,1,0:T(8,128)(2,1)S(1)}) custom-call(bf16[32,48,128]{2,1,0:T(8,128)(2,1)S(1)} %all-to-all-done.recv_ref, s32[4,8,128]{2,1,0:T(8,128)S(1)} %copy-done.5, f32[4,8,128]{2,1,0:T(8,128)S(1)} %copy-done.6), custom_call_target="tpu_custom_call" | custom-call | flops 49999998976 | bytes 966656 | tf_op jit(solution)/shard_map/pallas_call | solution.py:36
  26.4 4.4 %collective-permute-start.5 = (bf16[3,96,128]{2,1,0:T(8,128)(2,1)S(1)}, bf16[3,96,128]{2,1,0:T(8,128)(2,1)S(1)}, u32[]{:S(2)}, u32[]{:S(2)}) collective-permute-start(bf16[3,96,128]{2,1,0:T(8,128)(2,1)S(1)} %get-tuple-element.21), channel_id=1, source_target_pairs={{4,8},{8,4},{12,16},{16,12},{20,24},{24,20},{28,32},{32,28},{36,40... | collective-permute-start | bytes 221192 | tf_op jit(solution)/shard_map/ppermute | solution.py:172
  30.9 0.1 collective-permute-start.4
  31.0 0.0 collective-permute-done.ra_ref
  31.0 0.0 collective-permute-done.1.rb_ref
  31.0 2.3 %shard_map.116.own_ref = f32[392,128]{1,0:T(8,128)S(1)} custom-call(f32[3072,128]{1,0:T(8,128)S(1)} %bitcast.7, s32[8,128]{1,0:T(8,128)S(1)} %copy-done.1, f32[3,49,8,128]{3,2,1,0:T(8,128)S(1)} %collective-permute-done.ra_ref, f32[3,49,8,128]{3,2,1,0:T(8,128)S(1)} %collective-permute-done.1.rb_ref), custom_call_target="tpu_custom_call" | custom-call | tf_op jit(solution)/shard_map/pallas_call | solution.py:36
  33.3 3.5 %collective-permute-start.3 = (f32[392,128]{1,0:T(8,128)S(1)}, f32[392,128]{1,0:T(8,128)S(1)}, u32[]{:S(2)}, u32[]{:S(2)}) collective-permute-start(f32[392,128]{1,0:T(8,128)S(1)} %shard_map.116.own_ref), channel_id=1, source_target_pairs={{1,2},{2,1},{5,6},{6,5},{9,10},{10,9},{13,14},{14,13},{17,18},{18,... | collective-permute-start | bytes 602120 | tf_op jit(solution)/shard_map/ppermute | solution.py:172
  36.8 0.1 collective-permute-start.2
  36.9 0.0 collective-permute-done.5.rb_ref.wrb_ref
  36.9 0.0 collective-permute-done.4.ra_ref.wra_ref
  36.9 0.0 copy-start.2
  36.9 0.0 copy-start.3
  36.9 0.3 shard_map.117.wown_ref
  37.2 2.3 %collective-permute-start.7 = (bf16[96,128]{1,0:T(8,128)(2,1)S(1)}, bf16[96,128]{1,0:T(8,128)(2,1)S(1)}, u32[]{:S(2)}, u32[]{:S(2)}) collective-permute-start(bf16[96,128]{1,0:T(8,128)(2,1)S(1)} %shard_map.117.wown_ref), channel_id=1, source_target_pairs={{1,2},{2,1},{5,6},{6,5},{9,10},{10,9},{13,14},{14,13},{17,18},{18,... | collective-permute-start | bytes 73736 | tf_op jit(solution)/shard_map/ppermute | solution.py:172
  39.6 0.4 collective-permute-start.6
  40.0 3.2 %collective-permute-done.7.wcb_ref = bf16[96,128]{1,0:T(8,128)(2,1)S(1)} collective-permute-done((bf16[96,128]{1,0:T(8,128)(2,1)S(1)}, bf16[96,128]{1,0:T(8,128)(2,1)S(1)}, u32[]{:S(2)}, u32[]{:S(2)}) %collective-permute-start.7) | collective-permute-done | bytes 24608 | tf_op jit(solution)/shard_map/ppermute | solution.py:172
  43.1 1.4 %collective-permute-done.6.wca_ref = bf16[96,128]{1,0:T(8,128)(2,1)S(1)} collective-permute-done((bf16[96,128]{1,0:T(8,128)(2,1)S(1)}, bf16[96,128]{1,0:T(8,128)(2,1)S(1)}, u32[]{:S(2)}, u32[]{:S(2)}) %collective-permute-start.6) | collective-permute-done | bytes 24608 | tf_op jit(solution)/shard_map/ppermute | solution.py:172
  44.5 0.0 collective-permute-done.3.cb_ref
  44.5 0.0 collective-permute-done.2.ca_ref
  44.5 0.0 copy-done.2
  44.5 0.0 copy-done.3
  44.5 8.0 %shard_map.118 = (f32[3072,128]{1,0:T(8,128)}, f32[64,128]{1,0:T(8,128)}) custom-call(f32[3072,128]{1,0:T(8,128)S(1)} %bitcast.8, s32[8,128]{1,0:T(8,128)S(1)} %copy-done.1, f32[8]{0:T(128)S(1)} %copy-done.3, f32[8,48]{1,0:T(8,128)S(1)} %copy-done.2, f32[3,49,8,128]{3,2,1,0:T(8,128)S(1)} %collective-permute-done.ra_ref, ...), custom_call_target="tpu_custom_call" | custom-call | flops 23592960 | bytes 5604896 | tf_op jit(solution)/shard_map/pallas_call | solution.py:36
Async XLA Ops:
  0.6 1.7 %copy-start.4 = (s32[1,1,32,64]{3,2,1,0:T(8,128)S(1)}, s32[1,1,32,64]{3,2,1,0:T(8,128)}, u32[]{:S(2)}) copy-start(s32[1,1,32,64]{3,2,1,0:T(8,128)} %param.14) | copy-start | bytes 24580
  0.6 1.7 %copy-start.8 = (f32[48]{0:T(128)S(1)}, f32[48]{0:T(128)}, u32[]{:S(2)}) copy-start(f32[48]{0:T(128)} %param.13) | copy-start | bytes 580
  0.7 1.7 %copy-start.7 = (s32[48]{0:T(128)S(1)}, s32[48]{0:T(128)}, u32[]{:S(2)}) copy-start(s32[48]{0:T(128)} %param.12) | copy-start | bytes 580
  2.4 11.4 %copy-start = (f32[8,48,8,128]{3,2,1,0:T(8,128)S(1)}, f32[8,48,8,128]{3,2,1,0:T(8,128)}, u32[]{:S(2)}) copy-start(f32[8,48,8,128]{3,2,1,0:T(8,128)} %param.10) | copy-start | bytes 4718596
  2.4 11.4 %copy-start.1 = (s32[8,128]{1,0:T(8,128)S(1)}, s32[8,128]{1,0:T(8,128)}, u32[]{:S(2)}) copy-start(s32[8,128]{1,0:T(8,128)} %mask_ref.5) | copy-start | bytes 12292
  5.2 17.2 %copy-start.5 = (s32[4,8,128]{2,1,0:T(8,128)S(1)}, s32[4,8,128]{2,1,0:T(8,128)}, u32[]{:S(2)}) copy-start(s32[4,8,128]{2,1,0:T(8,128)} %slot_ref.1) | copy-start | bytes 49156
  5.2 17.2 %copy-start.6 = (f32[4,8,128]{2,1,0:T(8,128)S(1)}, f32[4,8,128]{2,1,0:T(8,128)}, u32[]{:S(2)}) copy-start(f32[4,8,128]{2,1,0:T(8,128)} %wt_ref.1) | copy-start | bytes 49156
  5.3 17.2 %all-to-all-start = ((bf16[32,48,128]{2,1,0:T(8,128)(2,1)}), bf16[32,48,128]{2,1,0:T(8,128)(2,1)S(1)}, u32[]{:S(2)}, u32[]{:S(2)}) async-start(bf16[32,48,128]{2,1,0:T(8,128)(2,1)} %shard_map.113), calls=%async_computation | async-start | bytes 786432 | tf_op jit(solution)/shard_map/all_to_all | solution.py:505
  15.5 15.4 %collective-permute-start = (f32[3,49,8,128]{3,2,1,0:T(8,128)}, f32[3,49,8,128]{3,2,1,0:T(8,128)S(1)}, u32[]{:S(2)}, u32[]{:S(2)}) collective-permute-start(f32[3,49,8,128]{3,2,1,0:T(8,128)} %get-tuple-element.14), channel_id=1, source_target_pairs={{0,4},{4,0},{8,12},{12,8},{16,20},{20,16},{24,28},{28,24},{32,36},... | collective-permute-start | bytes 1806344 | tf_op jit(solution)/shard_map/ppermute | solution.py:172
  15.7 15.3 %collective-permute-start.1 = (f32[3,49,8,128]{3,2,1,0:T(8,128)}, f32[3,49,8,128]{3,2,1,0:T(8,128)S(1)}, u32[]{:S(2)}, u32[]{:S(2)}) collective-permute-start(f32[3,49,8,128]{3,2,1,0:T(8,128)} %get-tuple-element.15), channel_id=1, source_target_pairs={{4,8},{8,4},{12,16},{16,12},{20,24},{24,20},{28,32},{32,28},{36,40... | collective-permute-start | bytes 1806344 | tf_op jit(solution)/shard_map/ppermute | solution.py:172
  26.4 10.5 %collective-permute-start.5 = (bf16[3,96,128]{2,1,0:T(8,128)(2,1)S(1)}, bf16[3,96,128]{2,1,0:T(8,128)(2,1)S(1)}, u32[]{:S(2)}, u32[]{:S(2)}) collective-permute-start(bf16[3,96,128]{2,1,0:T(8,128)(2,1)S(1)} %get-tuple-element.21), channel_id=1, source_target_pairs={{4,8},{8,4},{12,16},{16,12},{20,24},{24,20},{28,32},{32,28},{36,40... | collective-permute-start | bytes 221192 | tf_op jit(solution)/shard_map/ppermute | solution.py:172
  30.9 6.0 %collective-permute-start.4 = (bf16[3,96,128]{2,1,0:T(8,128)(2,1)S(1)}, bf16[3,96,128]{2,1,0:T(8,128)(2,1)S(1)}, u32[]{:S(2)}, u32[]{:S(2)}) collective-permute-start(bf16[3,96,128]{2,1,0:T(8,128)(2,1)S(1)} %get-tuple-element.17), channel_id=1, source_target_pairs={{0,4},{4,0},{8,12},{12,8},{16,20},{20,16},{24,28},{28,24},{32,36},... | collective-permute-start | bytes 221192 | tf_op jit(solution)/shard_map/ppermute | solution.py:172
  33.3 11.2 %collective-permute-start.3 = (f32[392,128]{1,0:T(8,128)S(1)}, f32[392,128]{1,0:T(8,128)S(1)}, u32[]{:S(2)}, u32[]{:S(2)}) collective-permute-start(f32[392,128]{1,0:T(8,128)S(1)} %shard_map.116.own_ref), channel_id=1, source_target_pairs={{1,2},{2,1},{5,6},{6,5},{9,10},{10,9},{13,14},{14,13},{17,18},{18,... | collective-permute-start | bytes 602120 | tf_op jit(solution)/shard_map/ppermute | solution.py:172
  36.8 7.7 %collective-permute-start.2 = (f32[392,128]{1,0:T(8,128)S(1)}, f32[392,128]{1,0:T(8,128)S(1)}, u32[]{:S(2)}, u32[]{:S(2)}) collective-permute-start(f32[392,128]{1,0:T(8,128)S(1)} %shard_map.116.own_ref), channel_id=1, source_target_pairs={{0,1},{1,0},{2,3},{3,2},{4,5},{5,4},{6,7},{7,6},{8,9},{9,8},{10,11... | collective-permute-start | bytes 602120 | tf_op jit(solution)/shard_map/ppermute | solution.py:172
  36.9 7.6 %copy-start.2 = (f32[8,48]{1,0:T(8,128)S(1)}, f32[8,48]{1,0:T(8,128)}, u32[]{:S(2)}) copy-start(f32[8,48]{1,0:T(8,128)} %profile_ref.1) | copy-start | bytes 4612
  36.9 7.6 %copy-start.3 = (f32[8]{0:T(128)S(1)}, f32[8]{0:T(128)}, u32[]{:S(2)}) copy-start(f32[8]{0:T(128)} %settle_ref.1) | copy-start | bytes 100
  37.2 5.9 %collective-permute-start.7 = (bf16[96,128]{1,0:T(8,128)(2,1)S(1)}, bf16[96,128]{1,0:T(8,128)(2,1)S(1)}, u32[]{:S(2)}, u32[]{:S(2)}) collective-permute-start(bf16[96,128]{1,0:T(8,128)(2,1)S(1)} %shard_map.117.wown_ref), channel_id=1, source_target_pairs={{1,2},{2,1},{5,6},{6,5},{9,10},{10,9},{13,14},{14,13},{17,18},{18,... | collective-permute-start | bytes 73736 | tf_op jit(solution)/shard_map/ppermute | solution.py:172
  39.6 4.9 %collective-permute-start.6 = (bf16[96,128]{1,0:T(8,128)(2,1)S(1)}, bf16[96,128]{1,0:T(8,128)(2,1)S(1)}, u32[]{:S(2)}, u32[]{:S(2)}) collective-permute-start(bf16[96,128]{1,0:T(8,128)(2,1)S(1)} %shard_map.117.wown_ref), channel_id=1, source_target_pairs={{0,1},{1,0},{2,3},{3,2},{4,5},{5,4},{6,7},{7,6},{8,9},{9,8},{10,11... | collective-permute-start | bytes 73736 | tf_op jit(solution)/shard_map/ppermute | solution.py:172

commit v3 on v2

--- a/solution.py
+++ b/solution.py
@@ -190,7 +190,7 @@
     return jnp.where(at < 3, from_left, jnp.where(at < 7, mine, from_right))
 
 
-def wind_strip_kernel(winds_ref, ra_ref, rb_ref, strip_ref):
+def side_strip_kernel(winds_ref, ra_ref, rb_ref, conc_ref, strip_ref):
     row_odd = lax.axis_index("rows") % 2 == 1
     rows = winds_ref.shape[0]
     chosen = strip_select()
@@ -204,170 +204,231 @@
             line = jnp.where(row_odd == (y < 0), ra_ref[j], rb_ref[j])
         term = jnp.dot(line, chosen[i], preferred_element_type=F32)
         total = term if total is None else total + term
-    strip_ref[...] = total.astype(BF16)
+    before = conc_ref.shape[0]
+    strip_ref[:before] = conc_ref[...]
+    strip_ref[before:] = total.astype(BF16)
 
 
 def conc_edge_kernel(conc_ref, mask_ref, a_ref, b_ref):
     odd = lax.axis_index("rows") % 2 == 1
-    bins = conc_ref.shape[0] // (mask_ref.shape[0] * (a_ref.shape[1] - 1))
-    levels = a_ref.shape[1] - 1
+    bins = a_ref.shape[2] // 2
+    pairs = a_ref.shape[1] - 1
     rows = mask_ref.shape[0]
-
-    def level(k, carry):
+    stride = 2 * pairs * rows
+
+    def pair(p, carry):
         for j in range(HALO):
-            upper = conc_ref[pl.ds(k * rows + j, bins, stride=levels * rows), :]
-            lower = conc_ref[pl.ds(k * rows + rows - HALO + j, bins, stride=levels * rows), :]
-            a_ref[j, k] = jnp.where(odd, upper, lower)
-            b_ref[j, k] = jnp.where(odd, lower, upper)
+            upper, lower = (
+                jnp.concatenate(
+                    [conc_ref[pl.ds((2 * p + h) * rows + y, bins, stride=stride), :] for h in range(2)]
+                )
+                for y in (j, rows - HALO + j)
+            )
+            a_ref[j, p] = jnp.where(odd, upper, lower).astype(BF16)
+            b_ref[j, p] = jnp.where(odd, lower, upper).astype(BF16)
         return carry
 
-    lax.fori_loop(0, levels, level, 0, unroll=4)
+    lax.fori_loop(0, pairs, pair, 0, unroll=4)
     mask = mask_ref[...].astype(F32)
     for j in range(HALO):
-        upper = jnp.broadcast_to(mask[j : j + 1], (bins, LANES))
-        lower = jnp.broadcast_to(mask[rows - HALO + j : rows - HALO + j + 1], (bins, LANES))
-        a_ref[j, levels] = jnp.where(odd, upper, lower)
-        b_ref[j, levels] = jnp.where(odd, lower, upper)
-
-
-def conc_strip_kernel(conc_ref, mask_ref, ra_ref, rb_ref, strip_ref, high_ref, low_ref):
+        upper = jnp.broadcast_to(mask[j : j + 1], (2 * bins, LANES))
+        lower = jnp.broadcast_to(mask[rows - HALO + j : rows - HALO + j + 1], (2 * bins, LANES))
+        a_ref[j, pairs] = jnp.where(odd, upper, lower).astype(BF16)
+        b_ref[j, pairs] = jnp.where(odd, lower, upper).astype(BF16)
+
+
+def conc_strip_kernel(conc_ref, mask_ref, ra_ref, rb_ref, strip_ref, line_ref):
     row_odd = lax.axis_index("rows") % 2 == 1
-    levels = ra_ref.shape[1] - 1
-    bins = ra_ref.shape[2]
+    pairs = ra_ref.shape[1] - 1
+    two = ra_ref.shape[2]
+    bins = two // 2
     rows = mask_ref.shape[0]
+    stride = 2 * pairs * rows
     mask = mask_ref[...].astype(F32)
     chosen = strip_select()
     total = None
     for i in range(STRIP_ROWS):
         y = i - 2
-        for k in range(0, levels + 1, 2):
-            pair = []
-            for level in (k, min(k + 1, levels)):
-                if not 0 <= y < rows:
-                    j = y + HALO if y < 0 else y - rows
-                    pair.append(jnp.where(row_odd == (y < 0), ra_ref[j, level], rb_ref[j, level]))
-                elif level < levels:
-                    pair.append(conc_ref[pl.ds(level * rows + y, bins, stride=levels * rows), :])
-                else:
-                    pair.append(jnp.broadcast_to(mask[y : y + 1], (bins, LANES)))
-            both = jnp.concatenate(pair, axis=0)
-            high = both.astype(BF16)
-            at = slice(k * bins, (k + 2) * bins)
-            high_ref[i % 2, at] = high
-            low_ref[i % 2, at] = (both - high.astype(F32)).astype(BF16)
-        term = jnp.dot(high_ref[i % 2], chosen[i], preferred_element_type=F32) + jnp.dot(
-            low_ref[i % 2], chosen[i], preferred_element_type=F32
-        )
+        for p in range(pairs + 1):
+            if not 0 <= y < rows:
+                j = y + HALO if y < 0 else y - rows
+                both = jnp.where(row_odd == (y < 0), ra_ref[j, p], rb_ref[j, p])
+            elif p < pairs:
+                both = jnp.concatenate(
+                    [conc_ref[pl.ds((2 * p + h) * rows + y, bins, stride=stride), :] for h in range(2)]
+                ).astype(BF16)
+            else:
+                both = jnp.broadcast_to(mask[y : y + 1], (two, LANES)).astype(BF16)
+            line_ref[i % 2, p * two : (p + 1) * two] = both
+        term = jnp.dot(line_ref[i % 2], chosen[i], preferred_element_type=F32)
         total = term if total is None else total + term
-    strip_ref[...] = total[: (levels + 1) * bins]
-
-
-def coefficients(east_w, east, east_e, north_s, north, north_n, valid):
-    face_w = 0.5 * (east_w + east)
-    face_e = 0.5 * (east + east_e)
-    face_s = 0.5 * (north_s + north)
-    face_n = 0.5 * (north + north_n)
-    out_e = jnp.maximum(face_e, 0.0)
-    out_n = jnp.maximum(face_n, 0.0)
-    out_w = jnp.minimum(face_w, 0.0)
-    out_s = jnp.minimum(face_s, 0.0)
-    centre = (1.0 - 4.0 * KAPPA) - (out_e - out_w) - (out_n - out_s)
-    west = KAPPA + jnp.maximum(face_w, 0.0)
-    east_c = KAPPA - jnp.minimum(face_e, 0.0)
-    south = KAPPA + jnp.maximum(face_s, 0.0)
-    north_c = KAPPA - jnp.minimum(face_n, 0.0)
-    result = (centre, west, east_c, south, north_c)
-    return result if valid is None else tuple(jnp.where(valid, c, 0.0) for c in result)
+    strip_ref[...] = total.astype(BF16)
+
+
+def coefficients(face_w, face_e, face_s, face_n):
+    return (
+        (1.0 - 4.0 * KAPPA)
+        - (jnp.maximum(face_e, 0.0) - jnp.minimum(face_w, 0.0))
+        - (jnp.maximum(face_n, 0.0) - jnp.minimum(face_s, 0.0)),
+        KAPPA + jnp.maximum(face_w, 0.0),
+        KAPPA - jnp.minimum(face_e, 0.0),
+        KAPPA + jnp.maximum(face_s, 0.0),
+        KAPPA - jnp.minimum(face_n, 0.0),
+    )
+
+
+def halo_at(y, rows):
+    return y + HALO if y < 0 else y - rows
+
+
+def settle_tile(settle_ref, tile):
+    sublanes = lax.broadcasted_iota(jnp.int32, tile, 0)
+    settle = jnp.zeros(tile, F32)
+    for b in range(tile[0]):
+        settle = jnp.where(sublanes == b, settle_ref[b], settle)
+    return settle
+
+
+def first_step_kernel(
+    conc_ref, settle_ref, ra_ref, rb_ref, winds_ref, wra_ref, wrb_ref,
+    coef_ref, part_ref, deposit_ref, fall_ref,
+):
+    row, last_row = lax.axis_index("rows"), lax.axis_size("rows") - 1
+    row_odd = row % 2 == 1
+    levels = coef_ref.shape[1]
+    bins = ra_ref.shape[2] // 2
+    rows = winds_ref.shape[0]
+    tile = (bins, LANES)
+    stride = levels * rows
+
+    def wind_row(y):
+        if 0 <= y < rows:
+            return winds_ref[y]
+        j = halo_at(y, rows)
+        return jnp.where(row_odd == (y < 0), wra_ref[j].astype(F32), wrb_ref[j].astype(F32))
+
+    lanes = lane_ids((levels, LANES))
+    at_west, at_east = lanes == 0, lanes == LANES - 1
+    for y in range(-2, rows + 2):
+        u = wind_row(y)[:levels]
+        north_s, north, north_n = (wind_row(y + d)[levels:] for d in (-1, 0, 1))
+        face_w = jnp.where(at_west, 0.0, 0.5 * (roll_lanes(u, 1) + u))
+        face_e = jnp.where(at_east, 0.0, 0.5 * (u + roll_lanes(u, -1)))
+        found = coefficients(face_w, face_e, 0.5 * (north_s + north), 0.5 * (north + north_n))
+        if not 0 <= y < rows:
+            valid = row > 0 if y < 0 else row < last_row
+            found = [jnp.where(valid, c, 0.0) for c in found]
+        found = [
+            found[0], jnp.where(at_west, 0.0, found[1]), jnp.where(at_east, 0.0, found[2]), *found[3:]
+        ]
+        for i in range(5):
+            coef_ref[5 * (y + 2) + i] = found[i]
+
+    settle = settle_tile(settle_ref, tile)
+    fall_ref[...] = jnp.zeros(fall_ref.shape, F32)
+    unroll = 8
+
+    def some_levels(trip, carry):
+        ks = [trip * unroll + u for u in range(unroll)]
+
+        def starts_of(y):
+            if 0 <= y < rows:
+                return [conc_ref[pl.ds(k * rows + y, bins, stride=stride), :] for k in ks]
+            j = halo_at(y, rows)
+            result = []
+            for p in range(unroll // 2):
+                at = trip * (unroll // 2) + p
+                both = jnp.where(row_odd == (y < 0), ra_ref[j, at].astype(F32), rb_ref[j, at].astype(F32))
+                result += [both[:bins], both[bins:]]
+            return result
+
+        below, here = starts_of(-3), starts_of(-2)
+        for y in range(-2, rows + 2):
+            above = starts_of(y + 1)
+            fall = fall_ref[y + 2]
+            for u, k in enumerate(ks):
+                c = [coef_ref[5 * (y + 2) + i, pl.ds(k, bins, stride=0), :] for i in range(5)]
+                a = here[u]
+                part_ref[y + 2, pl.ds(k * bins, bins), :] = (
+                    (c[0] - settle) * a
+                    + (c[1] * roll_lanes(a, 1) + c[2] * roll_lanes(a, -1))
+                    + (c[3] * below[u] + c[4] * above[u])
+                    + fall
+                )
+                fall = settle * a
+            fall_ref[y + 2] = fall
+            below, here = here, above
+        return carry
+
+    lax.fori_loop(0, levels // unroll, some_levels, 0)
+    for y in range(rows):
+        deposit_ref[y] = fall_ref[y + 2]
 
 
 def transport_kernel(
-    conc_ref, mask_ref, settle_ref, profile_ref,
-    ra_ref, rb_ref, own_ref, ca_ref, cb_ref,
-    winds_ref, wra_ref, wrb_ref, wown_ref, wca_ref, wcb_ref,
+    part_ref, coef_ref, fallen_ref, mask_ref, settle_ref, profile_ref,
+    ra_ref, rb_ref, own_ref, xa_ref, xb_ref,
     out_ref, deposit_ref,
-    coef_ref, strip_coef_ref, edge_ref, bound_ref, source_ref, fall_ref,
+    centre_ref, strip_coef_ref, bound_ref, source_ref, fall_ref,
 ):
     row, col = lax.axis_index("rows"), lax.axis_index("cols")
     last_row, last_col = lax.axis_size("rows") - 1, lax.axis_size("cols") - 1
     row_odd, col_odd = row % 2 == 1, col % 2 == 1
-    levels = ra_ref.shape[1] - 1
-    bins = ra_ref.shape[2]
+    levels = coef_ref.shape[1]
+    two = ra_ref.shape[2]
+    bins = two // 2
     rows = mask_ref.shape[0]
     tile = (bins, LANES)
     stride = levels * rows
 
-    def halo_of(y, get_a, get_b):
-        return jnp.where(row_odd == (y < 0), get_a, get_b)
-
-    def halo_at(y):
-        return y + HALO if y < 0 else y - rows
-
-    def wind_row(y):
-        if 0 <= y < rows:
-            return winds_ref[y]
-        j = halo_at(y)
-        return halo_of(y, wra_ref[j].astype(F32), wrb_ref[j].astype(F32))
+    def strip_at(start, size):
+        at = pl.ds(start, size)
+        return whole_strip(
+            own_ref[at, :].astype(F32), xa_ref[at, :].astype(F32), xb_ref[at, :].astype(F32),
+            lane_ids((size, LANES)) % STRIP, col_odd,
+        )
 
     lanes = lane_ids((levels, LANES))
     at = lanes % STRIP
-    wide = lane_ids((2 * levels, LANES)) % STRIP
-    strip = whole_strip(
-        wown_ref[...].astype(F32), wca_ref[...].astype(F32), wcb_ref[...].astype(F32), wide, col_odd
-    )
-    strip_u, strip_v = strip[:levels], strip[levels:]
+    winds_at = (levels + 2) * bins
+    strip_u, strip_v = strip_at(winds_at, levels), strip_at(winds_at + levels, levels)
     inside = (
         ((at >= 3) | (col > 0))
         & ((at < 7) | (col < last_col))
         & ((lanes >= 2 * STRIP) | (row > 0))
         & ((lanes < (2 + rows) * STRIP) | (row < last_row))
     )
+    face_w = 0.5 * (roll_lanes(strip_u, 1) + strip_u)
+    face_e = 0.5 * (strip_u + roll_lanes(strip_u, -1))
     found = coefficients(
-        roll_lanes(strip_u, 1), strip_u, roll_lanes(strip_u, -1),
-        roll_lanes(strip_v, STRIP), strip_v, roll_lanes(strip_v, -STRIP),
-        inside,
+        face_w, face_e,
+        0.5 * (roll_lanes(strip_v, STRIP) + strip_v),
+        0.5 * (strip_v + roll_lanes(strip_v, -STRIP)),
     )
     for i in range(5):
-        strip_coef_ref[i] = found[i]
-    for y in range(-2, rows + 2):
-        u = wind_row(y)[:levels]
+        strip_coef_ref[i] = jnp.where(inside, found[i], 0.0)
+    sides = jnp.where(at == 3, jnp.minimum(face_w, 0.0), jnp.where(at == 6, -jnp.maximum(face_e, 0.0), 0.0))
+    sides = jnp.where(inside, sides, 0.0)
+    strip_coef_ref[5] = sides
+    for y in range(-1, rows + 1):
         base = STRIP * (y + 2)
-        u_w = jnp.where(lanes == 0, roll_lanes(strip_u, -(base + 2)), roll_lanes(u, 1))
-        u_e = jnp.where(
-            lanes == LANES - 1, roll_lanes(strip_u, LANES - 1 - (base + 7)), roll_lanes(u, -1)
-        )
-        valid = None
-        if y < 0:
-            valid = row > 0
-        elif y >= rows:
-            valid = row < last_row
-        centre, west, east, south, north = coefficients(
-            u_w, u, u_e,
-            wind_row(y - 1)[levels:], wind_row(y)[levels:], wind_row(y + 1)[levels:],
-            valid,
-        )
-        west = jnp.where(lanes == 0, 0.0, west)
-        east = jnp.where(lanes == LANES - 1, 0.0, east)
-        for i, c in enumerate((centre, west, east, south, north)):
-            coef_ref[5 * (y + 2) + i] = c
-
-    sublanes = lax.broadcasted_iota(jnp.int32, tile, 0)
-    settle = jnp.zeros(tile, F32)
-    for b in range(bins):
-        settle = jnp.where(sublanes == b, settle_ref[b], settle)
+        west = roll_lanes(sides, -(base + 3))
+        east = roll_lanes(sides, LANES - 1 - (base + 6))
+        more = jnp.where(lanes == 0, west, jnp.where(lanes == LANES - 1, east, 0.0))
+        centre_ref[y + 1] = coef_ref[5 * (y + 2)] + more
+
+    settle = settle_tile(settle_ref, tile)
 
     tile_lanes = lane_ids(tile)
     tile_at = tile_lanes % STRIP
     spare = STRIP * STRIP_ROWS
-
-    def edge_of(k):
-        at_k = pl.ds(k * bins, bins)
-        return whole_strip(own_ref[at_k, :], ca_ref[at_k, :], cb_ref[at_k, :], tile_at, col_odd)
-
-    mask_strip = edge_of(levels)
-    zero = jnp.zeros(tile, F32)
-    fall_before = [zero] * (STEPS - 1)
+    mask_strip = strip_at(levels * bins, two)[:bins]
+    fall_before = [jnp.zeros(tile, F32)] * (STEPS - 1)
+    edges = None
     for k in range(levels):
-        edge = edge_of(k)
+        if k % 2 == 0:
+            edges = strip_at(k * bins, two)
+        edge = edges[:bins] if k % 2 == 0 else edges[bins:]
         prof = jnp.broadcast_to(profile_ref[:, k : k + 1], tile)
         parts = []
         rest = prof
@@ -376,11 +437,13 @@
             rest = rest - part
             parts.append(part)
         emitted = prof * mask_strip
-        c = [jnp.broadcast_to(strip_coef_ref[i, k : k + 1, :], tile) for i in range(5)]
+        c = [jnp.broadcast_to(strip_coef_ref[i, k : k + 1, :], tile) for i in range(6)]
         for step in range(STEPS):
             from_w = c[1] * roll_lanes(edge, 1)
             from_e = c[2] * roll_lanes(edge, -1)
             flow = jnp.where(tile_at == 3, from_w, jnp.where(tile_at == 6, from_e, 0.0))
+            if step == 0:
+                flow = flow + c[5] * edge
             for i, part in enumerate(parts):
                 flow = jnp.where(tile_lanes == spare + i, part, flow)
             flow = jnp.where(tile_lanes >= spare + 3, 0.0, flow)
@@ -398,6 +461,7 @@
     lane_of = lax.broadcasted_iota(jnp.int32, (LANES, LANES), 0)
     x_of = lane_ids((LANES, LANES))
     mask = mask_ref[...].astype(F32)
+    last_pair = ra_ref.shape[1] - 1
     spread = []
     for y in range(-2, rows + 2):
         base = STRIP * (y + 2)
@@ -405,8 +469,10 @@
         if 0 <= y < rows:
             line = mask[y : y + 1]
         else:
-            j = halo_at(y)
-            line = halo_of(y, ra_ref[j, levels], rb_ref[j, levels])[:1]
+            j = halo_at(y, rows)
+            line = jnp.where(
+                row_odd == (y < 0), ra_ref[j, last_pair].astype(F32), rb_ref[j, last_pair].astype(F32)
+            )[:1]
         emits = (lane_of >= spare) & (lane_of < spare + 3)
         table = jnp.where(hit, 1.0, jnp.where(emits, line, 0.0)).astype(BF16)
         spread.append(jnp.concatenate([table, table], axis=0))
@@ -428,21 +494,12 @@
 
     fall_ref[...] = jnp.zeros(fall_ref.shape, F32)
     unroll = 8
+    skipped = slots[1, -1]
 
     def some_levels(trip, carry):
         ks = [trip * unroll + u for u in range(unroll)]
-
-        def start_of(y, k):
-            if 0 <= y < rows:
-                return conc_ref[pl.ds(k * rows + y, bins, stride=stride), :]
-            j = halo_at(y)
-            return halo_of(y, ra_ref[j, k], rb_ref[j, k])
-
         coefs = [{} for _ in ks]
         states = [[{} for _ in range(STEPS + 1)] for _ in ks]
-        for u, k in enumerate(ks):
-            for y in (-3, -2):
-                states[u][0][y] = start_of(y, k)
         for front in range(-2, rows + 4):
             for step in range(STEPS):
                 y = front - step
@@ -450,15 +507,18 @@
                 if not -reach <= y < rows + reach:
                     continue
                 index = slots[step, y]
-                fall = fall_ref[index]
+                if step == 0:
+                    for u, k in enumerate(ks):
+                        at_k = pl.ds(k * bins, bins)
+                        states[u][1][y] = part_ref[y + 2, at_k, :] + source_ref[index, at_k, :]
+                    continue
+                fall = fall_ref[index - skipped]
                 for u, k in enumerate(ks):
+                    if step == 1:
+                        coefs[u][y] = [centre_ref[y + 1, pl.ds(k, bins, stride=0), :] - settle] + [
+                            coef_ref[5 * (y + 2) + i, pl.ds(k, bins, stride=0), :] for i in range(1, 5)
+                        ]
                     state = states[u][step]
-                    if step == 0:
-                        state[y + 1] = start_of(y + 1, k)
-                        coefs[u][y] = [
-                            coef_ref[5 * (y + 2) + i, pl.ds(k, bins, stride=0), :] for i in range(5)
-                        ]
-                        coefs[u][y][0] = coefs[u][y][0] - settle
                     c = coefs[u][y]
                     a = state[y]
                     source = source_ref[index, pl.ds(k * bins, bins), :] + fall
@@ -473,13 +533,13 @@
                         states[u][step + 1][y] = fresh
                     else:
                         out_ref[pl.ds(k * rows + y, bins, stride=stride), :] = fresh
-                fall_ref[index] = fall
+                fall_ref[index - skipped] = fall
         return carry
 
     lax.fori_loop(0, levels // unroll, some_levels, 0)
     for y in range(rows):
         deposit_ref[pl.ds(y, bins, stride=rows), :] = (
-            fall_ref[slots[0, y]] + fall_ref[slots[1, y]] + fall_ref[slots[2, y]]
+            fallen_ref[y] + fall_ref[slots[1, y] - skipped] + fall_ref[slots[2, y] - skipped]
         )
 
 
@@ -504,7 +564,8 @@
     flat, sent = lax.optimization_barrier((flat, sent))
     received = lax.all_to_all(sent, "rows", split_axis=0, concat_axis=0, tiled=True)
 
-    edge_rows = shape((HALO, levels + 1, bins, cols), F32)
+    pairs = levels // 2 + 1
+    edge_rows = shape((HALO, pairs, 2 * bins, cols), BF16)
     ca, cb = call(conc_edge_kernel, (edge_rows, edge_rows), (flat, source_mask), moved=0)
     ra, rb = swap(ca, "rows", True), swap(cb, "rows", False)
 
@@ -520,37 +581,49 @@
     wra, wrb = swap(wa, "rows", True), swap(wb, "rows", False)
 
     ra, rb, wa = lax.optimization_barrier((ra, rb, wa))
-    strips = shape(((levels + 1) * bins, LANES), F32)
-    padded = (levels + 2) * bins
+    strips = shape((pairs * 2 * bins, LANES), BF16)
+    conc_strip = call(
+        conc_strip_kernel, strips, (flat, source_mask, ra, rb),
+        scratch=(pltpu.VMEM((2, pairs * 2 * bins, LANES), BF16),),
+        moved=0,
+    )
     own = call(
-        conc_strip_kernel, strips, (flat, source_mask, ra, rb),
-        scratch=(pltpu.VMEM((2, padded, LANES), BF16), pltpu.VMEM((2, padded, LANES), BF16)),
+        side_strip_kernel,
+        shape((pairs * 2 * bins + 2 * levels, LANES), BF16),
+        (winds, wra, wrb, conc_strip),
+        flops=HIDES,
+    )
+    xa, xb = swap(own, "cols", True), swap(own, "cols", False)
+
+    tile = (bins, LANES)
+    part, coef, fallen = (
+        shape((rows + 4, levels * bins, LANES), F32),
+        shape((5 * (rows + 4), levels, LANES), F32),
+        shape((rows,) + tile, F32),
+    )
+    coef, part, fallen = call(
+        first_step_kernel,
+        (coef, part, fallen),
+        (flat, settle, ra, rb, winds, wra, wrb),
+        scratch=(pltpu.VMEM((rows + 4,) + tile, F32),),
+        smem=(1,),
         moved=0,
     )
-    xa, xb = swap(own, "cols", True), swap(own, "cols", False)
-    wown = call(
-        wind_strip_kernel, shape((2 * levels, LANES), BF16), (winds, wra, wrb), flops=HIDES
-    )
-    wxa, wxb = swap(wown, "cols", True), swap(wown, "cols", False)
-
-    tile = (bins, LANES)
     updates = sum(rows + 2 * (STEPS - 1 - s) for s in range(STEPS))
     final, deposit = call(
         transport_kernel,
         (shape(flat.shape, F32), shape((bins * rows, cols), F32)),
-        (flat, source_mask, settle, profile, ra, rb, own, xa, xb,
-         winds, wra, wrb, wown, wxa, wxb),
+        (part, coef, fallen, source_mask, settle, profile, ra, rb, own, xa, xb),
         scratch=(
-            pltpu.VMEM((5 * (rows + 4), levels, LANES), F32),
-            pltpu.VMEM((5, levels, LANES), F32),
-            pltpu.VMEM(tile, F32),
+            pltpu.VMEM((rows + 2, levels, LANES), F32),
+            pltpu.VMEM((6, levels, LANES), F32),
             pltpu.VMEM((STEPS, levels * bins, LANES), F32),
             pltpu.VMEM((updates, levels * bins, LANES), F32),
-            pltpu.VMEM((updates,) + tile, F32),
+            pltpu.VMEM((updates - rows - 4,) + tile, F32),
         ),
-        smem=(2,),
+        smem=(4,),
         flops=16 * updates * levels * bins * LANES,
-        limit=32,
+        limit=24,
     )
     return final.reshape(conc.shape), deposit.reshape(bins, rows, cols)
 

time: 52.9 us -> 50.2 us (0.949)
  starting transfers between devices: 24 us -> 20.9 us
  waiting for transfers between devices: 6.83 us -> 7.77 us
    ppermute x8 -> x6, starting transfers between devices: 15.5 us -> 12.4 us  [swap(): return lax.ppermute(array, axis, pairs)]
    all_to_all x1, waiting for transfers between devices: 2.25 us -> 3.79 us  [per_device(): lax.all_to_all(sent, 'rows', split_axis=0, concat_axis=0, tiled=True)]
    ppermute x8 -> x6, waiting for transfers between devices: 4.57 us -> 3.98 us  [swap(): return lax.ppermute(array, axis, pairs)]
    pallas_call x6 -> x7, Pallas kernels: 19.1 us -> 18.7 us  [call(): pl.pallas_call(kernel, out_shape=out_shape, in_specs=[pl.BlockSpec(memory...]
  transfers between devices with their start and end apart: 9 -> 7, of which waited for: 3 -> 4; matrix products, arithmetic and copies ran while one was open for 0% -> 0% of each run, Pallas kernels for 16% -> 19%
where the time goes in v3:
time: 50.2 us; the launch traced here: 49.9 us
  starting transfers between devices  20.9 us (42%)
  Pallas kernels  18.7 us (37%)
  waiting for transfers between devices  7.77 us (15%)
  local copies, waits for them, and re-layouts  1.73 us (3%)
  between operations  0.86 us (2%)
    pallas_call x7, Pallas kernels, call(): pl.pallas_call(kernel, out_shape=out_shape, in_specs=[pl.BlockSpec(memory...  18.7 us
    ppermute x6, starting transfers between devices, swap(): return lax.ppermute(array, axis, pairs)  12.4 us
    all_to_all x1, starting transfers between devices, per_device(): lax.all_to_all(sent, 'rows', split_axis=0, concat_axis=0, tiled=True)  8.47 us
    ppermute x6, waiting for transfers between devices, swap(): return lax.ppermute(array, axis, pairs)  3.98 us
    all_to_all x1, waiting for transfers between devices, per_device(): lax.all_to_all(sent, 'rows', split_axis=0, concat_axis=0, tiled=True)  3.79 us
    unnamed x19, local copies, waits for them, and re-layouts  1.73 us
  transfers between devices with their start and end apart: 7, of which 4 were waited for; matrix products, arithmetic and copies ran while one was open for 0% of the time, Pallas kernels for 19%

profile of v3, /device:TPU:10, one launch (start us, length us, event | category | flops | bytes accessed | tf_op | source)
XLA Modules:
  0.0 49.9 jit_solution(14071303384845829627)
XLA Ops:
  0.6 0.0 copy-start.4
  0.6 0.0 copy-start.8
  0.7 0.0 copy-start.7
  0.7 1.7 %copy.12.nwp_ref = bf16[2,137,2048]{2,1,0:T(8,128)(2,1)S(1)} copy(bf16[2,137,2048]{2,0,1:T(2,128)(2,1)} %param.11) | data formatting | bytes 2244608 | tf_op args[1]
  2.3 0.0 copy-done.4
  2.4 0.0 copy-done.8
  2.4 0.0 copy-done.7
  2.4 0.0 copy-start
  2.4 0.0 copy-start.1
  2.4 2.8 %shard_map.113 = bf16[32,48,128]{2,1,0:T(8,128)(2,1)} custom-call(s32[1,48]{1,0:T(1,128)S(1)} %bitcast.10, f32[1,48]{1,0:T(1,128)S(1)} %bitcast.11, s32[32,64]{1,0:T(8,128)S(1)} %bitcast.9, bf16[2,137,2048]{2,1,0:T(8,128)(2,1)S(1)} %copy.12.nwp_ref), custom_call_target="tpu_custom_call" | custom-call | flops 805306368 | bytes 1524096 | tf_op jit(solution)/shard_map/pallas_call | solution.py:36
  5.2 0.0 copy-start.5
  5.2 0.0 copy-start.6
  5.3 8.5 %all-to-all-start = ((bf16[32,48,128]{2,1,0:T(8,128)(2,1)}), bf16[32,48,128]{2,1,0:T(8,128)(2,1)S(1)}, u32[]{:S(2)}, u32[]{:S(2)}) async-start(bf16[32,48,128]{2,1,0:T(8,128)(2,1)} %shard_map.113), calls=%async_computation | async-start | bytes 786432 | tf_op jit(solution)/shard_map/all_to_all | solution.py:565
  13.7 0.0 copy-done
  13.8 0.0 copy-done.1
  13.8 0.7 %shard_map.114 = (bf16[3,25,16,128]{3,2,1,0:T(8,128)(2,1)S(1)}, bf16[3,25,16,128]{3,2,1,0:T(8,128)(2,1)S(1)}) custom-call(f32[3072,128]{1,0:T(8,128)S(1)} %bitcast.6, s32[8,128]{1,0:T(8,128)S(1)} %copy-done.1), custom_call_target="tpu_custom_call" | custom-call | tf_op jit(solution)/shard_map/pallas_call | solution.py:36
  14.5 0.2 collective-permute-start
  14.7 4.5 %collective-permute-start.1 = (bf16[3,25,16,128]{3,2,1,0:T(8,128)(2,1)S(1)}, bf16[3,25,16,128]{3,2,1,0:T(8,128)(2,1)S(1)}, u32[]{:S(2)}, u32[]{:S(2)}) collective-permute-start(bf16[3,25,16,128]{3,2,1,0:T(8,128)(2,1)S(1)} %get-tuple-element.18), channel_id=1, source_target_pairs={{4,8},{8,4},{12,16},{16,12},{20,24},{24,20},{28,32},{32,28},{36,40... | collective-permute-start | bytes 921608 | tf_op jit(solution)/shard_map/ppermute | solution.py:172
  19.2 3.8 %all-to-all-done.recv_ref = bf16[32,48,128]{2,1,0:T(8,128)(2,1)S(1)} async-done(((bf16[32,48,128]{2,1,0:T(8,128)(2,1)}), bf16[32,48,128]{2,1,0:T(8,128)(2,1)S(1)}, u32[]{:S(2)}, u32[]{:S(2)}) %all-to-all-start) | async-done | bytes 393248 | tf_op jit(solution)/shard_map/all_to_all | solution.py:565
  23.0 0.0 copy-done.5
  23.0 0.0 copy-done.6
  23.0 4.0 %shard_map.115 = (f32[8,96,128]{2,1,0:T(8,128)S(1)}, bf16[3,96,128]{2,1,0:T(8,128)(2,1)S(1)}, bf16[3,96,128]{2,1,0:T(8,128)(2,1)S(1)}) custom-call(bf16[32,48,128]{2,1,0:T(8,128)(2,1)S(1)} %all-to-all-done.recv_ref, s32[4,8,128]{2,1,0:T(8,128)S(1)} %copy-done.5, f32[4,8,128]{2,1,0:T(8,128)S(1)} %copy-done.6), custom_call_target="tpu_custom_call" | custom-call | flops 49999998976 | bytes 966656 | tf_op jit(solution)/shard_map/pallas_call | solution.py:36
  27.0 4.0 %collective-permute-start.3 = (bf16[3,96,128]{2,1,0:T(8,128)(2,1)S(1)}, bf16[3,96,128]{2,1,0:T(8,128)(2,1)S(1)}, u32[]{:S(2)}, u32[]{:S(2)}) collective-permute-start(bf16[3,96,128]{2,1,0:T(8,128)(2,1)S(1)} %get-tuple-element.24), channel_id=1, source_target_pairs={{4,8},{8,4},{12,16},{16,12},{20,24},{24,20},{28,32},{32,28},{36,40... | collective-permute-start | bytes 221192 | tf_op jit(solution)/shard_map/ppermute | solution.py:172
  30.9 0.1 collective-permute-start.2
  31.0 0.0 collective-permute-done.ra_ref
  31.1 0.0 collective-permute-done.1.rb_ref
  31.1 1.7 %shard_map.117.conc_ref = bf16[400,128]{1,0:T(8,128)(2,1)S(1)} custom-call(f32[3072,128]{1,0:T(8,128)S(1)} %bitcast.7, s32[8,128]{1,0:T(8,128)S(1)} %copy-done.1, bf16[3,25,16,128]{3,2,1,0:T(8,128)(2,1)S(1)} %collective-permute-done.ra_ref, bf16[3,25,16,128]{3,2,1,0:T(8,128)(2,1)S(1)} %collective-permute-done.1.rb_ref), custom_call_target="tpu_custom_call" | custom-call | tf_op jit(solution)/shard_map/pallas_call | solution.py:36
  32.8 2.0 %collective-permute-done.3.wrb_ref.rb_ref = bf16[3,96,128]{2,1,0:T(8,128)(2,1)S(1)} collective-permute-done((bf16[3,96,128]{2,1,0:T(8,128)(2,1)S(1)}, bf16[3,96,128]{2,1,0:T(8,128)(2,1)S(1)}, u32[]{:S(2)}, u32[]{:S(2)}) %collective-permute-start.3) | collective-permute-done | bytes 73760 | tf_op jit(solution)/shard_map/ppermute | solution.py:172
  34.8 0.0 collective-permute-done.2.wra_ref.ra_ref
  34.8 0.0 copy-start.3
  34.8 0.3 shard_map.118.own_ref
  35.0 0.0 copy-start.2
  35.0 3.5 %collective-permute-start.5 = (bf16[496,128]{1,0:T(8,128)(2,1)S(1)}, bf16[496,128]{1,0:T(8,128)(2,1)S(1)}, u32[]{:S(2)}, u32[]{:S(2)}) collective-permute-start(bf16[496,128]{1,0:T(8,128)(2,1)S(1)} %shard_map.118.own_ref), channel_id=1, source_target_pairs={{1,2},{2,1},{5,6},{6,5},{9,10},{10,9},{13,14},{14,13},{17,18},{18,... | collective-permute-start | bytes 380936 | tf_op jit(solution)/shard_map/ppermute | solution.py:172
  38.5 0.1 collective-permute-start.4
  38.6 0.0 copy-done.3
  38.6 2.9 %shard_map.116 = (f32[60,48,128]{2,1,0:T(8,128)S(1)}, f32[12,384,128]{2,1,0:T(8,128)S(1)}, f32[8,8,128]{2,1,0:T(8,128)S(1)}) custom-call(f32[3072,128]{1,0:T(8,128)S(1)} %bitcast.8, f32[8]{0:T(128)S(1)} %copy-done.3, bf16[3,25,16,128]{3,2,1,0:T(8,128)(2,1)S(1)} %collective-permute-done.ra_ref, bf16[3,25,16,128]{3,2,1,0:T(8,128)(2,1)S(1)} %collective-permute-done.1.rb_ref, ...), custom_call_target="tpu_custom_call" | custom-call | tf_op jit(solution)/shard_map/pallas_call | solution.py:36
  41.6 0.3 collective-permute-done.5.xb_ref
  41.9 1.7 %collective-permute-done.4.xa_ref = bf16[496,128]{1,0:T(8,128)(2,1)S(1)} collective-permute-done((bf16[496,128]{1,0:T(8,128)(2,1)S(1)}, bf16[496,128]{1,0:T(8,128)(2,1)S(1)}, u32[]{:S(2)}, u32[]{:S(2)}) %collective-permute-start.4) | collective-permute-done | bytes 127008 | tf_op jit(solution)/shard_map/ppermute | solution.py:172
  43.5 0.0 copy-done.2
  43.5 6.4 %shard_map.119 = (f32[3072,128]{1,0:T(8,128)}, f32[64,128]{1,0:T(8,128)}) custom-call(f32[12,384,128]{2,1,0:T(8,128)S(1)} %get-tuple-element.25.part_ref, f32[60,48,128]{2,1,0:T(8,128)S(1)} %get-tuple-element.26.coef_ref, f32[8,8,128]{2,1,0:T(8,128)S(1)} %get-tuple-element.27.fallen_ref, s32[8,128]{1,0:T(8,128)S(1)} %copy-done.1, f32[8]{0:T(128)S(1)} %copy-done.3, ...), custom_call_target="tpu_custom_call" | custom-call | flops 23592960 | bytes 6473248 | tf_op jit(solution)/shard_map/pallas_call | solution.py:36
Async XLA Ops:
  0.6 1.7 %copy-start.4 = (s32[1,1,32,64]{3,2,1,0:T(8,128)S(1)}, s32[1,1,32,64]{3,2,1,0:T(8,128)}, u32[]{:S(2)}) copy-start(s32[1,1,32,64]{3,2,1,0:T(8,128)} %param.14) | copy-start | bytes 24580
  0.6 1.7 %copy-start.8 = (f32[48]{0:T(128)S(1)}, f32[48]{0:T(128)}, u32[]{:S(2)}) copy-start(f32[48]{0:T(128)} %param.13) | copy-start | bytes 580
  0.7 1.7 %copy-start.7 = (s32[48]{0:T(128)S(1)}, s32[48]{0:T(128)}, u32[]{:S(2)}) copy-start(s32[48]{0:T(128)} %param.12) | copy-start | bytes 580
  2.4 11.4 %copy-start = (f32[8,48,8,128]{3,2,1,0:T(8,128)S(1)}, f32[8,48,8,128]{3,2,1,0:T(8,128)}, u32[]{:S(2)}) copy-start(f32[8,48,8,128]{3,2,1,0:T(8,128)} %param.10) | copy-start | bytes 4718596
  2.4 11.4 %copy-start.1 = (s32[8,128]{1,0:T(8,128)S(1)}, s32[8,128]{1,0:T(8,128)}, u32[]{:S(2)}) copy-start(s32[8,128]{1,0:T(8,128)} %mask_ref.5) | copy-start | bytes 12292
  5.2 17.8 %copy-start.5 = (s32[4,8,128]{2,1,0:T(8,128)S(1)}, s32[4,8,128]{2,1,0:T(8,128)}, u32[]{:S(2)}) copy-start(s32[4,8,128]{2,1,0:T(8,128)} %slot_ref.1) | copy-start | bytes 49156
  5.2 17.8 %copy-start.6 = (f32[4,8,128]{2,1,0:T(8,128)S(1)}, f32[4,8,128]{2,1,0:T(8,128)}, u32[]{:S(2)}) copy-start(f32[4,8,128]{2,1,0:T(8,128)} %wt_ref.1) | copy-start | bytes 49156
  5.3 17.8 %all-to-all-start = ((bf16[32,48,128]{2,1,0:T(8,128)(2,1)}), bf16[32,48,128]{2,1,0:T(8,128)(2,1)S(1)}, u32[]{:S(2)}, u32[]{:S(2)}) async-start(bf16[32,48,128]{2,1,0:T(8,128)(2,1)} %shard_map.113), calls=%async_computation | async-start | bytes 786432 | tf_op jit(solution)/shard_map/all_to_all | solution.py:565
  14.5 16.6 %collective-permute-start = (bf16[3,25,16,128]{3,2,1,0:T(8,128)(2,1)S(1)}, bf16[3,25,16,128]{3,2,1,0:T(8,128)(2,1)S(1)}, u32[]{:S(2)}, u32[]{:S(2)}) collective-permute-start(bf16[3,25,16,128]{3,2,1,0:T(8,128)(2,1)S(1)} %get-tuple-element.17), channel_id=1, source_target_pairs={{0,4},{4,0},{8,12},{12,8},{16,20},{20,16},{24,28},{28,24},{32,36},... | collective-permute-start | bytes 921608 | tf_op jit(solution)/shard_map/ppermute | solution.py:172
  14.7 16.4 %collective-permute-start.1 = (bf16[3,25,16,128]{3,2,1,0:T(8,128)(2,1)S(1)}, bf16[3,25,16,128]{3,2,1,0:T(8,128)(2,1)S(1)}, u32[]{:S(2)}, u32[]{:S(2)}) collective-permute-start(bf16[3,25,16,128]{3,2,1,0:T(8,128)(2,1)S(1)} %get-tuple-element.18), channel_id=1, source_target_pairs={{4,8},{8,4},{12,16},{16,12},{20,24},{24,20},{28,32},{32,28},{36,40... | collective-permute-start | bytes 921608 | tf_op jit(solution)/shard_map/ppermute | solution.py:172
  27.0 7.8 %collective-permute-start.3 = (bf16[3,96,128]{2,1,0:T(8,128)(2,1)S(1)}, bf16[3,96,128]{2,1,0:T(8,128)(2,1)S(1)}, u32[]{:S(2)}, u32[]{:S(2)}) collective-permute-start(bf16[3,96,128]{2,1,0:T(8,128)(2,1)S(1)} %get-tuple-element.24), channel_id=1, source_target_pairs={{4,8},{8,4},{12,16},{16,12},{20,24},{24,20},{28,32},{32,28},{36,40... | collective-permute-start | bytes 221192 | tf_op jit(solution)/shard_map/ppermute | solution.py:172
  30.9 3.8 %collective-permute-start.2 = (bf16[3,96,128]{2,1,0:T(8,128)(2,1)S(1)}, bf16[3,96,128]{2,1,0:T(8,128)(2,1)S(1)}, u32[]{:S(2)}, u32[]{:S(2)}) collective-permute-start(bf16[3,96,128]{2,1,0:T(8,128)(2,1)S(1)} %get-tuple-element.20), channel_id=1, source_target_pairs={{0,4},{4,0},{8,12},{12,8},{16,20},{20,16},{24,28},{28,24},{32,36},... | collective-permute-start | bytes 221192 | tf_op jit(solution)/shard_map/ppermute | solution.py:172
  34.8 3.9 %copy-start.3 = (f32[8]{0:T(128)S(1)}, f32[8]{0:T(128)}, u32[]{:S(2)}) copy-start(f32[8]{0:T(128)} %settle_ref.3) | copy-start | bytes 100
  35.0 8.5 %copy-start.2 = (f32[8,48]{1,0:T(8,128)S(1)}, f32[8,48]{1,0:T(8,128)}, u32[]{:S(2)}) copy-start(f32[8,48]{1,0:T(8,128)} %profile_ref.1) | copy-start | bytes 4612
  35.0 6.8 %collective-permute-start.5 = (bf16[496,128]{1,0:T(8,128)(2,1)S(1)}, bf16[496,128]{1,0:T(8,128)(2,1)S(1)}, u32[]{:S(2)}, u32[]{:S(2)}) collective-permute-start(bf16[496,128]{1,0:T(8,128)(2,1)S(1)} %shard_map.118.own_ref), channel_id=1, source_target_pairs={{1,2},{2,1},{5,6},{6,5},{9,10},{10,9},{13,14},{14,13},{17,18},{18,... | collective-permute-start | bytes 380936 | tf_op jit(solution)/shard_map/ppermute | solution.py:172
  38.5 5.0 %collective-permute-start.4 = (bf16[496,128]{1,0:T(8,128)(2,1)S(1)}, bf16[496,128]{1,0:T(8,128)(2,1)S(1)}, u32[]{:S(2)}, u32[]{:S(2)}) collective-permute-start(bf16[496,128]{1,0:T(8,128)(2,1)S(1)} %shard_map.118.own_ref), channel_id=1, source_target_pairs={{0,1},{1,0},{2,3},{3,2},{4,5},{5,4},{6,7},{7,6},{8,9},{9,8},{10,11... | collective-permute-start | bytes 380936 | tf_op jit(solution)/shard_map/ppermute | solution.py:172

commit v4 on v3

--- a/solution.py
+++ b/solution.py
@@ -28,11 +28,13 @@
     return pltpu.roll(x, shift % LANES, x.ndim - 1)
 
 
-def call(kernel, out_shape, args, scratch=(), flops=0, smem=(), limit=16, moved=None, out_space=pltpu.VMEM):
+def call(kernel, out_shape, args, scratch=(), flops=0, smem=(), limit=16, moved=None, out_spaces=None):
     if moved is None:
         moved = sum(a.size * a.dtype.itemsize for a in args) + sum(
             s.size * s.dtype.itemsize for s in jax.tree.leaves(out_shape)
         )
+    leaves, tree = jax.tree.flatten(out_shape)
+    spaces = out_spaces or (pltpu.VMEM,) * len(leaves)
     return pl.pallas_call(
         kernel,
         out_shape=out_shape,
@@ -40,11 +42,21 @@
             pl.BlockSpec(memory_space=pltpu.SMEM if i in smem else pltpu.VMEM)
             for i in range(len(args))
         ],
-        out_specs=jax.tree.map(lambda _: pl.BlockSpec(memory_space=out_space), out_shape),
+        out_specs=jax.tree.unflatten(tree, [pl.BlockSpec(memory_space=m) for m in spaces]),
         scratch_shapes=list(scratch),
         compiler_params=pltpu.CompilerParams(vmem_limit_bytes=limit * MIB),
         cost_estimate=pl.CostEstimate(flops=flops, bytes_accessed=moved, transcendentals=0),
     )(*args)
+
+
+def one_hot(wanted, count):
+    width = wanted.shape[1]
+    group = wanted // SPLIT
+    place = lax.broadcasted_iota(jnp.int32, (SPLIT, width), 0)
+    unit = jnp.where(place == wanted - group * SPLIT, 1.0, 0.0).astype(BF16)
+    none = jnp.zeros((SPLIT, width), BF16)
+    group = jnp.broadcast_to(group.astype(F32), (SPLIT, width)).astype(BF16)
+    return jnp.concatenate([jnp.where(group == g, unit, none) for g in range(count // SPLIT)], axis=0)
 
 
 def select_kernel(lev_ref, frac_ref, pick_ref, nwp_ref, sent_ref, out_ref, sem):
@@ -58,28 +70,21 @@
         part = weight.astype(BF16)
         weight = weight - part.astype(F32)
         parts.append(part)
+    stacked = jnp.concatenate(parts, axis=1)
     rows = []
     for field in range(fields):
-        mixed = None
-        for part in parts:
-            term = lax.dot_general(
-                part, nwp_ref[field], (((0,), (0,)), ((), ())), preferred_element_type=F32
-            )
-            mixed = term if mixed is None else mixed + term
-        rows.append(mixed.astype(BF16))
+        mixed = lax.dot_general(
+            stacked, nwp_ref[field], (((0,), (0,)), ((), ())), preferred_element_type=F32
+        )
+        rows.append((mixed[:kept] + mixed[kept : 2 * kept] + mixed[2 * kept :]).astype(BF16))
     levels = jnp.concatenate(rows, axis=0)
     half = LANES // 2
     width = 2 * LANES
-    inner = lax.broadcasted_iota(jnp.int32, (SPLIT, width), 0)
-    none = jnp.zeros((SPLIT, width), BF16)
     first = lane_ids((kept, LANES)) < half
     copies = []
     for block in range(pick_ref.shape[0] // 4):
         wanted = jnp.concatenate([pick_ref[4 * block + i : 4 * block + i + 1] for i in range(4)], axis=1)
-        group = wanted // SPLIT
-        unit = jnp.where(inner == wanted - group * SPLIT, 1.0, 0.0).astype(BF16)
-        group = jnp.broadcast_to(group.astype(F32), (SPLIT, width)).astype(BF16)
-        hit = jnp.concatenate([jnp.where(group == g, unit, none) for g in range(count // SPLIT)], axis=0)
+        hit = one_hot(wanted, count)
         got = jnp.dot(levels, hit, preferred_element_type=F32)
         for h in range(2):
             east = got[:kept, h * LANES : (h + 1) * LANES]
@@ -95,45 +100,6 @@
         copy.wait()
 
 
-def corner_tables(slot_ref, wt_ref, count):
-    slots = [slot_ref[q] for q in range(4)]
-    raw = [wt_ref[q] for q in range(4)]
-    total = raw[0] + raw[1] + raw[2] + raw[3]
-    norm = [w / total for w in raw]
-    groups, units, highs, lows = [], [], [], []
-    for q in range(4):
-        share = None
-        for other in range(4):
-            term = jnp.where(slots[q] == slots[other], norm[other], 0.0)
-            share = term if share is None else share + term
-        for other in range(q):
-            share = jnp.where(slots[q] == slots[other], 0.0, share)
-        high = share.astype(BF16).astype(F32)
-        group = slots[q] // SPLIT
-        groups.append(group.astype(F32))
-        units.append(slots[q] - group * SPLIT)
-        highs.append(high)
-        lows.append(share - high)
-    inner = lax.broadcasted_iota(jnp.int32, (SPLIT, LANES), 0)
-    none = jnp.zeros((SPLIT, LANES), BF16)
-
-    def tables(y):
-        line = slice(y, y + 1)
-        hits = [inner == units[q][line] for q in range(4)]
-        group = [jnp.broadcast_to(groups[q][line], (SPLIT, LANES)).astype(BF16) for q in range(4)]
-        result = []
-        for parts in (highs, lows):
-            own = [jnp.where(hits[q], parts[q][line], 0.0).astype(BF16) for q in range(4)]
-            blocks = []
-            for g in range(count // SPLIT):
-                two = [jnp.where(group[q] == g, own[q], none) for q in range(4)]
-                blocks.append((two[0] + two[1]) + (two[2] + two[3]))
-            result.append(jnp.concatenate(blocks, axis=0))
-        return result
-
-    return tables
-
-
 def horizontal_kernel(recv_ref, slot_ref, wt_ref, winds_ref, a_ref, b_ref, lev_ref):
     kept = recv_ref.shape[1]
     half = LANES // 2
@@ -146,15 +112,19 @@
         lev_ref[kept:, at] = jnp.where(first, roll_lanes(one, half), two).astype(BF16)
     rows = winds_ref.shape[0]
     lev = lev_ref[...]
-    tables = corner_tables(slot_ref, wt_ref, lev_ref.shape[1])
+    raw = [wt_ref[q] for q in range(4)]
+    total = raw[0] + raw[1] + raw[2] + raw[3]
+    norm = [w / total for w in raw]
     for y in range(0, rows, 2):
-        one, two = tables(y), tables(y + 1)
-        got = sum(
-            jnp.dot(lev, jnp.concatenate(pair, axis=1), preferred_element_type=F32)
-            for pair in zip(one, two)
-        )
-        winds_ref[y] = got[:, :LANES]
-        winds_ref[y + 1] = got[:, LANES:]
+        winds = [None, None]
+        for q in range(4):
+            wanted = jnp.concatenate([slot_ref[q, y + h : y + h + 1] for h in range(2)], axis=1)
+            got = jnp.dot(lev, one_hot(wanted, lev_ref.shape[1]), preferred_element_type=F32)
+            for h in range(2):
+                term = norm[q][y + h : y + h + 1] * got[:, h * LANES : (h + 1) * LANES]
+                winds[h] = term if winds[h] is None else winds[h] + term
+        winds_ref[y] = winds[0]
+        winds_ref[y + 1] = winds[1]
     odd = lax.axis_index("rows") % 2 == 1
     for j in range(HALO):
         upper = winds_ref[j]
@@ -557,7 +527,7 @@
             pltpu.VMEM((peers, levels, LANES), BF16),
             pltpu.SemaphoreType.DMA((peers // 4,)),
         ),
-        out_space=pltpu.HBM,
+        out_spaces=(pltpu.HBM,),
         flops=2 * 2 * levels * 2048 * 2048,
     )
 

time: 50.2 us -> 49.1 us (0.978)
  Pallas kernels: 18.7 us -> 17.5 us
    pallas_call x7, Pallas kernels: 18.7 us -> 17.5 us  [call(): pl.pallas_call(kernel, out_shape=out_shape, in_specs=[pl.BlockSpec(memory...]
  transfers between devices with their start and end apart: 7 -> 7, of which waited for: 4 -> 4; matrix products, arithmetic and copies ran while one was open for 0% -> 0% of each run, Pallas kernels for 19% -> 17%
where the time goes in v4:
time: 49.1 us; the launch traced here: 48.7 us
  starting transfers between devices  20.9 us (43%)
  Pallas kernels  17.5 us (36%)
  waiting for transfers between devices  7.76 us (16%)
  local copies, waits for them, and re-layouts  1.73 us (4%)
  between operations  0.85 us (2%)
    pallas_call x7, Pallas kernels, call(): pl.pallas_call(kernel, out_shape=out_shape, in_specs=[pl.BlockSpec(memory...  17.5 us
    ppermute x6, starting transfers between devices, swap(): return lax.ppermute(array, axis, pairs)  12.4 us
    all_to_all x1, starting transfers between devices, per_device(): lax.all_to_all(sent, 'rows', split_axis=0, concat_axis=0, tiled=True)  8.48 us
    ppermute x6, waiting for transfers between devices, swap(): return lax.ppermute(array, axis, pairs)  3.97 us
    all_to_all x1, waiting for transfers between devices, per_device(): lax.all_to_all(sent, 'rows', split_axis=0, concat_axis=0, tiled=True)  3.79 us
    unnamed x19, local copies, waits for them, and re-layouts  1.73 us
  transfers between devices with their start and end apart: 7, of which 4 were waited for; matrix products, arithmetic and copies ran while one was open for 0% of the time, Pallas kernels for 17%

profile of v4, /device:TPU:10, one launch (start us, length us, event | category | flops | bytes accessed | tf_op | source)
XLA Modules:
  0.0 48.7 jit_solution(1824341577234906750)
XLA Ops:
  0.6 0.0 copy-start.4
  0.6 0.0 copy-start.8
  0.7 0.0 copy-start.7
  0.7 1.7 %copy.12.nwp_ref = bf16[2,137,2048]{2,1,0:T(8,128)(2,1)S(1)} copy(bf16[2,137,2048]{2,0,1:T(2,128)(2,1)} %param.11) | data formatting | bytes 2244608 | tf_op args[1]
  2.3 0.0 copy-done.4
  2.4 0.0 copy-done.8
  2.4 0.0 copy-done.7
  2.4 0.0 copy-start
  2.4 0.0 copy-start.1
  2.4 2.7 %shard_map.113 = bf16[32,48,128]{2,1,0:T(8,128)(2,1)} custom-call(s32[1,48]{1,0:T(1,128)S(1)} %bitcast.10, f32[1,48]{1,0:T(1,128)S(1)} %bitcast.11, s32[32,64]{1,0:T(8,128)S(1)} %bitcast.9, bf16[2,137,2048]{2,1,0:T(8,128)(2,1)S(1)} %copy.12.nwp_ref), custom_call_target="tpu_custom_call" | custom-call | flops 805306368 | bytes 1524096 | tf_op jit(solution)/shard_map/pallas_call | solution.py:38
  5.1 0.0 copy-start.5
  5.1 0.0 copy-start.6
  5.1 8.5 %all-to-all-start = ((bf16[32,48,128]{2,1,0:T(8,128)(2,1)}), bf16[32,48,128]{2,1,0:T(8,128)(2,1)S(1)}, u32[]{:S(2)}, u32[]{:S(2)}) async-start(bf16[32,48,128]{2,1,0:T(8,128)(2,1)} %shard_map.113), calls=%async_computation | async-start | bytes 786432 | tf_op jit(solution)/shard_map/all_to_all | solution.py:535
  13.6 0.0 copy-done
  13.6 0.0 copy-done.1
  13.7 0.7 %shard_map.114 = (bf16[3,25,16,128]{3,2,1,0:T(8,128)(2,1)S(1)}, bf16[3,25,16,128]{3,2,1,0:T(8,128)(2,1)S(1)}) custom-call(f32[3072,128]{1,0:T(8,128)S(1)} %bitcast.6, s32[8,128]{1,0:T(8,128)S(1)} %copy-done.1), custom_call_target="tpu_custom_call" | custom-call | tf_op jit(solution)/shard_map/pallas_call | solution.py:38
  14.3 0.2 collective-permute-start
  14.6 4.5 %collective-permute-start.1 = (bf16[3,25,16,128]{3,2,1,0:T(8,128)(2,1)S(1)}, bf16[3,25,16,128]{3,2,1,0:T(8,128)(2,1)S(1)}, u32[]{:S(2)}, u32[]{:S(2)}) collective-permute-start(bf16[3,25,16,128]{3,2,1,0:T(8,128)(2,1)S(1)} %get-tuple-element.18), channel_id=1, source_target_pairs={{4,8},{8,4},{12,16},{16,12},{20,24},{24,20},{28,32},{32,28},{36,40... | collective-permute-start | bytes 921608 | tf_op jit(solution)/shard_map/ppermute | solution.py:142
  19.1 3.8 %all-to-all-done.recv_ref = bf16[32,48,128]{2,1,0:T(8,128)(2,1)S(1)} async-done(((bf16[32,48,128]{2,1,0:T(8,128)(2,1)}), bf16[32,48,128]{2,1,0:T(8,128)(2,1)S(1)}, u32[]{:S(2)}, u32[]{:S(2)}) %all-to-all-start) | async-done | bytes 393248 | tf_op jit(solution)/shard_map/all_to_all | solution.py:535
  22.9 0.0 copy-done.5
  22.9 0.0 copy-done.6
  22.9 2.9 %shard_map.115 = (f32[8,96,128]{2,1,0:T(8,128)S(1)}, bf16[3,96,128]{2,1,0:T(8,128)(2,1)S(1)}, bf16[3,96,128]{2,1,0:T(8,128)(2,1)S(1)}) custom-call(bf16[32,48,128]{2,1,0:T(8,128)(2,1)S(1)} %all-to-all-done.recv_ref, s32[4,8,128]{2,1,0:T(8,128)S(1)} %copy-done.5, f32[4,8,128]{2,1,0:T(8,128)S(1)} %copy-done.6), custom_call_target="tpu_custom_call" | custom-call | flops 49999998976 | bytes 966656 | tf_op jit(solution)/shard_map/pallas_call | solution.py:38
  25.8 4.0 %collective-permute-start.3 = (bf16[3,96,128]{2,1,0:T(8,128)(2,1)S(1)}, bf16[3,96,128]{2,1,0:T(8,128)(2,1)S(1)}, u32[]{:S(2)}, u32[]{:S(2)}) collective-permute-start(bf16[3,96,128]{2,1,0:T(8,128)(2,1)S(1)} %get-tuple-element.24), channel_id=1, source_target_pairs={{4,8},{8,4},{12,16},{16,12},{20,24},{24,20},{28,32},{32,28},{36,40... | collective-permute-start | bytes 221192 | tf_op jit(solution)/shard_map/ppermute | solution.py:142
  29.8 0.1 collective-permute-start.2
  29.9 0.0 collective-permute-done.ra_ref
  29.9 0.0 collective-permute-done.1.rb_ref
  29.9 1.7 %shard_map.117.conc_ref = bf16[400,128]{1,0:T(8,128)(2,1)S(1)} custom-call(f32[3072,128]{1,0:T(8,128)S(1)} %bitcast.7, s32[8,128]{1,0:T(8,128)S(1)} %copy-done.1, bf16[3,25,16,128]{3,2,1,0:T(8,128)(2,1)S(1)} %collective-permute-done.ra_ref, bf16[3,25,16,128]{3,2,1,0:T(8,128)(2,1)S(1)} %collective-permute-done.1.rb_ref), custom_call_target="tpu_custom_call" | custom-call | tf_op jit(solution)/shard_map/pallas_call | solution.py:38
  31.6 2.0 %collective-permute-done.3.wrb_ref.rb_ref = bf16[3,96,128]{2,1,0:T(8,128)(2,1)S(1)} collective-permute-done((bf16[3,96,128]{2,1,0:T(8,128)(2,1)S(1)}, bf16[3,96,128]{2,1,0:T(8,128)(2,1)S(1)}, u32[]{:S(2)}, u32[]{:S(2)}) %collective-permute-start.3) | collective-permute-done | bytes 73760 | tf_op jit(solution)/shard_map/ppermute | solution.py:142
  33.6 0.0 collective-permute-done.2.wra_ref.ra_ref
  33.6 0.0 copy-start.3
  33.6 0.3 shard_map.118.own_ref
  33.9 0.0 copy-start.2
  33.9 3.5 %collective-permute-start.5 = (bf16[496,128]{1,0:T(8,128)(2,1)S(1)}, bf16[496,128]{1,0:T(8,128)(2,1)S(1)}, u32[]{:S(2)}, u32[]{:S(2)}) collective-permute-start(bf16[496,128]{1,0:T(8,128)(2,1)S(1)} %shard_map.118.own_ref), channel_id=1, source_target_pairs={{1,2},{2,1},{5,6},{6,5},{9,10},{10,9},{13,14},{14,13},{17,18},{18,... | collective-permute-start | bytes 380936 | tf_op jit(solution)/shard_map/ppermute | solution.py:142
  37.4 0.1 collective-permute-start.4
  37.5 0.0 copy-done.3
  37.5 2.9 %shard_map.116 = (f32[60,48,128]{2,1,0:T(8,128)S(1)}, f32[12,384,128]{2,1,0:T(8,128)S(1)}, f32[8,8,128]{2,1,0:T(8,128)S(1)}) custom-call(f32[3072,128]{1,0:T(8,128)S(1)} %bitcast.8, f32[8]{0:T(128)S(1)} %copy-done.3, bf16[3,25,16,128]{3,2,1,0:T(8,128)(2,1)S(1)} %collective-permute-done.ra_ref, bf16[3,25,16,128]{3,2,1,0:T(8,128)(2,1)S(1)} %collective-permute-done.1.rb_ref, ...), custom_call_target="tpu_custom_call" | custom-call | tf_op jit(solution)/shard_map/pallas_call | solution.py:38
  40.4 0.3 collective-permute-done.5.xb_ref
  40.7 1.7 %collective-permute-done.4.xa_ref = bf16[496,128]{1,0:T(8,128)(2,1)S(1)} collective-permute-done((bf16[496,128]{1,0:T(8,128)(2,1)S(1)}, bf16[496,128]{1,0:T(8,128)(2,1)S(1)}, u32[]{:S(2)}, u32[]{:S(2)}) %collective-permute-start.4) | collective-permute-done | bytes 127008 | tf_op jit(solution)/shard_map/ppermute | solution.py:142
  42.4 0.0 copy-done.2
  42.4 6.4 %shard_map.119 = (f32[3072,128]{1,0:T(8,128)}, f32[64,128]{1,0:T(8,128)}) custom-call(f32[12,384,128]{2,1,0:T(8,128)S(1)} %get-tuple-element.25.part_ref, f32[60,48,128]{2,1,0:T(8,128)S(1)} %get-tuple-element.26.coef_ref, f32[8,8,128]{2,1,0:T(8,128)S(1)} %get-tuple-element.27.fallen_ref, s32[8,128]{1,0:T(8,128)S(1)} %copy-done.1, f32[8]{0:T(128)S(1)} %copy-done.3, ...), custom_call_target="tpu_custom_call" | custom-call | flops 23592960 | bytes 6473248 | tf_op jit(solution)/shard_map/pallas_call | solution.py:38
Async XLA Ops:
  0.6 1.7 %copy-start.4 = (s32[1,1,32,64]{3,2,1,0:T(8,128)S(1)}, s32[1,1,32,64]{3,2,1,0:T(8,128)}, u32[]{:S(2)}) copy-start(s32[1,1,32,64]{3,2,1,0:T(8,128)} %param.14) | copy-start | bytes 24580
  0.6 1.7 %copy-start.8 = (f32[48]{0:T(128)S(1)}, f32[48]{0:T(128)}, u32[]{:S(2)}) copy-start(f32[48]{0:T(128)} %param.13) | copy-start | bytes 580
  0.7 1.7 %copy-start.7 = (s32[48]{0:T(128)S(1)}, s32[48]{0:T(128)}, u32[]{:S(2)}) copy-start(s32[48]{0:T(128)} %param.12) | copy-start | bytes 580
  2.4 11.3 %copy-start = (f32[8,48,8,128]{3,2,1,0:T(8,128)S(1)}, f32[8,48,8,128]{3,2,1,0:T(8,128)}, u32[]{:S(2)}) copy-start(f32[8,48,8,128]{3,2,1,0:T(8,128)} %param.10) | copy-start | bytes 4718596
  2.4 11.3 %copy-start.1 = (s32[8,128]{1,0:T(8,128)S(1)}, s32[8,128]{1,0:T(8,128)}, u32[]{:S(2)}) copy-start(s32[8,128]{1,0:T(8,128)} %mask_ref.5) | copy-start | bytes 12292
  5.1 17.8 %copy-start.5 = (s32[4,8,128]{2,1,0:T(8,128)S(1)}, s32[4,8,128]{2,1,0:T(8,128)}, u32[]{:S(2)}) copy-start(s32[4,8,128]{2,1,0:T(8,128)} %slot_ref.1) | copy-start | bytes 49156
  5.1 17.8 %copy-start.6 = (f32[4,8,128]{2,1,0:T(8,128)S(1)}, f32[4,8,128]{2,1,0:T(8,128)}, u32[]{:S(2)}) copy-start(f32[4,8,128]{2,1,0:T(8,128)} %wt_ref.1) | copy-start | bytes 49156
  5.1 17.8 %all-to-all-start = ((bf16[32,48,128]{2,1,0:T(8,128)(2,1)}), bf16[32,48,128]{2,1,0:T(8,128)(2,1)S(1)}, u32[]{:S(2)}, u32[]{:S(2)}) async-start(bf16[32,48,128]{2,1,0:T(8,128)(2,1)} %shard_map.113), calls=%async_computation | async-start | bytes 786432 | tf_op jit(solution)/shard_map/all_to_all | solution.py:535
  14.3 15.5 %collective-permute-start = (bf16[3,25,16,128]{3,2,1,0:T(8,128)(2,1)S(1)}, bf16[3,25,16,128]{3,2,1,0:T(8,128)(2,1)S(1)}, u32[]{:S(2)}, u32[]{:S(2)}) collective-permute-start(bf16[3,25,16,128]{3,2,1,0:T(8,128)(2,1)S(1)} %get-tuple-element.17), channel_id=1, source_target_pairs={{0,4},{4,0},{8,12},{12,8},{16,20},{20,16},{24,28},{28,24},{32,36},... | collective-permute-start | bytes 921608 | tf_op jit(solution)/shard_map/ppermute | solution.py:142
  14.6 15.3 %collective-permute-start.1 = (bf16[3,25,16,128]{3,2,1,0:T(8,128)(2,1)S(1)}, bf16[3,25,16,128]{3,2,1,0:T(8,128)(2,1)S(1)}, u32[]{:S(2)}, u32[]{:S(2)}) collective-permute-start(bf16[3,25,16,128]{3,2,1,0:T(8,128)(2,1)S(1)} %get-tuple-element.18), channel_id=1, source_target_pairs={{4,8},{8,4},{12,16},{16,12},{20,24},{24,20},{28,32},{32,28},{36,40... | collective-permute-start | bytes 921608 | tf_op jit(solution)/shard_map/ppermute | solution.py:142
  25.8 7.8 %collective-permute-start.3 = (bf16[3,96,128]{2,1,0:T(8,128)(2,1)S(1)}, bf16[3,96,128]{2,1,0:T(8,128)(2,1)S(1)}, u32[]{:S(2)}, u32[]{:S(2)}) collective-permute-start(bf16[3,96,128]{2,1,0:T(8,128)(2,1)S(1)} %get-tuple-element.24), channel_id=1, source_target_pairs={{4,8},{8,4},{12,16},{16,12},{20,24},{24,20},{28,32},{32,28},{36,40... | collective-permute-start | bytes 221192 | tf_op jit(solution)/shard_map/ppermute | solution.py:142
  29.8 3.8 %collective-permute-start.2 = (bf16[3,96,128]{2,1,0:T(8,128)(2,1)S(1)}, bf16[3,96,128]{2,1,0:T(8,128)(2,1)S(1)}, u32[]{:S(2)}, u32[]{:S(2)}) collective-permute-start(bf16[3,96,128]{2,1,0:T(8,128)(2,1)S(1)} %get-tuple-element.20), channel_id=1, source_target_pairs={{0,4},{4,0},{8,12},{12,8},{16,20},{20,16},{24,28},{28,24},{32,36},... | collective-permute-start | bytes 221192 | tf_op jit(solution)/shard_map/ppermute | solution.py:142
  33.6 3.9 %copy-start.3 = (f32[8]{0:T(128)S(1)}, f32[8]{0:T(128)}, u32[]{:S(2)}) copy-start(f32[8]{0:T(128)} %settle_ref.3) | copy-start | bytes 100
  33.9 8.5 %copy-start.2 = (f32[8,48]{1,0:T(8,128)S(1)}, f32[8,48]{1,0:T(8,128)}, u32[]{:S(2)}) copy-start(f32[8,48]{1,0:T(8,128)} %profile_ref.1) | copy-start | bytes 4612
  33.9 6.8 %collective-permute-start.5 = (bf16[496,128]{1,0:T(8,128)(2,1)S(1)}, bf16[496,128]{1,0:T(8,128)(2,1)S(1)}, u32[]{:S(2)}, u32[]{:S(2)}) collective-permute-start(bf16[496,128]{1,0:T(8,128)(2,1)S(1)} %shard_map.118.own_ref), channel_id=1, source_target_pairs={{1,2},{2,1},{5,6},{6,5},{9,10},{10,9},{13,14},{14,13},{17,18},{18,... | collective-permute-start | bytes 380936 | tf_op jit(solution)/shard_map/ppermute | solution.py:142
  37.4 5.0 %collective-permute-start.4 = (bf16[496,128]{1,0:T(8,128)(2,1)S(1)}, bf16[496,128]{1,0:T(8,128)(2,1)S(1)}, u32[]{:S(2)}, u32[]{:S(2)}) collective-permute-start(bf16[496,128]{1,0:T(8,128)(2,1)S(1)} %shard_map.118.own_ref), channel_id=1, source_target_pairs={{0,1},{1,0},{2,3},{3,2},{4,5},{5,4},{6,7},{7,6},{8,9},{9,8},{10,11... | collective-permute-start | bytes 380936 | tf_op jit(solution)/shard_map/ppermute | solution.py:142

commit v5 on v4

--- a/solution.py
+++ b/solution.py
@@ -296,7 +296,7 @@
 
     settle = settle_tile(settle_ref, tile)
     fall_ref[...] = jnp.zeros(fall_ref.shape, F32)
-    unroll = 8
+    unroll = 16
 
     def some_levels(trip, carry):
         ks = [trip * unroll + u for u in range(unroll)]
@@ -394,6 +394,7 @@
     spare = STRIP * STRIP_ROWS
     mask_strip = strip_at(levels * bins, two)[:bins]
     fall_before = [jnp.zeros(tile, F32)] * (STEPS - 1)
+    flows = [[] for _ in range(STEPS)]
     edges = None
     for k in range(levels):
         if k % 2 == 0:
@@ -417,7 +418,9 @@
             for i, part in enumerate(parts):
                 flow = jnp.where(tile_lanes == spare + i, part, flow)
             flow = jnp.where(tile_lanes >= spare + 3, 0.0, flow)
-            bound_ref[step, k * bins : (k + 1) * bins] = flow
+            flows[step].append(flow)
+            if k % 2:
+                bound_ref[step, (k - 1) * bins : (k + 1) * bins] = jnp.concatenate(flows[step][-2:]).astype(BF16)
             if step < STEPS - 1:
                 fall = settle * edge
                 edge = (
@@ -445,14 +448,11 @@
             )[:1]
         emits = (lane_of >= spare) & (lane_of < spare + 3)
         table = jnp.where(hit, 1.0, jnp.where(emits, line, 0.0)).astype(BF16)
-        spread.append(jnp.concatenate([table, table], axis=0))
+        spread.append(table)
     slot = 0
     slots = {}
     for step in range(STEPS):
-        flow = bound_ref[step]
-        high = flow.astype(BF16)
-        low = (flow - high.astype(F32)).astype(BF16)
-        both = jnp.concatenate([high, low], axis=1)
+        both = bound_ref[step]
         reach = STEPS - 1 - step
         for y in range(-reach, rows + reach, 2):
             pair = jnp.concatenate([spread[y + 2], spread[y + 3]], axis=1)
@@ -463,7 +463,7 @@
                 slot += 1
 
     fall_ref[...] = jnp.zeros(fall_ref.shape, F32)
-    unroll = 8
+    unroll = 16
     skipped = slots[1, -1]
 
     def some_levels(trip, carry):
@@ -587,7 +587,7 @@
         scratch=(
             pltpu.VMEM((rows + 2, levels, LANES), F32),
             pltpu.VMEM((6, levels, LANES), F32),
-            pltpu.VMEM((STEPS, levels * bins, LANES), F32),
+            pltpu.VMEM((STEPS, levels * bins, LANES), BF16),
             pltpu.VMEM((updates, levels * bins, LANES), F32),
             pltpu.VMEM((updates - rows - 4,) + tile, F32),
         ),

time: 49.1 us -> 48.8 us (level)
  no operation moved by 1% of the time
where the time goes in v5:
time: 48.8 us; the launch traced here: 48.5 us
  starting transfers between devices  20.9 us (43%)
  Pallas kernels  17.2 us (35%)
  waiting for transfers between devices  7.8 us (16%)
  local copies, waits for them, and re-layouts  1.73 us (4%)
  between operations  0.85 us (2%)
    pallas_call x7, Pallas kernels, call(): pl.pallas_call(kernel, out_shape=out_shape, in_specs=[pl.BlockSpec(memory...  17.2 us
    ppermute x6, starting transfers between devices, swap(): return lax.ppermute(array, axis, pairs)  12.4 us
    all_to_all x1, starting transfers between devices, per_device(): lax.all_to_all(sent, 'rows', split_axis=0, concat_axis=0, tiled=True)  8.48 us
    ppermute x6, waiting for transfers between devices, swap(): return lax.ppermute(array, axis, pairs)  4.01 us
    all_to_all x1, waiting for transfers between devices, per_device(): lax.all_to_all(sent, 'rows', split_axis=0, concat_axis=0, tiled=True)  3.79 us
    unnamed x19, local copies, waits for them, and re-layouts  1.73 us
  transfers between devices with their start and end apart: 7, of which 4 were waited for; matrix products, arithmetic and copies ran while one was open for 0% of the time, Pallas kernels for 17%

profile of v5, /device:TPU:10, one launch (start us, length us, event | category | flops | bytes accessed | tf_op | source)
XLA Modules:
  0.0 48.5 jit_solution(8052535220988298753)
XLA Ops:
  0.6 0.0 copy-start.4
  0.6 0.0 copy-start.8
  0.7 0.0 copy-start.7
  0.7 1.7 %copy.12.nwp_ref = bf16[2,137,2048]{2,1,0:T(8,128)(2,1)S(1)} copy(bf16[2,137,2048]{2,0,1:T(2,128)(2,1)} %param.11) | data formatting | bytes 2244608 | tf_op args[1]
  2.3 0.0 copy-done.4
  2.4 0.0 copy-done.8
  2.4 0.0 copy-done.7
  2.4 0.0 copy-start
  2.4 0.0 copy-start.1
  2.4 2.7 %shard_map.113 = bf16[32,48,128]{2,1,0:T(8,128)(2,1)} custom-call(s32[1,48]{1,0:T(1,128)S(1)} %bitcast.10, f32[1,48]{1,0:T(1,128)S(1)} %bitcast.11, s32[32,64]{1,0:T(8,128)S(1)} %bitcast.9, bf16[2,137,2048]{2,1,0:T(8,128)(2,1)S(1)} %copy.12.nwp_ref), custom_call_target="tpu_custom_call" | custom-call | flops 805306368 | bytes 1524096 | tf_op jit(solution)/shard_map/pallas_call | solution.py:38
  5.1 0.0 copy-start.5
  5.1 0.0 copy-start.6
  5.1 8.5 %all-to-all-start = ((bf16[32,48,128]{2,1,0:T(8,128)(2,1)}), bf16[32,48,128]{2,1,0:T(8,128)(2,1)S(1)}, u32[]{:S(2)}, u32[]{:S(2)}) async-start(bf16[32,48,128]{2,1,0:T(8,128)(2,1)} %shard_map.113), calls=%async_computation | async-start | bytes 786432 | tf_op jit(solution)/shard_map/all_to_all | solution.py:535
  13.6 0.0 copy-done
  13.6 0.0 copy-done.1
  13.7 0.7 %shard_map.114 = (bf16[3,25,16,128]{3,2,1,0:T(8,128)(2,1)S(1)}, bf16[3,25,16,128]{3,2,1,0:T(8,128)(2,1)S(1)}) custom-call(f32[3072,128]{1,0:T(8,128)S(1)} %bitcast.6, s32[8,128]{1,0:T(8,128)S(1)} %copy-done.1), custom_call_target="tpu_custom_call" | custom-call | tf_op jit(solution)/shard_map/pallas_call | solution.py:38
  14.3 0.2 collective-permute-start
  14.6 4.5 %collective-permute-start.1 = (bf16[3,25,16,128]{3,2,1,0:T(8,128)(2,1)S(1)}, bf16[3,25,16,128]{3,2,1,0:T(8,128)(2,1)S(1)}, u32[]{:S(2)}, u32[]{:S(2)}) collective-permute-start(bf16[3,25,16,128]{3,2,1,0:T(8,128)(2,1)S(1)} %get-tuple-element.18), channel_id=1, source_target_pairs={{4,8},{8,4},{12,16},{16,12},{20,24},{24,20},{28,32},{32,28},{36,40... | collective-permute-start | bytes 921608 | tf_op jit(solution)/shard_map/ppermute | solution.py:142
  19.1 3.8 %all-to-all-done.recv_ref = bf16[32,48,128]{2,1,0:T(8,128)(2,1)S(1)} async-done(((bf16[32,48,128]{2,1,0:T(8,128)(2,1)}), bf16[32,48,128]{2,1,0:T(8,128)(2,1)S(1)}, u32[]{:S(2)}, u32[]{:S(2)}) %all-to-all-start) | async-done | bytes 393248 | tf_op jit(solution)/shard_map/all_to_all | solution.py:535
  22.9 0.0 copy-done.5
  22.9 0.0 copy-done.6
  22.9 2.9 %shard_map.115 = (f32[8,96,128]{2,1,0:T(8,128)S(1)}, bf16[3,96,128]{2,1,0:T(8,128)(2,1)S(1)}, bf16[3,96,128]{2,1,0:T(8,128)(2,1)S(1)}) custom-call(bf16[32,48,128]{2,1,0:T(8,128)(2,1)S(1)} %all-to-all-done.recv_ref, s32[4,8,128]{2,1,0:T(8,128)S(1)} %copy-done.5, f32[4,8,128]{2,1,0:T(8,128)S(1)} %copy-done.6), custom_call_target="tpu_custom_call" | custom-call | flops 49999998976 | bytes 966656 | tf_op jit(solution)/shard_map/pallas_call | solution.py:38
  25.8 4.0 %collective-permute-start.3 = (bf16[3,96,128]{2,1,0:T(8,128)(2,1)S(1)}, bf16[3,96,128]{2,1,0:T(8,128)(2,1)S(1)}, u32[]{:S(2)}, u32[]{:S(2)}) collective-permute-start(bf16[3,96,128]{2,1,0:T(8,128)(2,1)S(1)} %get-tuple-element.24), channel_id=1, source_target_pairs={{4,8},{8,4},{12,16},{16,12},{20,24},{24,20},{28,32},{32,28},{36,40... | collective-permute-start | bytes 221192 | tf_op jit(solution)/shard_map/ppermute | solution.py:142
  29.8 0.1 collective-permute-start.2
  29.9 0.0 collective-permute-done.ra_ref
  29.9 0.0 collective-permute-done.1.rb_ref
  29.9 1.7 %shard_map.117.conc_ref = bf16[400,128]{1,0:T(8,128)(2,1)S(1)} custom-call(f32[3072,128]{1,0:T(8,128)S(1)} %bitcast.7, s32[8,128]{1,0:T(8,128)S(1)} %copy-done.1, bf16[3,25,16,128]{3,2,1,0:T(8,128)(2,1)S(1)} %collective-permute-done.ra_ref, bf16[3,25,16,128]{3,2,1,0:T(8,128)(2,1)S(1)} %collective-permute-done.1.rb_ref), custom_call_target="tpu_custom_call" | custom-call | tf_op jit(solution)/shard_map/pallas_call | solution.py:38
  31.6 2.0 %collective-permute-done.3.wrb_ref.rb_ref = bf16[3,96,128]{2,1,0:T(8,128)(2,1)S(1)} collective-permute-done((bf16[3,96,128]{2,1,0:T(8,128)(2,1)S(1)}, bf16[3,96,128]{2,1,0:T(8,128)(2,1)S(1)}, u32[]{:S(2)}, u32[]{:S(2)}) %collective-permute-start.3) | collective-permute-done | bytes 73760 | tf_op jit(solution)/shard_map/ppermute | solution.py:142
  33.6 0.0 collective-permute-done.2.wra_ref.ra_ref
  33.6 0.0 copy-start.3
  33.6 0.3 shard_map.118.own_ref
  33.9 0.0 copy-start.2
  33.9 3.5 %collective-permute-start.5 = (bf16[496,128]{1,0:T(8,128)(2,1)S(1)}, bf16[496,128]{1,0:T(8,128)(2,1)S(1)}, u32[]{:S(2)}, u32[]{:S(2)}) collective-permute-start(bf16[496,128]{1,0:T(8,128)(2,1)S(1)} %shard_map.118.own_ref), channel_id=1, source_target_pairs={{1,2},{2,1},{5,6},{6,5},{9,10},{10,9},{13,14},{14,13},{17,18},{18,... | collective-permute-start | bytes 380936 | tf_op jit(solution)/shard_map/ppermute | solution.py:142
  37.4 0.1 collective-permute-start.4
  37.5 0.0 copy-done.3
  37.5 2.9 %shard_map.116 = (f32[60,48,128]{2,1,0:T(8,128)S(1)}, f32[12,384,128]{2,1,0:T(8,128)S(1)}, f32[8,8,128]{2,1,0:T(8,128)S(1)}) custom-call(f32[3072,128]{1,0:T(8,128)S(1)} %bitcast.8, f32[8]{0:T(128)S(1)} %copy-done.3, bf16[3,25,16,128]{3,2,1,0:T(8,128)(2,1)S(1)} %collective-permute-done.ra_ref, bf16[3,25,16,128]{3,2,1,0:T(8,128)(2,1)S(1)} %collective-permute-done.1.rb_ref, ...), custom_call_target="tpu_custom_call" | custom-call | tf_op jit(solution)/shard_map/pallas_call | solution.py:38
  40.4 0.3 collective-permute-done.5.xb_ref
  40.7 1.7 %collective-permute-done.4.xa_ref = bf16[496,128]{1,0:T(8,128)(2,1)S(1)} collective-permute-done((bf16[496,128]{1,0:T(8,128)(2,1)S(1)}, bf16[496,128]{1,0:T(8,128)(2,1)S(1)}, u32[]{:S(2)}, u32[]{:S(2)}) %collective-permute-start.4) | collective-permute-done | bytes 127008 | tf_op jit(solution)/shard_map/ppermute | solution.py:142
  42.4 0.0 copy-done.2
  42.4 6.1 %shard_map.119 = (f32[3072,128]{1,0:T(8,128)}, f32[64,128]{1,0:T(8,128)}) custom-call(f32[12,384,128]{2,1,0:T(8,128)S(1)} %get-tuple-element.25.part_ref, f32[60,48,128]{2,1,0:T(8,128)S(1)} %get-tuple-element.26.coef_ref, f32[8,8,128]{2,1,0:T(8,128)S(1)} %get-tuple-element.27.fallen_ref, s32[8,128]{1,0:T(8,128)S(1)} %copy-done.1, f32[8]{0:T(128)S(1)} %copy-done.3, ...), custom_call_target="tpu_custom_call" | custom-call | flops 23592960 | bytes 6473248 | tf_op jit(solution)/shard_map/pallas_call | solution.py:38
Async XLA Ops:
  0.6 1.7 %copy-start.4 = (s32[1,1,32,64]{3,2,1,0:T(8,128)S(1)}, s32[1,1,32,64]{3,2,1,0:T(8,128)}, u32[]{:S(2)}) copy-start(s32[1,1,32,64]{3,2,1,0:T(8,128)} %param.14) | copy-start | bytes 24580
  0.6 1.7 %copy-start.8 = (f32[48]{0:T(128)S(1)}, f32[48]{0:T(128)}, u32[]{:S(2)}) copy-start(f32[48]{0:T(128)} %param.13) | copy-start | bytes 580
  0.7 1.7 %copy-start.7 = (s32[48]{0:T(128)S(1)}, s32[48]{0:T(128)}, u32[]{:S(2)}) copy-start(s32[48]{0:T(128)} %param.12) | copy-start | bytes 580
  2.4 11.3 %copy-start = (f32[8,48,8,128]{3,2,1,0:T(8,128)S(1)}, f32[8,48,8,128]{3,2,1,0:T(8,128)}, u32[]{:S(2)}) copy-start(f32[8,48,8,128]{3,2,1,0:T(8,128)} %param.10) | copy-start | bytes 4718596
  2.4 11.3 %copy-start.1 = (s32[8,128]{1,0:T(8,128)S(1)}, s32[8,128]{1,0:T(8,128)}, u32[]{:S(2)}) copy-start(s32[8,128]{1,0:T(8,128)} %mask_ref.5) | copy-start | bytes 12292
  5.1 17.8 %copy-start.5 = (s32[4,8,128]{2,1,0:T(8,128)S(1)}, s32[4,8,128]{2,1,0:T(8,128)}, u32[]{:S(2)}) copy-start(s32[4,8,128]{2,1,0:T(8,128)} %slot_ref.1) | copy-start | bytes 49156
  5.1 17.8 %copy-start.6 = (f32[4,8,128]{2,1,0:T(8,128)S(1)}, f32[4,8,128]{2,1,0:T(8,128)}, u32[]{:S(2)}) copy-start(f32[4,8,128]{2,1,0:T(8,128)} %wt_ref.1) | copy-start | bytes 49156
  5.1 17.8 %all-to-all-start = ((bf16[32,48,128]{2,1,0:T(8,128)(2,1)}), bf16[32,48,128]{2,1,0:T(8,128)(2,1)S(1)}, u32[]{:S(2)}, u32[]{:S(2)}) async-start(bf16[32,48,128]{2,1,0:T(8,128)(2,1)} %shard_map.113), calls=%async_computation | async-start | bytes 786432 | tf_op jit(solution)/shard_map/all_to_all | solution.py:535
  14.3 15.5 %collective-permute-start = (bf16[3,25,16,128]{3,2,1,0:T(8,128)(2,1)S(1)}, bf16[3,25,16,128]{3,2,1,0:T(8,128)(2,1)S(1)}, u32[]{:S(2)}, u32[]{:S(2)}) collective-permute-start(bf16[3,25,16,128]{3,2,1,0:T(8,128)(2,1)S(1)} %get-tuple-element.17), channel_id=1, source_target_pairs={{0,4},{4,0},{8,12},{12,8},{16,20},{20,16},{24,28},{28,24},{32,36},... | collective-permute-start | bytes 921608 | tf_op jit(solution)/shard_map/ppermute | solution.py:142
  14.6 15.3 %collective-permute-start.1 = (bf16[3,25,16,128]{3,2,1,0:T(8,128)(2,1)S(1)}, bf16[3,25,16,128]{3,2,1,0:T(8,128)(2,1)S(1)}, u32[]{:S(2)}, u32[]{:S(2)}) collective-permute-start(bf16[3,25,16,128]{3,2,1,0:T(8,128)(2,1)S(1)} %get-tuple-element.18), channel_id=1, source_target_pairs={{4,8},{8,4},{12,16},{16,12},{20,24},{24,20},{28,32},{32,28},{36,40... | collective-permute-start | bytes 921608 | tf_op jit(solution)/shard_map/ppermute | solution.py:142
  25.8 7.8 %collective-permute-start.3 = (bf16[3,96,128]{2,1,0:T(8,128)(2,1)S(1)}, bf16[3,96,128]{2,1,0:T(8,128)(2,1)S(1)}, u32[]{:S(2)}, u32[]{:S(2)}) collective-permute-start(bf16[3,96,128]{2,1,0:T(8,128)(2,1)S(1)} %get-tuple-element.24), channel_id=1, source_target_pairs={{4,8},{8,4},{12,16},{16,12},{20,24},{24,20},{28,32},{32,28},{36,40... | collective-permute-start | bytes 221192 | tf_op jit(solution)/shard_map/ppermute | solution.py:142
  29.8 3.8 %collective-permute-start.2 = (bf16[3,96,128]{2,1,0:T(8,128)(2,1)S(1)}, bf16[3,96,128]{2,1,0:T(8,128)(2,1)S(1)}, u32[]{:S(2)}, u32[]{:S(2)}) collective-permute-start(bf16[3,96,128]{2,1,0:T(8,128)(2,1)S(1)} %get-tuple-element.20), channel_id=1, source_target_pairs={{0,4},{4,0},{8,12},{12,8},{16,20},{20,16},{24,28},{28,24},{32,36},... | collective-permute-start | bytes 221192 | tf_op jit(solution)/shard_map/ppermute | solution.py:142
  33.6 3.9 %copy-start.3 = (f32[8]{0:T(128)S(1)}, f32[8]{0:T(128)}, u32[]{:S(2)}) copy-start(f32[8]{0:T(128)} %settle_ref.3) | copy-start | bytes 100
  33.9 8.5 %copy-start.2 = (f32[8,48]{1,0:T(8,128)S(1)}, f32[8,48]{1,0:T(8,128)}, u32[]{:S(2)}) copy-start(f32[8,48]{1,0:T(8,128)} %profile_ref.1) | copy-start | bytes 4612
  33.9 6.8 %collective-permute-start.5 = (bf16[496,128]{1,0:T(8,128)(2,1)S(1)}, bf16[496,128]{1,0:T(8,128)(2,1)S(1)}, u32[]{:S(2)}, u32[]{:S(2)}) collective-permute-start(bf16[496,128]{1,0:T(8,128)(2,1)S(1)} %shard_map.118.own_ref), channel_id=1, source_target_pairs={{1,2},{2,1},{5,6},{6,5},{9,10},{10,9},{13,14},{14,13},{17,18},{18,... | collective-permute-start | bytes 380936 | tf_op jit(solution)/shard_map/ppermute | solution.py:142
  37.4 5.0 %collective-permute-start.4 = (bf16[496,128]{1,0:T(8,128)(2,1)S(1)}, bf16[496,128]{1,0:T(8,128)(2,1)S(1)}, u32[]{:S(2)}, u32[]{:S(2)}) collective-permute-start(bf16[496,128]{1,0:T(8,128)(2,1)S(1)} %shard_map.118.own_ref), channel_id=1, source_target_pairs={{0,1},{1,0},{2,3},{3,2},{4,5},{5,4},{6,7},{7,6},{8,9},{9,8},{10,11... | collective-permute-start | bytes 380936 | tf_op jit(solution)/shard_map/ppermute | solution.py:142

commit v6 on v5

--- a/solution.py
+++ b/solution.py
@@ -103,13 +103,11 @@
 def horizontal_kernel(recv_ref, slot_ref, wt_ref, winds_ref, a_ref, b_ref, lev_ref):
     kept = recv_ref.shape[1]
     half = LANES // 2
-    first = lane_ids((kept, LANES)) < half
     for pair in range(recv_ref.shape[0] // 2):
-        one = recv_ref[2 * pair].astype(F32)
-        two = recv_ref[2 * pair + 1].astype(F32)
+        one, two = recv_ref[2 * pair], recv_ref[2 * pair + 1]
         at = slice(pair * LANES, (pair + 1) * LANES)
-        lev_ref[:kept, at] = jnp.where(first, one, roll_lanes(two, half)).astype(BF16)
-        lev_ref[kept:, at] = jnp.where(first, roll_lanes(one, half), two).astype(BF16)
+        lev_ref[:kept, at] = jnp.concatenate([one[:, :half], two[:, :half]], axis=1)
+        lev_ref[kept:, at] = jnp.concatenate([one[:, half:], two[:, half:]], axis=1)
     rows = winds_ref.shape[0]
     lev = lev_ref[...]
     raw = [wt_ref[q] for q in range(4)]

time: 48.8 us -> 48.8 us (level)
  no operation moved by 1% of the time
where the time goes in v6:
time: 48.8 us; the launch traced here: 48.5 us
  starting transfers between devices  20.9 us (43%)
  Pallas kernels  17.2 us (35%)
  waiting for transfers between devices  7.81 us (16%)
  local copies, waits for them, and re-layouts  1.73 us (4%)
  between operations  0.85 us (2%)
    pallas_call x7, Pallas kernels, call(): pl.pallas_call(kernel, out_shape=out_shape, in_specs=[pl.BlockSpec(memory...  17.2 us
    ppermute x6, starting transfers between devices, swap(): return lax.ppermute(array, axis, pairs)  12.4 us
    all_to_all x1, starting transfers between devices, per_device(): lax.all_to_all(sent, 'rows', split_axis=0, concat_axis=0, tiled=True)  8.48 us
    ppermute x6, waiting for transfers between devices, swap(): return lax.ppermute(array, axis, pairs)  4.02 us
    all_to_all x1, waiting for transfers between devices, per_device(): lax.all_to_all(sent, 'rows', split_axis=0, concat_axis=0, tiled=True)  3.79 us
    unnamed x19, local copies, waits for them, and re-layouts  1.73 us
  transfers between devices with their start and end apart: 7, of which 4 were waited for; matrix products, arithmetic and copies ran while one was open for 0% of the time, Pallas kernels for 17%

profile of v6, /device:TPU:10, one launch (start us, length us, event | category | flops | bytes accessed | tf_op | source)
XLA Modules:
  0.0 48.5 jit_solution(4489453060627750631)
XLA Ops:
  0.6 0.0 copy-start.4
  0.6 0.0 copy-start.8
  0.7 0.0 copy-start.7
  0.7 1.7 %copy.12.nwp_ref = bf16[2,137,2048]{2,1,0:T(8,128)(2,1)S(1)} copy(bf16[2,137,2048]{2,0,1:T(2,128)(2,1)} %param.11) | data formatting | bytes 2244608 | tf_op args[1]
  2.3 0.0 copy-done.4
  2.4 0.0 copy-done.8
  2.4 0.0 copy-done.7
  2.4 0.0 copy-start
  2.4 0.0 copy-start.1
  2.4 2.7 %shard_map.113 = bf16[32,48,128]{2,1,0:T(8,128)(2,1)} custom-call(s32[1,48]{1,0:T(1,128)S(1)} %bitcast.10, f32[1,48]{1,0:T(1,128)S(1)} %bitcast.11, s32[32,64]{1,0:T(8,128)S(1)} %bitcast.9, bf16[2,137,2048]{2,1,0:T(8,128)(2,1)S(1)} %copy.12.nwp_ref), custom_call_target="tpu_custom_call" | custom-call | flops 805306368 | bytes 1524096 | tf_op jit(solution)/shard_map/pallas_call | solution.py:38
  5.1 0.0 copy-start.5
  5.1 0.0 copy-start.6
  5.1 8.5 %all-to-all-start = ((bf16[32,48,128]{2,1,0:T(8,128)(2,1)}), bf16[32,48,128]{2,1,0:T(8,128)(2,1)S(1)}, u32[]{:S(2)}, u32[]{:S(2)}) async-start(bf16[32,48,128]{2,1,0:T(8,128)(2,1)} %shard_map.113), calls=%async_computation | async-start | bytes 786432 | tf_op jit(solution)/shard_map/all_to_all | solution.py:533
  13.6 0.0 copy-done
  13.6 0.0 copy-done.1
  13.7 0.7 %shard_map.114 = (bf16[3,25,16,128]{3,2,1,0:T(8,128)(2,1)S(1)}, bf16[3,25,16,128]{3,2,1,0:T(8,128)(2,1)S(1)}) custom-call(f32[3072,128]{1,0:T(8,128)S(1)} %bitcast.6, s32[8,128]{1,0:T(8,128)S(1)} %copy-done.1), custom_call_target="tpu_custom_call" | custom-call | tf_op jit(solution)/shard_map/pallas_call | solution.py:38
  14.3 0.2 collective-permute-start
  14.6 4.5 %collective-permute-start.1 = (bf16[3,25,16,128]{3,2,1,0:T(8,128)(2,1)S(1)}, bf16[3,25,16,128]{3,2,1,0:T(8,128)(2,1)S(1)}, u32[]{:S(2)}, u32[]{:S(2)}) collective-permute-start(bf16[3,25,16,128]{3,2,1,0:T(8,128)(2,1)S(1)} %get-tuple-element.18), channel_id=1, source_target_pairs={{4,8},{8,4},{12,16},{16,12},{20,24},{24,20},{28,32},{32,28},{36,40... | collective-permute-start | bytes 921608 | tf_op jit(solution)/shard_map/ppermute | solution.py:140
  19.1 3.8 %all-to-all-done.recv_ref = bf16[32,48,128]{2,1,0:T(8,128)(2,1)S(1)} async-done(((bf16[32,48,128]{2,1,0:T(8,128)(2,1)}), bf16[32,48,128]{2,1,0:T(8,128)(2,1)S(1)}, u32[]{:S(2)}, u32[]{:S(2)}) %all-to-all-start) | async-done | bytes 393248 | tf_op jit(solution)/shard_map/all_to_all | solution.py:533
  22.9 0.0 copy-done.5
  22.9 0.0 copy-done.6
  22.9 2.9 %shard_map.115 = (f32[8,96,128]{2,1,0:T(8,128)S(1)}, bf16[3,96,128]{2,1,0:T(8,128)(2,1)S(1)}, bf16[3,96,128]{2,1,0:T(8,128)(2,1)S(1)}) custom-call(bf16[32,48,128]{2,1,0:T(8,128)(2,1)S(1)} %all-to-all-done.recv_ref, s32[4,8,128]{2,1,0:T(8,128)S(1)} %copy-done.5, f32[4,8,128]{2,1,0:T(8,128)S(1)} %copy-done.6), custom_call_target="tpu_custom_call" | custom-call | flops 49999998976 | bytes 966656 | tf_op jit(solution)/shard_map/pallas_call | solution.py:38
  25.8 4.0 %collective-permute-start.3 = (bf16[3,96,128]{2,1,0:T(8,128)(2,1)S(1)}, bf16[3,96,128]{2,1,0:T(8,128)(2,1)S(1)}, u32[]{:S(2)}, u32[]{:S(2)}) collective-permute-start(bf16[3,96,128]{2,1,0:T(8,128)(2,1)S(1)} %get-tuple-element.24), channel_id=1, source_target_pairs={{4,8},{8,4},{12,16},{16,12},{20,24},{24,20},{28,32},{32,28},{36,40... | collective-permute-start | bytes 221192 | tf_op jit(solution)/shard_map/ppermute | solution.py:140
  29.8 0.1 collective-permute-start.2
  29.9 0.0 collective-permute-done.ra_ref
  29.9 0.0 collective-permute-done.1.rb_ref
  29.9 1.7 %shard_map.117.conc_ref = bf16[400,128]{1,0:T(8,128)(2,1)S(1)} custom-call(f32[3072,128]{1,0:T(8,128)S(1)} %bitcast.7, s32[8,128]{1,0:T(8,128)S(1)} %copy-done.1, bf16[3,25,16,128]{3,2,1,0:T(8,128)(2,1)S(1)} %collective-permute-done.ra_ref, bf16[3,25,16,128]{3,2,1,0:T(8,128)(2,1)S(1)} %collective-permute-done.1.rb_ref), custom_call_target="tpu_custom_call" | custom-call | tf_op jit(solution)/shard_map/pallas_call | solution.py:38
  31.6 2.0 %collective-permute-done.3.wrb_ref.rb_ref = bf16[3,96,128]{2,1,0:T(8,128)(2,1)S(1)} collective-permute-done((bf16[3,96,128]{2,1,0:T(8,128)(2,1)S(1)}, bf16[3,96,128]{2,1,0:T(8,128)(2,1)S(1)}, u32[]{:S(2)}, u32[]{:S(2)}) %collective-permute-start.3) | collective-permute-done | bytes 73760 | tf_op jit(solution)/shard_map/ppermute | solution.py:140
  33.6 0.0 collective-permute-done.2.wra_ref.ra_ref
  33.6 0.0 copy-start.3
  33.6 0.3 shard_map.118.own_ref
  33.9 0.0 copy-start.2
  33.9 3.5 %collective-permute-start.5 = (bf16[496,128]{1,0:T(8,128)(2,1)S(1)}, bf16[496,128]{1,0:T(8,128)(2,1)S(1)}, u32[]{:S(2)}, u32[]{:S(2)}) collective-permute-start(bf16[496,128]{1,0:T(8,128)(2,1)S(1)} %shard_map.118.own_ref), channel_id=1, source_target_pairs={{1,2},{2,1},{5,6},{6,5},{9,10},{10,9},{13,14},{14,13},{17,18},{18,... | collective-permute-start | bytes 380936 | tf_op jit(solution)/shard_map/ppermute | solution.py:140
  37.4 0.1 collective-permute-start.4
  37.5 0.0 copy-done.3
  37.5 2.9 %shard_map.116 = (f32[60,48,128]{2,1,0:T(8,128)S(1)}, f32[12,384,128]{2,1,0:T(8,128)S(1)}, f32[8,8,128]{2,1,0:T(8,128)S(1)}) custom-call(f32[3072,128]{1,0:T(8,128)S(1)} %bitcast.8, f32[8]{0:T(128)S(1)} %copy-done.3, bf16[3,25,16,128]{3,2,1,0:T(8,128)(2,1)S(1)} %collective-permute-done.ra_ref, bf16[3,25,16,128]{3,2,1,0:T(8,128)(2,1)S(1)} %collective-permute-done.1.rb_ref, ...), custom_call_target="tpu_custom_call" | custom-call | tf_op jit(solution)/shard_map/pallas_call | solution.py:38
  40.3 0.3 collective-permute-done.5.xb_ref
  40.7 1.7 %collective-permute-done.4.xa_ref = bf16[496,128]{1,0:T(8,128)(2,1)S(1)} collective-permute-done((bf16[496,128]{1,0:T(8,128)(2,1)S(1)}, bf16[496,128]{1,0:T(8,128)(2,1)S(1)}, u32[]{:S(2)}, u32[]{:S(2)}) %collective-permute-start.4) | collective-permute-done | bytes 127008 | tf_op jit(solution)/shard_map/ppermute | solution.py:140
  42.4 0.0 copy-done.2
  42.4 6.1 %shard_map.119 = (f32[3072,128]{1,0:T(8,128)}, f32[64,128]{1,0:T(8,128)}) custom-call(f32[12,384,128]{2,1,0:T(8,128)S(1)} %get-tuple-element.25.part_ref, f32[60,48,128]{2,1,0:T(8,128)S(1)} %get-tuple-element.26.coef_ref, f32[8,8,128]{2,1,0:T(8,128)S(1)} %get-tuple-element.27.fallen_ref, s32[8,128]{1,0:T(8,128)S(1)} %copy-done.1, f32[8]{0:T(128)S(1)} %copy-done.3, ...), custom_call_target="tpu_custom_call" | custom-call | flops 23592960 | bytes 6473248 | tf_op jit(solution)/shard_map/pallas_call | solution.py:38
Async XLA Ops:
  0.6 1.7 %copy-start.4 = (s32[1,1,32,64]{3,2,1,0:T(8,128)S(1)}, s32[1,1,32,64]{3,2,1,0:T(8,128)}, u32[]{:S(2)}) copy-start(s32[1,1,32,64]{3,2,1,0:T(8,128)} %param.14) | copy-start | bytes 24580
  0.6 1.7 %copy-start.8 = (f32[48]{0:T(128)S(1)}, f32[48]{0:T(128)}, u32[]{:S(2)}) copy-start(f32[48]{0:T(128)} %param.13) | copy-start | bytes 580
  0.7 1.7 %copy-start.7 = (s32[48]{0:T(128)S(1)}, s32[48]{0:T(128)}, u32[]{:S(2)}) copy-start(s32[48]{0:T(128)} %param.12) | copy-start | bytes 580
  2.4 11.3 %copy-start = (f32[8,48,8,128]{3,2,1,0:T(8,128)S(1)}, f32[8,48,8,128]{3,2,1,0:T(8,128)}, u32[]{:S(2)}) copy-start(f32[8,48,8,128]{3,2,1,0:T(8,128)} %param.10) | copy-start | bytes 4718596
  2.4 11.3 %copy-start.1 = (s32[8,128]{1,0:T(8,128)S(1)}, s32[8,128]{1,0:T(8,128)}, u32[]{:S(2)}) copy-start(s32[8,128]{1,0:T(8,128)} %mask_ref.5) | copy-start | bytes 12292
  5.1 17.8 %copy-start.5 = (s32[4,8,128]{2,1,0:T(8,128)S(1)}, s32[4,8,128]{2,1,0:T(8,128)}, u32[]{:S(2)}) copy-start(s32[4,8,128]{2,1,0:T(8,128)} %slot_ref.1) | copy-start | bytes 49156
  5.1 17.8 %copy-start.6 = (f32[4,8,128]{2,1,0:T(8,128)S(1)}, f32[4,8,128]{2,1,0:T(8,128)}, u32[]{:S(2)}) copy-start(f32[4,8,128]{2,1,0:T(8,128)} %wt_ref.1) | copy-start | bytes 49156
  5.1 17.8 %all-to-all-start = ((bf16[32,48,128]{2,1,0:T(8,128)(2,1)}), bf16[32,48,128]{2,1,0:T(8,128)(2,1)S(1)}, u32[]{:S(2)}, u32[]{:S(2)}) async-start(bf16[32,48,128]{2,1,0:T(8,128)(2,1)} %shard_map.113), calls=%async_computation | async-start | bytes 786432 | tf_op jit(solution)/shard_map/all_to_all | solution.py:533
  14.3 15.5 %collective-permute-start = (bf16[3,25,16,128]{3,2,1,0:T(8,128)(2,1)S(1)}, bf16[3,25,16,128]{3,2,1,0:T(8,128)(2,1)S(1)}, u32[]{:S(2)}, u32[]{:S(2)}) collective-permute-start(bf16[3,25,16,128]{3,2,1,0:T(8,128)(2,1)S(1)} %get-tuple-element.17), channel_id=1, source_target_pairs={{0,4},{4,0},{8,12},{12,8},{16,20},{20,16},{24,28},{28,24},{32,36},... | collective-permute-start | bytes 921608 | tf_op jit(solution)/shard_map/ppermute | solution.py:140
  14.6 15.3 %collective-permute-start.1 = (bf16[3,25,16,128]{3,2,1,0:T(8,128)(2,1)S(1)}, bf16[3,25,16,128]{3,2,1,0:T(8,128)(2,1)S(1)}, u32[]{:S(2)}, u32[]{:S(2)}) collective-permute-start(bf16[3,25,16,128]{3,2,1,0:T(8,128)(2,1)S(1)} %get-tuple-element.18), channel_id=1, source_target_pairs={{4,8},{8,4},{12,16},{16,12},{20,24},{24,20},{28,32},{32,28},{36,40... | collective-permute-start | bytes 921608 | tf_op jit(solution)/shard_map/ppermute | solution.py:140
  25.8 7.8 %collective-permute-start.3 = (bf16[3,96,128]{2,1,0:T(8,128)(2,1)S(1)}, bf16[3,96,128]{2,1,0:T(8,128)(2,1)S(1)}, u32[]{:S(2)}, u32[]{:S(2)}) collective-permute-start(bf16[3,96,128]{2,1,0:T(8,128)(2,1)S(1)} %get-tuple-element.24), channel_id=1, source_target_pairs={{4,8},{8,4},{12,16},{16,12},{20,24},{24,20},{28,32},{32,28},{36,40... | collective-permute-start | bytes 221192 | tf_op jit(solution)/shard_map/ppermute | solution.py:140
  29.8 3.8 %collective-permute-start.2 = (bf16[3,96,128]{2,1,0:T(8,128)(2,1)S(1)}, bf16[3,96,128]{2,1,0:T(8,128)(2,1)S(1)}, u32[]{:S(2)}, u32[]{:S(2)}) collective-permute-start(bf16[3,96,128]{2,1,0:T(8,128)(2,1)S(1)} %get-tuple-element.20), channel_id=1, source_target_pairs={{0,4},{4,0},{8,12},{12,8},{16,20},{20,16},{24,28},{28,24},{32,36},... | collective-permute-start | bytes 221192 | tf_op jit(solution)/shard_map/ppermute | solution.py:140
  33.6 3.9 %copy-start.3 = (f32[8]{0:T(128)S(1)}, f32[8]{0:T(128)}, u32[]{:S(2)}) copy-start(f32[8]{0:T(128)} %settle_ref.3) | copy-start | bytes 100
  33.9 8.5 %copy-start.2 = (f32[8,48]{1,0:T(8,128)S(1)}, f32[8,48]{1,0:T(8,128)}, u32[]{:S(2)}) copy-start(f32[8,48]{1,0:T(8,128)} %profile_ref.1) | copy-start | bytes 4612
  33.9 6.8 %collective-permute-start.5 = (bf16[496,128]{1,0:T(8,128)(2,1)S(1)}, bf16[496,128]{1,0:T(8,128)(2,1)S(1)}, u32[]{:S(2)}, u32[]{:S(2)}) collective-permute-start(bf16[496,128]{1,0:T(8,128)(2,1)S(1)} %shard_map.118.own_ref), channel_id=1, source_target_pairs={{1,2},{2,1},{5,6},{6,5},{9,10},{10,9},{13,14},{14,13},{17,18},{18,... | collective-permute-start | bytes 380936 | tf_op jit(solution)/shard_map/ppermute | solution.py:140
  37.4 5.0 %collective-permute-start.4 = (bf16[496,128]{1,0:T(8,128)(2,1)S(1)}, bf16[496,128]{1,0:T(8,128)(2,1)S(1)}, u32[]{:S(2)}, u32[]{:S(2)}) collective-permute-start(bf16[496,128]{1,0:T(8,128)(2,1)S(1)} %shard_map.118.own_ref), channel_id=1, source_target_pairs={{0,1},{1,0},{2,3},{3,2},{4,5},{5,4},{6,7},{7,6},{8,9},{9,8},{10,11... | collective-permute-start | bytes 380936 | tf_op jit(solution)/shard_map/ppermute | solution.py:140
